TPU v7x, 128 devices: a whole 4x4x4 slice. The times are simulated.
128 devices in a mesh: req: 4 (over z), exp: 32 (over y, x, core).
Axes of the slice: x: 4, y: 4, z: 4, core: 2. Of those that a mesh axis runs over, the one named last changes fastest.
Arguments:
- hidden: bfloat16 [16384, 1536], P(('req', 'exp')), may hold values from -6 to 6
- attn_gain: float32 [1536], replicated, may hold values from 0.5 to 1.5
- query_weight: bfloat16 [1536, 1536], replicated
- key_matrix: bfloat16 [1536, 512], replicated
- value_matrix: bfloat16 [1536, 512], replicated, may hold values from -0.15625 to 0.15625
- output_weight: bfloat16 [1536, 1536], replicated, may hold values from -0.15625 to 0.15625
- prompt_start: int32 [16384], P(('req', 'exp')), may hold values from 0 to 4095, as said below
- ffn_gain: float32 [1536], replicated, may hold values from 0.5 to 1.5
- routes: int32 [16384, 8], P(('req', 'exp')), may hold values from 0 to 31, all different within a row; in each aligned block of 128 rows (0 to 127, 128 to 255, ...) at most 64 rows name the same one
- route_weights: float32 [16384, 8], P(('req', 'exp')), may hold values from 0.02 to 0.3
- expert_weights: bfloat16 [32, 3, 1536, 512], P('exp', None, None, 'req'), may hold values from -0.15625 to 0.15625
Outputs:
- layer_out: bfloat16 [16384, 1536], P(('req', 'exp'))
- rotated_key_cache: bfloat16 [16384, 512], P(('req', 'exp'))
- value_cache: bfloat16 [16384, 512], P(('req', 'exp'))
Inputs may be any that keep to these rules, and one draw needn't show every extreme that they name: prompt_start never falls along a stream, is at most the token's own position in it, is 0 at each stream's first position, and tokens of one stream with the same value form one prompt; each stream's last position begins a prompt of its own. `routes`: each row names 8 different experts; among the rows of one device no expert is named by more than 64 rows, a bound that some block reaches.
All inputs are finite; a program needn't handle non-finite values.
Results may differ from a plain program's by a relative error of at most 0.0096.
Values may be sent and summed in bfloat16 or wider, within the bound.
A program may use at most 192 MiB of HBM per device.

v0:
```python
import jax
import jax.numpy as jnp
from jax import lax
from jax.sharding import PartitionSpec as P

QUERY_HEADS = 24
KEY_VALUE_HEADS = 8
HEAD_SIZE = 64
TOP = 8


epsilon = 1e-05


def rms_norm(values, gain):
    mean_square = jnp.mean(values * values, axis=-1, keepdims=True)
    return values * lax.rsqrt(mean_square + epsilon) * gain


def rotary_embedding(heads_in, stream_offsets):
    half = heads_in.shape[-1] // 2
    freqs = 10000.0 ** (-jnp.arange(half, dtype=jnp.float32) / half)
    angle = stream_offsets.astype(jnp.float32)[:, None] * freqs[None, :]
    cosine = jnp.cos(angle)[:, None, :]
    sine = jnp.sin(angle)[:, None, :]
    first_half = heads_in[..., :half]
    second_half = heads_in[..., half:]
    return jnp.concatenate(
        [first_half * cosine - second_half * sine, second_half * cosine + first_half * sine],
        axis=-1,
    )


def shards(
    hidden,
    attn_gain,
    query_weight,
    key_matrix,
    value_matrix,
    output_weight,
    prompt_start,
    ffn_gain,
    routes,
    route_weights,
    expert_weights,
):
    total_row_count = hidden.shape[0]
    lane_index = lax.axis_index("exp")
    lane_count = lax.axis_size("exp")
    heads_per_group = QUERY_HEADS // KEY_VALUE_HEADS
    positions = lane_index * total_row_count + jnp.arange(total_row_count, dtype=jnp.int32)
    stream_offsets = positions - prompt_start
    inputs = hidden.astype(jnp.float32)
    normalized_input = rms_norm(inputs, attn_gain).astype(jnp.bfloat16)
    query_rows_all = jnp.dot(
        normalized_input, query_weight, preferred_element_type=jnp.float32
    ).reshape(total_row_count, QUERY_HEADS, HEAD_SIZE)
    query_rows_all = (
        rotary_embedding(query_rows_all, stream_offsets)
        .astype(jnp.bfloat16)
        .reshape(total_row_count, KEY_VALUE_HEADS, heads_per_group, HEAD_SIZE)
    )
    shard_keys = jnp.dot(normalized_input, key_matrix, preferred_element_type=jnp.float32).reshape(
        total_row_count, KEY_VALUE_HEADS, HEAD_SIZE
    )
    shard_keys = (
        rotary_embedding(shard_keys, stream_offsets)
        .astype(jnp.bfloat16)
        .reshape(total_row_count, KEY_VALUE_HEADS * HEAD_SIZE)
    )
    values_local = jnp.dot(
        normalized_input, value_matrix, preferred_element_type=jnp.float32
    ).astype(jnp.bfloat16)
    stacked = jnp.stack([shard_keys, values_local])
    initial = (
        jnp.full((total_row_count, KEY_VALUE_HEADS, heads_per_group), -1e30, jnp.float32),
        jnp.zeros((total_row_count, KEY_VALUE_HEADS, heads_per_group), jnp.float32),
        jnp.zeros((total_row_count, KEY_VALUE_HEADS, heads_per_group, HEAD_SIZE), jnp.float32),
    )
    key_value_slice = lax.all_gather(stacked, "exp", axis=1, tiled=True)
    feature_width = key_value_slice.shape[1]
    key_tile = key_value_slice[0].reshape(feature_width, KEY_VALUE_HEADS, HEAD_SIZE)
    value_tile = key_value_slice[1].reshape(feature_width, KEY_VALUE_HEADS, HEAD_SIZE)
    key_pos = jnp.arange(feature_width, dtype=jnp.int32)
    scores = jnp.einsum(
        "tgrd,sgd->tgrs", query_rows_all, key_tile, preferred_element_type=jnp.float32
    ) * HEAD_SIZE ** (-0.5)
    valid = (key_pos[None, :] >= prompt_start[:, None]) & (key_pos[None, :] <= positions[:, None])
    valid = valid[:, None, None, :]
    masked = jnp.where(valid, scores, jnp.float32(-1e30))
    new_max = jnp.maximum(initial[0], jnp.max(masked, axis=-1))
    probs = jnp.where(valid, jnp.exp(masked - new_max[..., None]), jnp.float32(0.0))
    totals = jnp.sum(probs, axis=-1)
    attention_mixed = jnp.einsum(
        "tgrs,sgd->tgrd", probs.astype(jnp.bfloat16), value_tile, preferred_element_type=jnp.float32
    )
    attention = (
        (attention_mixed / totals[..., None])
        .reshape(total_row_count, QUERY_HEADS * HEAD_SIZE)
        .astype(jnp.bfloat16)
    )
    residual = inputs + jnp.dot(attention, output_weight, preferred_element_type=jnp.float32)
    moe_in = rms_norm(residual, ffn_gain).astype(jnp.bfloat16)
    capacity = min(total_row_count, 2 * total_row_count * TOP // lane_count)
    flat_routes = routes.reshape(-1)
    hit_table = (flat_routes[:, None] == jnp.arange(lane_count, dtype=jnp.int32)[None, :]).astype(
        jnp.int32
    )
    slot_rank = jnp.cumsum(hit_table, axis=0) - hit_table
    slot_index = jnp.sum(slot_rank * hit_table, axis=1)
    dest_grid = (flat_routes * capacity + slot_index).reshape(total_row_count, TOP)
    slot_table = jnp.any(
        dest_grid[:, :, None] == jnp.arange(lane_count * capacity, dtype=jnp.int32)[None, None, :],
        axis=1,
    ).astype(jnp.bfloat16)
    outgoing = lax.dot_general(
        slot_table, moe_in, (((0,), (0,)), ((), ())), preferred_element_type=jnp.float32
    ).astype(jnp.bfloat16)
    outgoing = outgoing.reshape(lane_count, capacity, moe_in.shape[1])
    incoming = lax.all_to_all(outgoing, "exp", split_axis=0, concat_axis=0, tiled=True)
    rows_in = incoming.reshape(lane_count * capacity, moe_in.shape[1])
    weight_piece = lax.all_gather(expert_weights, "req", axis=3, tiled=True)
    gate_out = jnp.dot(rows_in, weight_piece[0, 0], preferred_element_type=jnp.float32)
    up_out = jnp.dot(rows_in, weight_piece[0, 1], preferred_element_type=jnp.float32)
    hidden_units = (jax.nn.silu(gate_out) * up_out).astype(jnp.bfloat16)
    expert_sum = lax.dot_general(
        hidden_units,
        weight_piece[0, 2],
        (((1,), (1,)), ((), ())),
        preferred_element_type=jnp.float32,
    )
    expert_out = expert_sum.astype(jnp.bfloat16).reshape(lane_count, capacity, moe_in.shape[1])
    returned = lax.all_to_all(expert_out, "exp", split_axis=0, concat_axis=0, tiled=True).reshape(
        lane_count * capacity, moe_in.shape[1]
    )
    moe_sum = jnp.zeros((total_row_count, moe_in.shape[1]), jnp.float32)
    for column in range(TOP):
        moe_sum = moe_sum + route_weights[:, column : column + 1] * returned[
            dest_grid[:, column]
        ].astype(jnp.float32)
    layer_out = (residual + moe_sum).astype(jnp.bfloat16)
    return (layer_out, stacked[0], stacked[1])


def solution(mesh):
    in_specs = (
        P(("req", "exp"), None),
        P(),
        P(),
        P(),
        P(),
        P(),
        P(("req", "exp")),
        P(),
        P(("req", "exp"), None),
        P(("req", "exp"), None),
        P("exp", None, None, "req"),
    )
    out_specs = (P(("req", "exp"), None), P(("req", "exp"), None), P(("req", "exp"), None))
    return jax.shard_map(shards, mesh=mesh, in_specs=in_specs, out_specs=out_specs, check_vma=False)
```

profile of v0, /device:TPU:0, one launch (start us, length us, event | category | flops | bytes accessed | tf_op | source)
XLA Modules:
  0.0 402.0 jit_solution(10042116273317455146)
XLA Ops:
  15.2 4.3 %fusion.44 = f32[128,1536]{0,1:T(8,128)S(1)} fusion(bf16[1536,1536]{1,0:T(8,128)(2,1)} %param.13, bf16[128,1536]{1,0:T(8,128)(2,1)S(1)} %copy-done.2, f32[1536]{0:T(1024)S(1)} %copy-done.4, f32[128]{0:T(128)S(1)} %add_rsqrt_fusion.1), kind=kOutput, calls=%fused_computation.106 | convolution fusion | flops 604766208 | bytes 5904896 | tf_op jit(solution)/shard_map/dot_general | solution.py:55
  19.7 9.5 %reduce-window.6 = s32[32,8,128]{2,1,0:T(8,128)S(1)} reduce-window(s32[32,8,128]{2,1,0:T(8,128)S(1)} %fusion.30, s32[]{:T(128)} %constant.38.clone.1), window={size=1x1x128 pad=0_0x0_0x127_0}, to_apply=%region_3.4 | reduce-window | flops 4161536 | bytes 262148 | tf_op jit(solution)/shard_map/reduce-window
  33.9 35.2 %all-gather.3.cloned.1.call-done = bf16[2,4096,512]{2,1,0:T(8,128)(2,1)} async-done(((bf16[2,128,512]{2,1,0:T(8,128)(2,1)}), bf16[2,4096,512]{2,1,0:T(8,128)(2,1)}) %all-gather.3.cloned.1.call-update) | async-done | bytes 8388624 | tf_op jit(solution)/shard_map/all_gather | solution.py:80
  69.1 5.7 %fusion.49 = (bf16[1,4096,512]{2,1,0:T(8,128)(2,1)}, bf16[1,4096,512]{2,1,0:T(8,128)(2,1)}) fusion(bf16[2,4096,512]{2,1,0:T(8,128)(2,1)} %all-gather.3.cloned.1.call-done), kind=kLoop, calls=%fused_computation.108 | loop fusion | bytes 16777216 | tf_op jit(solution)/shard_map/slice | solution.py:82
  74.8 6.5 %copy.61 = bf16[1,4096,512]{1,2,0:T(8,128)(2,1)} copy(bf16[1,4096,512]{2,1,0:T(8,128)(2,1)} %get-tuple-element.16) | data formatting | bytes 8388608 | tf_op jit(solution)/shard_map/slice | solution.py:83
  81.3 6.4 %copy.62 = bf16[1,4096,512]{1,2,0:T(8,128)(2,1)} copy(bf16[1,4096,512]{2,1,0:T(8,128)(2,1)} %get-tuple-element.15) | data formatting | bytes 8388608 | tf_op jit(solution)/shard_map/slice | solution.py:82
  87.8 21.9 %fusion = (f32[128,8,3]{0,2,1:T(4,128)S(1)}, f32[8,4096,128,3]{2,1,3,0:T(8,128)}) fusion(pred[128,4096]{0,1:T(8,128)(4,1)S(1)} %fusion.7, bf16[4096,8,64,1]{0,2,3,1:T(8,128)(2,1)} %bitcast.117, bf16[128,8,3,32]{0,3,2,1:T(8,128)(2,1)S(1)} %bitcast.125, bf16[128,8,3,32]{0,3,2,1:T(8,128)(2,1)S(1)} %bitcast.124), kind=kOutput, calls=%fused_computation.10 | convolution fusion | flops 1649144832 | bytes 55455744 | tf_op jit(solution)/shard_map/tgrd,sgd->tgrs/dot_general | solution.py:85
  109.6 21.6 %fusion.1 = f32[128,8,3]{0,2,1:T(4,128)S(1)} fusion(f32[8,4096,128,3]{2,1,3,0:T(8,128)} %get-tuple-element.40, f32[128,8,3]{0,2,1:T(4,128)S(1)} %broadcast_maximum_fusion, pred[128,4096]{0,1:T(8,128)(4,1)S(1)} %fusion.7), kind=kLoop, calls=%fused_computation.11 | loop fusion | flops 62911488 | bytes 50880512 | tf_op jit(solution)/shard_map/reduce_sum | solution.py:93
  131.3 23.1 %fusion.15 = bf16[128,8,3,64]{0,3,2,1:T(8,128)(2,1)S(1)} fusion(bf16[4096,8,64,1]{0,2,3,1:T(8,128)(2,1)} %bitcast.119, f32[8,4096,128,3]{2,1,3,0:T(8,128)} %get-tuple-element.40, f32[128,8,3]{0,2,1:T(4,128)S(1)} %broadcast_maximum_fusion, pred[128,4096]{0,1:T(8,128)(4,1)S(1)} %fusion.7, f32[128,8,3]{0,2,1:T(4,128)S(1)} %fusion.1), kind=kOutput, calls=%fused_computation.33 | convolution fusion | flops 1673920512 | bytes 55468032 | tf_op jit(solution)/shard_map/tgrs,sgd->tgrd/dot_general | solution.py:94
  157.7 4.5 %convolution_convert_fusion.1 = bf16[2048,1536]{1,0:T(8,128)(2,1)} fusion(pred[128,2048]{1,0:T(8,128)(4,1)S(1)} %fusion.6, f32[128,1536]{1,0:T(8,128)S(1)} %get-tuple-element.42, f32[1536]{0:T(1024)S(1)} %copy-done.6, f32[128]{0:T(128)S(1)} %add_rsqrt_fusion), kind=kOutput, calls=%fused_computation.18 | convolution fusion | flops 809041920 | bytes 7346688 | tf_op jit(solution)/shard_map/dot_general | solution.py:116
  162.2 5.7 %all-to-all-start = ((bf16[32,64,1536]{2,1,0:T(8,128)(2,1)}), bf16[32,64,1536]{2,1,0:T(8,128)(2,1)}, u32[]{:S(2)}, u32[]{:S(2)}) async-start(bf16[32,64,1536]{2,1,0:T(8,128)(2,1)} %bitcast.116), calls=%async_computation | async-start | bytes 12582912 | tf_op jit(solution)/shard_map/all_to_all | solution.py:120
  167.9 77.9 %all-to-all-done = bf16[32,64,1536]{2,1,0:T(8,128)(2,1)} async-done(((bf16[32,64,1536]{2,1,0:T(8,128)(2,1)}), bf16[32,64,1536]{2,1,0:T(8,128)(2,1)}, u32[]{:S(2)}, u32[]{:S(2)}) %all-to-all-start) | async-done | bytes 6291488 | tf_op jit(solution)/shard_map/all_to_all | solution.py:120
  245.8 8.6 %fusion.8 = f32[2048,512]{1,0:T(8,128)} fusion(bf16[2048,1536]{1,0:T(8,128)(2,1)} %bitcast.19, bf16[1,3,1536,512]{3,2,1,0:T(8,128)(2,1)} %all-gather.5.cloned.1.call-done), kind=kOutput, calls=%fused_computation.27 | convolution fusion | flops 3221225472 | bytes 12058624 | tf_op jit(solution)/shard_map/dot_general | solution.py:123
  254.4 12.1 %convolution_convert_fusion = bf16[2048,1536]{1,0:T(8,128)(2,1)} fusion(bf16[1,3,1536,512]{3,2,1,0:T(8,128)(2,1)} %all-gather.5.cloned.1.call-done, f32[2048,512]{1,0:T(8,128)} %fusion.8, bf16[2048,1536]{1,0:T(8,128)(2,1)} %bitcast.19), kind=kOutput, calls=%fused_computation.17 | convolution fusion | flops 6451888128 | bytes 19922944 | tf_op jit(solution)/shard_map/dot_general | solution.py:126
  266.4 5.2 %all-to-all-start.1 = ((bf16[32,64,1536]{2,1,0:T(8,128)(2,1)}), bf16[32,64,1536]{2,1,0:T(8,128)(2,1)}, u32[]{:S(2)}, u32[]{:S(2)}) async-start(bf16[32,64,1536]{2,1,0:T(8,128)(2,1)} %bitcast.118), calls=%async_computation.1 | async-start | bytes 12582912 | tf_op jit(solution)/shard_map/all_to_all | solution.py:133
  273.1 76.3 %all-to-all-done.1 = bf16[32,64,1536]{2,1,0:T(8,128)(2,1)} async-done(((bf16[32,64,1536]{2,1,0:T(8,128)(2,1)}), bf16[32,64,1536]{2,1,0:T(8,128)(2,1)}, u32[]{:S(2)}, u32[]{:S(2)}) %all-to-all-start.1) | async-done | bytes 6291488 | tf_op jit(solution)/shard_map/all_to_all | solution.py:133
  349.4 4.8 %gather_fusion.7 = bf16[128,1536]{1,0:T(8,128)(2,1)S(1)} fusion(bf16[2048,1536]{1,0:T(8,128)(2,1)} %bitcast.24, s32[1024]{0:T(1024)S(1)} %get-tuple-element.45), kind=kCustom, calls=%fused_computation.7 | custom fusion | bytes 786944 | tf_op jit(solution)/shard_map/gather | solution.py:138
  354.2 4.8 %gather_fusion.6 = bf16[128,1536]{1,0:T(8,128)(2,1)S(1)} fusion(bf16[2048,1536]{1,0:T(8,128)(2,1)} %bitcast.24, s32[1024]{0:T(1024)S(1)} %get-tuple-element.46), kind=kCustom, calls=%fused_computation.6 | custom fusion | bytes 786944 | tf_op jit(solution)/shard_map/gather | solution.py:138
  359.1 4.8 %gather_fusion.5 = bf16[128,1536]{1,0:T(8,128)(2,1)S(1)} fusion(bf16[2048,1536]{1,0:T(8,128)(2,1)} %bitcast.24, s32[1024]{0:T(1024)S(1)} %get-tuple-element.47), kind=kCustom, calls=%fused_computation.5 | custom fusion | bytes 786944 | tf_op jit(solution)/shard_map/gather | solution.py:138
  363.9 5.6 %gather_fusion.4 = bf16[128,1536]{1,0:T(8,128)(2,1)} fusion(bf16[2048,1536]{1,0:T(8,128)(2,1)} %bitcast.24, s32[1024]{0:T(1024)S(1)} %get-tuple-element.48), kind=kCustom, calls=%fused_computation.4 | custom fusion | bytes 786944 | tf_op jit(solution)/shard_map/gather | solution.py:138
  369.5 5.6 %gather_fusion.3 = bf16[128,1536]{1,0:T(8,128)(2,1)} fusion(bf16[2048,1536]{1,0:T(8,128)(2,1)} %bitcast.24, s32[1024]{0:T(1024)S(1)} %get-tuple-element.49), kind=kCustom, calls=%fused_computation.3 | custom fusion | bytes 786944 | tf_op jit(solution)/shard_map/gather | solution.py:138
  375.1 5.6 %gather_fusion.2 = bf16[128,1536]{1,0:T(8,128)(2,1)} fusion(bf16[2048,1536]{1,0:T(8,128)(2,1)} %bitcast.24, s32[1024]{0:T(1024)S(1)} %get-tuple-element.50), kind=kCustom, calls=%fused_computation.2 | custom fusion | bytes 786944 | tf_op jit(solution)/shard_map/gather | solution.py:138
  380.7 5.7 %gather_fusion.1 = bf16[128,1536]{1,0:T(8,128)(2,1)} fusion(bf16[2048,1536]{1,0:T(8,128)(2,1)} %bitcast.24, s32[1024]{0:T(1024)S(1)} %get-tuple-element.51), kind=kCustom, calls=%fused_computation.1 | custom fusion | bytes 786944 | tf_op jit(solution)/shard_map/gather | solution.py:138
  386.4 5.6 %gather_fusion = bf16[128,1536]{1,0:T(8,128)(2,1)} fusion(bf16[2048,1536]{1,0:T(8,128)(2,1)} %bitcast.24, s32[1024]{0:T(1024)S(1)} %get-tuple-element.52), kind=kCustom, calls=%fused_computation | custom fusion | bytes 786944 | tf_op jit(solution)/shard_map/gather | solution.py:138
  (63 shorter events, 20.2 us)
Async XLA Ops:
  7.2 1.6 copy-start
  7.2 8.0 %copy-start.2 = (bf16[128,1536]{1,0:T(8,128)(2,1)S(1)}, bf16[128,1536]{1,0:T(8,128)(2,1)}, u32[]{:S(2)}) copy-start(bf16[128,1536]{1,0:T(8,128)(2,1)} %param.11) | copy-start | bytes 1179652
  7.2 8.0 %copy-start.4 = (f32[1536]{0:T(1024)S(1)}, f32[1536]{0:T(1024)}, u32[]{:S(2)}) copy-start(f32[1536]{0:T(1024)} %param.12) | copy-start | bytes 18436
  7.2 5.3 %copy-start.8 = (s32[128]{0:T(128)S(1)}, s32[128]{0:T(128)}, u32[]{:S(2)}) copy-start(s32[128]{0:T(128)} %param.17) | copy-start | bytes 1540
  7.2 7.2 %copy-start.5 = (s32[128,8]{0,1:T(8,128)S(1)}, s32[128,8]{0,1:T(8,128)}, u32[]{:S(2)}) copy-start(s32[128,8]{0,1:T(8,128)} %param.19) | copy-start | bytes 12292
  7.2 61.9 %all-gather.3.cloned.1.call-start = ((), (), s32[]{:S(2)}) async-start(), calls=%async_computation.2 | async-start | bytes 8650752 | tf_op jit(solution)/shard_map/all_gather | solution.py:80
  10.1 9.4 %copy-start.3 = (bf16[128,512]{1,0:T(8,128)(2,1)}, bf16[128,512]{1,0:T(8,128)(2,1)S(1)}, u32[]{:S(2)}) copy-start(bf16[128,512]{1,0:T(8,128)(2,1)S(1)} %convolution_convert_fusion.2) | copy-start | bytes 393220
  13.6 154.3 %all-gather.5.cloned.1.call-start = ((), (), s32[]{:S(2)}) async-start(), calls=%async_computation.3 | async-start | bytes 5898240 | tf_op jit(solution)/shard_map/all_gather | solution.py:122
  154.4 3.3 copy-start.6
  162.2 83.6 %all-to-all-start = ((bf16[32,64,1536]{2,1,0:T(8,128)(2,1)}), bf16[32,64,1536]{2,1,0:T(8,128)(2,1)}, u32[]{:S(2)}, u32[]{:S(2)}) async-start(bf16[32,64,1536]{2,1,0:T(8,128)(2,1)} %bitcast.116), calls=%async_computation | async-start | bytes 12582912 | tf_op jit(solution)/shard_map/all_to_all | solution.py:120
  266.4 6.1 %copy-start.7 = (f32[128,8]{0,1:T(8,128)S(1)}, f32[128,8]{0,1:T(8,128)}, u32[]{:S(2)}) copy-start(f32[128,8]{0,1:T(8,128)} %param.20) | copy-start | bytes 12292
  266.4 82.9 %all-to-all-start.1 = ((bf16[32,64,1536]{2,1,0:T(8,128)(2,1)}), bf16[32,64,1536]{2,1,0:T(8,128)(2,1)}, u32[]{:S(2)}, u32[]{:S(2)}) async-start(bf16[32,64,1536]{2,1,0:T(8,128)(2,1)} %bitcast.118), calls=%async_computation.1 | async-start | bytes 12582912 | tf_op jit(solution)/shard_map/all_to_all | solution.py:133
  380.7 14.2 %copy-start.1 = (bf16[1536,512]{1,0:T(8,128)(2,1)S(1)}, bf16[1536,512]{1,0:T(8,128)(2,1)}, u32[]{:S(2)}) copy-start(bf16[1536,512]{1,0:T(8,128)(2,1)} %param.15) | copy-start | bytes 4718596
Sparse Core Ops, SparseCore 0:
  13.8 55.3 all-gather.2
  70.8 56.2 all-gather.4
where the time goes:
time: 407 us; the launch traced here: 402 us
  waiting for transfers between devices  190 us (47%)
  matrix products  81.5 us (20%)
  local copies, waits for them, and re-layouts  63.8 us (16%)
  other arithmetic  41 us (10%)
  between operations  14.6 us (4%)
  starting transfers between devices  11 us (3%)
    all_to_all x1, waiting for transfers between devices, shards(): lax.all_to_all(outgoing, 'exp', split_axis=0, concat_axis=0, tiled=True)  77.9 us
    all_to_all x1, waiting for transfers between devices, shards(): lax.all_to_all(expert_out, 'exp', split_axis=0, concat_axis=0, tiled=True)  76.3 us
    gather x8, local copies, waits for them, and re-layouts, shards(): returned[dest_grid[:, column]].astype(jnp.float32)  42.6 us
    all_gather x1, waiting for transfers between devices, shards(): key_value_slice = lax.all_gather(stacked, 'exp', axis=1, tiled=True)  35.2 us
    dot_general x1, matrix products, shards(): jnp.einsum('tgrs,sgd->tgrd', probs.astype(jnp.bfloat16), value_tile, pref...  23.1 us
    dot_general x1, matrix products, shards(): jnp.einsum('tgrd,sgd->tgrs', query_rows_all, key_tile, preferred_element_...  21.9 us
    reduce_sum x1, other arithmetic, shards(): totals = jnp.sum(probs, axis=-1)  21.6 us
    slice x2, local copies, waits for them, and re-layouts, shards(): key_value_slice[0].reshape(feature_width, KEY_VALUE_HEADS, HEAD_SIZE)  12.1 us
  transfers between devices with their start and end apart: 4, of which 3 were waited for; matrix products, arithmetic and copies ran while one was open for 28% of the time, Pallas kernels for 0%

commit v1 on v0

v1 whole, which is shorter than its diff:
```python
import jax
import jax.numpy as jnp
from jax import lax
from jax.experimental import pallas as pl
from jax.experimental.pallas import tpu as pltpu
from jax.sharding import PartitionSpec as P

QUERY_HEADS = 24
KEY_VALUE_HEADS = 8
HEAD_SIZE = 64
TOP = 8
SIDE = 4
CHIPS = SIDE * SIDE
EXPERTS = 32
SLOTS = 64
FF = 512


epsilon = 1e-05


def rms_norm(values, gain):
    mean_square = jnp.mean(values * values, axis=-1, keepdims=True)
    return values * lax.rsqrt(mean_square + epsilon) * gain


def rotary_embedding(heads_in, stream_offsets):
    half = heads_in.shape[-1] // 2
    freqs = 10000.0 ** (-jnp.arange(half, dtype=jnp.float32) / half)
    angle = stream_offsets.astype(jnp.float32)[:, None] * freqs[None, :]
    cosine = jnp.cos(angle)[:, None, :]
    sine = jnp.sin(angle)[:, None, :]
    first_half = heads_in[..., :half]
    second_half = heads_in[..., half:]
    return jnp.concatenate(
        [first_half * cosine - second_half * sine, second_half * cosine + first_half * sine],
        axis=-1,
    )


class Plane:
    def __init__(self):
        me = lax.axis_index("exp")
        self.core = lax.rem(me, 2)
        chip = lax.div(me, 2)
        self.y = lax.div(chip, SIDE)
        self.x = lax.rem(chip, SIDE)

    def chip(self, dy, dx):
        return lax.rem(self.y + dy + SIDE, SIDE) * SIDE + lax.rem(self.x + dx + SIDE, SIDE)

    def device(self, dy, dx):
        return {"exp": self.chip(dy, dx) * 2 + self.core}

    def partner(self):
        return {"exp": self.chip(0, 0) * 2 + 1 - self.core}


def greet(plane, with_partner=False):
    barrier = pltpu.get_barrier_semaphore()
    for dy, dx in ((0, 1), (0, -1), (1, 0), (-1, 0)):
        pl.semaphore_signal(
            barrier, inc=1, device_id=plane.device(dy, dx), device_id_type=pl.DeviceIdType.MESH
        )
    if with_partner:
        pl.semaphore_signal(
            barrier, inc=1, device_id=plane.partner(), device_id_type=pl.DeviceIdType.MESH
        )
    pl.semaphore_wait(barrier, 5 if with_partner else 4)


def turn(h, a, b):
    return (b, a) if h == 0 else (a, b)


class Gather:
    COPIES = 20

    def __init__(self, plane, own, slots, send, recv, rows, slot_of):
        self.plane, self.own, self.slots = plane, own, slots
        self.send, self.recv, self.rows, self.slot_of = send, recv, rows, slot_of

    def span(self, h, part):
        half = self.rows // 2
        if part is None:
            return pl.ds(h * half, half)
        return pl.ds(h * half + part * (half // 2), half // 2)

    def step(self, k):
        if k < 4:
            return (
                ((0, 0), None, (1, 0)),
                ((0, 0), None, (-1, 0)),
                ((-1, 0), 0, (1, 0)),
                ((1, 0), 1, (-1, 0)),
            )[k]
        a = (0, -1, 1, 2)[(k - 4) // 4]
        return (
            ((a, 0), None, (0, 1)),
            ((a, 0), None, (0, -1)),
            ((a, -1), 0, (0, 1)),
            ((a, 1), 1, (0, -1)),
        )[(k - 4) % 4]

    def make(self, h, k, incoming):
        (a, b), part, (da, db) = self.step(k)
        span = self.span(h, part)
        if incoming:
            a, b = a - da, b - db
        slot = self.slot_of(self.plane.chip(*turn(h, a, b)))
        there = self.slots.at[slot, span]
        here = self.own.at[span] if (a, b) == (0, 0) else there
        return pltpu.make_async_remote_copy(
            src_ref=here,
            dst_ref=there,
            send_sem=self.send.at[h * self.COPIES + k],
            recv_sem=self.recv.at[h * self.COPIES + k],
            device_id=self.plane.device(*turn(h, da, db)),
            device_id_type=pl.DeviceIdType.MESH,
        )

    def start(self, *ks):
        for k in ks:
            for h in (0, 1):
                self.make(h, k, False).start()

    def arrive(self, k, *then):
        for h in (0, 1):
            self.make(h, k, True).wait_recv()
            for t in then:
                self.make(h, t, False).start()

    def run(self):
        self.start(0, 1)
        self.start(4, 5)
        self.arrive(0, 2, 8, 9)
        self.arrive(1, 3, 12, 13)
        self.arrive(4, 6)
        self.arrive(5, 7)
        self.arrive(2)
        self.arrive(3, 16, 17)
        for base in (8, 12, 16):
            self.arrive(base, base + 2)
            self.arrive(base + 1, base + 3)
        for base in (4, 8, 12, 16):
            self.arrive(base + 2)
            self.arrive(base + 3)

    def finish(self):
        for h in (0, 1):
            for k in range(self.COPIES):
                self.make(h, k, False).wait_send()


def gather_rows(block, collective_id):
    rows, width = block.shape

    def kernel(own, slots, send, recv, mine_sem):
        plane = Plane()
        greet(plane)
        gather = Gather(plane, own, slots, send, recv, rows, lambda chip: chip)
        mine = pltpu.make_async_copy(own, slots.at[plane.chip(0, 0)], mine_sem)
        mine.start()
        gather.run()
        gather.finish()
        mine.wait()

    return pl.pallas_call(
        kernel,
        out_shape=jax.ShapeDtypeStruct((CHIPS, rows, width), block.dtype),
        in_specs=[pl.BlockSpec(memory_space=pltpu.VMEM)],
        out_specs=pl.BlockSpec(memory_space=pl.ANY),
        scratch_shapes=[
            pltpu.SemaphoreType.DMA((2 * Gather.COPIES,)),
            pltpu.SemaphoreType.DMA((2 * Gather.COPIES,)),
            pltpu.SemaphoreType.DMA,
        ],
        compiler_params=pltpu.CompilerParams(collective_id=collective_id, has_side_effects=True),
        name="gather_rows",
    )(block)


class Scatter:
    COPIES = 20

    def __init__(self, plane, parts, hold, send, recv, rows):
        self.plane, self.parts, self.hold = plane, parts, hold
        self.send, self.recv, self.rows = send, recv, rows

    def span(self, h, part):
        half = self.rows // 2
        if part is None:
            return pl.ds(h * half, half)
        return pl.ds(h * half + part * (half // 2), half // 2)

    def step(self, k):
        if k < 16:
            q = (2, 1, 3, 0)[k // 4]
            return (
                ((2, q), 0, (1, 0)),
                ((2, q), 1, (-1, 0)),
                ((1, q), None, (1, 0)),
                ((3, q), None, (-1, 0)),
            )[k % 4]
        return (
            ((0, 2), 0, (0, 1)),
            ((0, 2), 1, (0, -1)),
            ((0, 1), None, (0, 1)),
            ((0, 3), None, (0, -1)),
        )[k % 4]

    def make(self, h, k):
        (a, b), part, (da, db) = self.step(k)
        span = self.span(h, part)
        size = self.rows // 2 if part is None else self.rows // 4
        return pltpu.make_async_remote_copy(
            src_ref=self.parts.at[self.plane.chip(*turn(h, a, b)), span],
            dst_ref=self.hold.at[h, k, pl.ds(0, size)],
            send_sem=self.send.at[h * self.COPIES + k],
            recv_sem=self.recv.at[h * self.COPIES + k],
            device_id=self.plane.device(*turn(h, da, db)),
            device_id_type=pl.DeviceIdType.MESH,
        )

    def start(self, k):
        for h in (0, 1):
            self.make(h, k).start()

    def add(self, h, k, place, part):
        size = self.rows // 4
        at = (self.plane.chip(*turn(h, *place)), self.span(h, part))
        self.parts[at] = (
            self.parts[at].astype(jnp.float32)
            + self.hold[h, k, pl.ds(0, size)].astype(jnp.float32)
        ).astype(jnp.bfloat16)

    def relay(self, base, near, far):
        for h in (0, 1):
            self.make(h, base).wait_recv()
            self.add(h, base, near, 0)
            self.make(h, base + 2).start()
        for h in (0, 1):
            self.make(h, base + 1).wait_recv()
            self.add(h, base + 1, far, 1)
            self.make(h, base + 3).start()

    def total(self, h, base, place):
        self.make(h, base + 2).wait_recv()
        self.make(h, base + 3).wait_recv()
        at = (self.plane.chip(*turn(h, *place)), self.span(h, None))
        return (
            self.parts[at].astype(jnp.float32)
            + self.hold[h, base + 2].astype(jnp.float32)
            + self.hold[h, base + 3].astype(jnp.float32)
        )

    def run(self, out):
        for i in range(4):
            self.start(4 * i)
            self.start(4 * i + 1)
        for i, q in enumerate((2, 1, 3, 0)):
            self.relay(4 * i, (1, q), (3, q))
        for i, q in enumerate((2, 1, 3, 0)):
            for h in (0, 1):
                at = (self.plane.chip(*turn(h, 0, q)), self.span(h, None))
                self.parts[at] = self.total(h, 4 * i, (0, q)).astype(jnp.bfloat16)
            if i == 0:
                self.start(16)
                self.start(17)
            if i == 2:
                self.relay(16, (0, 1), (0, 3))
        for h in (0, 1):
            out[self.span(h, None)] = self.total(h, 16, (0, 0))

    def finish(self):
        for h in (0, 1):
            for k in range(self.COPIES):
                self.make(h, k).wait_send()


def scatter_sums(parts, collective_id):
    _, rows, width = parts.shape

    def kernel(given, out, held, hold, send, recv, in_sem):
        load = pltpu.make_async_copy(given, held, in_sem)
        load.start()
        plane = Plane()
        greet(plane)
        load.wait()
        scatter = Scatter(plane, held, hold, send, recv, rows)
        scatter.run(out)
        scatter.finish()

    return pl.pallas_call(
        kernel,
        out_shape=jax.ShapeDtypeStruct((rows, width), jnp.float32),
        in_specs=[pl.BlockSpec(memory_space=pl.ANY)],
        out_specs=pl.BlockSpec(memory_space=pltpu.VMEM),
        scratch_shapes=[
            pltpu.VMEM((CHIPS, rows, width), jnp.bfloat16),
            pltpu.VMEM((2, Scatter.COPIES, rows // 2, width), jnp.bfloat16),
            pltpu.SemaphoreType.DMA((2 * Scatter.COPIES,)),
            pltpu.SemaphoreType.DMA((2 * Scatter.COPIES,)),
            pltpu.SemaphoreType.DMA,
        ],
        compiler_params=pltpu.CompilerParams(
            collective_id=collective_id, has_side_effects=True, vmem_limit_bytes=60 << 20
        ),
        name="scatter_sums",
    )(parts)


BLOCKS = 4


def expert_kernel(ranks, gains, rows_in, own, other, out, weights, picked, made, sems):
    step = pl.program_id(0)

    def loads():
        for e, source in enumerate((own, other)):
            for r in range(4):
                yield pltpu.make_async_copy(
                    source.at[r],
                    weights.at[e, :, :, pl.ds(r * 128, 128)],
                    sems.at[e * 4 + r],
                )

    @pl.when(step == 0)
    def _():
        for load in loads():
            load.start()

    tokens = rows_in.shape[1]
    slot = lax.broadcasted_iota(jnp.int32, (SLOTS, tokens), 0).astype(jnp.float32)

    def hits(j):
        return jnp.concatenate([ranks[j, e : e + 1, :] == slot for e in (0, 1)], axis=0)

    for j in range(BLOCKS):
        choose = jnp.where(hits(j), 1.0, 0.0).astype(jnp.bfloat16)
        picked[j] = jnp.dot(choose, rows_in[j], preferred_element_type=jnp.float32).astype(
            jnp.bfloat16
        )

    @pl.when(step == 0)
    def _():
        for load in loads():
            load.wait()

    width = rows_in.shape[2]
    for e in (0, 1):
        rows = picked[:, e * SLOTS : (e + 1) * SLOTS, :].reshape(BLOCKS * SLOTS, width)
        gate = jnp.dot(rows, weights[e, 0], preferred_element_type=jnp.float32)
        up = jnp.dot(rows, weights[e, 1], preferred_element_type=jnp.float32)
        units = (gate / (1.0 + jnp.exp(-gate)) * up).astype(jnp.bfloat16)
        result = lax.dot_general(
            units, weights[e, 2], (((1,), (1,)), ((), ())), preferred_element_type=jnp.float32
        )
        for j in range(BLOCKS):
            gain = jnp.sum(
                jnp.where(ranks[j, e : e + 1, :] == slot, gains[j, e : e + 1, :], 0.0),
                axis=1,
                keepdims=True,
            )
            made[j, e * SLOTS : (e + 1) * SLOTS, :] = (
                result[j * SLOTS : (j + 1) * SLOTS, :] * gain
            ).astype(jnp.bfloat16)

    for j in range(BLOCKS):
        choose = jnp.where(hits(j), 1.0, 0.0).astype(jnp.bfloat16)
        out[j] = lax.dot_general(
            choose, made[j], (((0,), (0,)), ((), ())), preferred_element_type=jnp.float32
        ).astype(jnp.bfloat16)


def run_experts(ranks, gains, rows_in, own, other):
    chips, tokens, width = rows_in.shape
    return pl.pallas_call(
        expert_kernel,
        grid=(chips // BLOCKS,),
        out_shape=jax.ShapeDtypeStruct(rows_in.shape, jnp.bfloat16),
        in_specs=[
            pl.BlockSpec((BLOCKS, 2, tokens), lambda i: (i, 0, 0)),
            pl.BlockSpec((BLOCKS, 2, tokens), lambda i: (i, 0, 0)),
            pl.BlockSpec((BLOCKS, tokens, width), lambda i: (i, 0, 0)),
            pl.BlockSpec(memory_space=pl.ANY),
            pl.BlockSpec(memory_space=pl.ANY),
        ],
        out_specs=pl.BlockSpec((BLOCKS, tokens, width), lambda i: (i, 0, 0)),
        scratch_shapes=[
            pltpu.VMEM((2, 3, width, FF), jnp.bfloat16),
            pltpu.VMEM((BLOCKS, 2 * SLOTS, width), jnp.bfloat16),
            pltpu.VMEM((BLOCKS, 2 * SLOTS, width), jnp.bfloat16),
            pltpu.SemaphoreType.DMA((8,)),
        ],
        compiler_params=pltpu.CompilerParams(vmem_limit_bytes=60 << 20),
        name="experts",
    )(ranks, gains, rows_in, own, other)


def slot_tables(routes, route_weights):
    tokens = routes.shape[0]
    hit = routes[None] == jnp.arange(EXPERTS, dtype=jnp.int32)[:, None, None]
    gains = jnp.sum(jnp.where(hit, route_weights[None], 0.0), axis=2)
    named = jnp.any(hit, axis=2)
    earlier = jnp.triu(jnp.ones((tokens, tokens), jnp.bfloat16), 1)
    ranks = jnp.dot(named.astype(jnp.bfloat16), earlier, preferred_element_type=jnp.float32)
    return jnp.where(named, ranks, -1.0), gains


def shards(
    hidden,
    attn_gain,
    query_weight,
    key_matrix,
    value_matrix,
    output_weight,
    prompt_start,
    ffn_gain,
    routes,
    route_weights,
    expert_weights,
):
    total_row_count = hidden.shape[0]
    lane_index = lax.axis_index("exp")
    heads_per_group = QUERY_HEADS // KEY_VALUE_HEADS

    tables = jnp.stack(slot_tables(routes, route_weights))
    tables = lax.all_gather(tables, "exp", axis=0)
    weight_piece = lax.all_gather(expert_weights[0], "req", axis=0)
    weight_other = lax.ppermute(weight_piece, "exp", [(i, i ^ 1) for i in range(EXPERTS)])
    tables = lax.dynamic_index_in_dim(
        tables.reshape(CHIPS, 2, 2, CHIPS, 2, total_row_count),
        lax.rem(lane_index, 2),
        1,
        keepdims=False,
    )
    tables = lax.dynamic_index_in_dim(tables, lax.div(lane_index, 2), 2, keepdims=False)
    tables = jnp.where(lax.rem(lane_index, 2) == 0, tables, tables[:, :, ::-1])

    positions = lane_index * total_row_count + jnp.arange(total_row_count, dtype=jnp.int32)
    stream_offsets = positions - prompt_start
    inputs = hidden.astype(jnp.float32)
    normalized_input = rms_norm(inputs, attn_gain).astype(jnp.bfloat16)
    query_rows_all = jnp.dot(
        normalized_input, query_weight, preferred_element_type=jnp.float32
    ).reshape(total_row_count, QUERY_HEADS, HEAD_SIZE)
    query_rows_all = (
        rotary_embedding(query_rows_all, stream_offsets)
        .astype(jnp.bfloat16)
        .reshape(total_row_count, KEY_VALUE_HEADS, heads_per_group, HEAD_SIZE)
    )
    shard_keys = jnp.dot(normalized_input, key_matrix, preferred_element_type=jnp.float32).reshape(
        total_row_count, KEY_VALUE_HEADS, HEAD_SIZE
    )
    shard_keys = (
        rotary_embedding(shard_keys, stream_offsets)
        .astype(jnp.bfloat16)
        .reshape(total_row_count, KEY_VALUE_HEADS * HEAD_SIZE)
    )
    values_local = jnp.dot(
        normalized_input, value_matrix, preferred_element_type=jnp.float32
    ).astype(jnp.bfloat16)
    stacked = jnp.stack([shard_keys, values_local])
    key_value_slice = lax.all_gather(stacked, "exp", axis=1, tiled=True)
    feature_width = key_value_slice.shape[1]
    key_tile = key_value_slice[0].reshape(feature_width, KEY_VALUE_HEADS, HEAD_SIZE)
    value_tile = key_value_slice[1].reshape(feature_width, KEY_VALUE_HEADS, HEAD_SIZE)
    key_pos = jnp.arange(feature_width, dtype=jnp.int32)
    scores = jnp.einsum(
        "tgrd,sgd->tgrs", query_rows_all, key_tile, preferred_element_type=jnp.float32
    ) * HEAD_SIZE ** (-0.5)
    valid = (key_pos[None, :] >= prompt_start[:, None]) & (key_pos[None, :] <= positions[:, None])
    valid = valid[:, None, None, :]
    masked = jnp.where(valid, scores, jnp.float32(-1e30))
    new_max = jnp.max(masked, axis=-1)
    probs = jnp.where(valid, jnp.exp(masked - new_max[..., None]), jnp.float32(0.0))
    totals = jnp.sum(probs, axis=-1)
    attention_mixed = jnp.einsum(
        "tgrs,sgd->tgrd", probs.astype(jnp.bfloat16), value_tile, preferred_element_type=jnp.float32
    )
    attention = (
        (attention_mixed / totals[..., None])
        .reshape(total_row_count, QUERY_HEADS * HEAD_SIZE)
        .astype(jnp.bfloat16)
    )
    residual = inputs + jnp.dot(attention, output_weight, preferred_element_type=jnp.float32)
    moe_in = rms_norm(residual, ffn_gain).astype(jnp.bfloat16)

    rows_in = gather_rows(moe_in, 1)
    parts = run_experts(tables[:, 0], tables[:, 1], rows_in, weight_piece, weight_other)
    moe_sum = scatter_sums(parts, 2)
    layer_out = (residual + moe_sum).astype(jnp.bfloat16)
    return (layer_out, stacked[0], stacked[1])


def solution(mesh):
    in_specs = (
        P(("req", "exp"), None),
        P(),
        P(),
        P(),
        P(),
        P(),
        P(("req", "exp")),
        P(),
        P(("req", "exp"), None),
        P(("req", "exp"), None),
        P("exp", None, None, "req"),
    )
    out_specs = (P(("req", "exp"), None), P(("req", "exp"), None), P(("req", "exp"), None))
    return jax.shard_map(shards, mesh=mesh, in_specs=in_specs, out_specs=out_specs, check_vma=False)
```

time: 407 us -> 337 us (0.83)
  Pallas kernels: 0 us -> 98.6 us
  waiting for transfers between devices: 190 us -> 141 us
  local copies, waits for them, and re-layouts: 63.8 us -> 21 us
  other arithmetic: 41 us -> 9.23 us
  matrix products: 81.5 us -> 51.2 us
  starting transfers between devices: 11 us -> 0.12 us
    all_to_all x2 -> x0, waiting for transfers between devices: 154 us -> none  [the longest x1 77.9 us: shards(): lax.all_to_all(outgoing, 'exp', split_axis=0, concat_axis=0, tiled=True)]
    pallas_call x0 -> x3, Pallas kernels: none -> 98.6 us  [the longest x1 39.4 us: scatter_sums(): pl.pallas_call(kernel, out_shape=jax.ShapeDtypeStruct((rows, width), jnp....]
    all_gather x1 -> x2, waiting for transfers between devices: 0.02 us -> 84.3 us  [the longest x1 51.7 us: shards(): weight_piece = lax.all_gather(expert_weights[0], 'req', axis=0)]
    dot_general x4 -> x1, matrix products: 47 us -> 0.13 us  [slot_tables(): jnp.dot(named.astype(jnp.bfloat16), earlier, preferred_element_type=jnp.f...]
    gather x8 -> x0, local copies, waits for them, and re-layouts: 42.6 us -> none  [shards(): returned[dest_grid[:, column]].astype(jnp.float32)]
    sub x0 -> x1, matrix products: none -> 26.6 us  [shards(): masked - new_max[..., None]]
    reduce_sum x2 -> x1, other arithmetic: 21.6 us -> 0.75 us  [slot_tables(): gains = jnp.sum(jnp.where(hit, route_weights[None], 0.0), axis=2)]
    all_gather x1, waiting for transfers between devices: 35.2 us -> 56 us  [shards(): key_value_slice = lax.all_gather(stacked, 'exp', axis=1, tiled=True)]
  transfers between devices with their start and end apart: 4 -> 4, of which waited for: 3 -> 3; matrix products, arithmetic and copies ran while one was open for 28% -> 23% of each run, Pallas kernels for 0% -> 11%
where the time goes in v1:
time: 337 us; the launch traced here: 335 us
  waiting for transfers between devices  141 us (42%)
  Pallas kernels  98.6 us (29%)
  matrix products  51.2 us (15%)
  local copies, waits for them, and re-layouts  21 us (6%)
  between operations  14 us (4%)
  other arithmetic  9.23 us (3%)
    all_gather x1, waiting for transfers between devices, shards(): key_value_slice = lax.all_gather(stacked, 'exp', axis=1, tiled=True)  56 us
    all_gather x1, waiting for transfers between devices, shards(): weight_piece = lax.all_gather(expert_weights[0], 'req', axis=0)  51.7 us
    pallas_call x1, Pallas kernels, scatter_sums(): pl.pallas_call(kernel, out_shape=jax.ShapeDtypeStruct((rows, width), jnp....  39.4 us
    pallas_call x1, Pallas kernels, gather_rows(): pl.pallas_call(kernel, out_shape=jax.ShapeDtypeStruct((CHIPS, rows, width...  37.9 us
    all_gather x1, waiting for transfers between devices, shards(): tables = lax.all_gather(tables, 'exp', axis=0)  32.7 us
    sub x1, matrix products, shards(): masked - new_max[..., None]  26.6 us
    pallas_call x1, Pallas kernels, run_experts(): pl.pallas_call(expert_kernel, grid=(chips // BLOCKS,), out_shape=jax.Shap...  21.4 us
    dot_general x1, matrix products, shards(): jnp.einsum('tgrs,sgd->tgrd', probs.astype(jnp.bfloat16), value_tile, pref...  13.2 us
  transfers between devices with their start and end apart: 4, of which 3 were waited for; matrix products, arithmetic and copies ran while one was open for 23% of the time, Pallas kernels for 11%

profile of v1, /device:TPU:0, one launch (start us, length us, event | category | flops | bytes accessed | tf_op | source)
XLA Modules:
  0.0 335.2 jit_solution(8610308742565796753)
XLA Ops:
  7.3 0.9 fusion.24
  8.1 0.7 select_reduce_fusion
  10.4 1.2 fusion.20
  12.4 1.8 fusion.40
  14.4 1.8 convolution_convert_fusion
  16.3 0.7 pad_maximum_fusion.1
  17.1 0.8 copy.49
  17.8 4.3 %fusion.37 = f32[128,1536]{0,1:T(8,128)S(1)} fusion(bf16[1536,1536]{1,0:T(8,128)(2,1)} %param.13, bf16[128,1536]{1,0:T(8,128)(2,1)S(1)} %copy-done.2, f32[1536]{0:T(1024)S(1)} %copy-done.4, f32[128]{0:T(128)S(1)} %add_rsqrt_fusion.1), kind=kOutput, calls=%fused_computation.62 | convolution fusion | flops 604766208 | bytes 5904896 | tf_op jit(solution)/shard_map/dot_general | solution.py:445
  22.8 32.7 %all-gather.9.cloned.1.call-done = f32[64,32,128]{2,1,0:T(8,128)} async-done(((f32[2,32,128]{2,1,0:T(8,128)}), f32[64,32,128]{2,1,0:T(8,128)}) %all-gather.9.cloned.1.call-update) | async-done | bytes 1048592 | tf_op jit(solution)/shard_map/all_gather | solution.py:429
  55.4 0.8 copy_bitcast_fusion
  56.3 0.8 broadcast_select_fusion
  57.7 51.7 %all-gather.7.cloned.1.call-done.own = bf16[4,3,1536,128]{3,2,1,0:T(8,128)(2,1)} async-done(((bf16[1,3,1536,128]{3,2,1,0:T(8,128)(2,1)}), bf16[4,3,1536,128]{3,2,1,0:T(8,128)(2,1)}) %all-gather.7.cloned.1.call-update) | async-done | bytes 4718608 | tf_op jit(solution)/shard_map/all_gather | solution.py:430
  109.4 56.0 %all-gather.5.cloned.1.call-done = bf16[2,4096,512]{2,1,0:T(8,128)(2,1)} async-done(((bf16[2,128,512]{2,1,0:T(8,128)(2,1)}), bf16[2,4096,512]{2,1,0:T(8,128)(2,1)}) %all-gather.5.cloned.1.call-update) | async-done | bytes 8388624 | tf_op jit(solution)/shard_map/all_gather | solution.py:465
  165.4 5.8 %fusion.42 = (bf16[1,4096,512]{2,1,0:T(8,128)(2,1)}, bf16[1,4096,512]{2,1,0:T(8,128)(2,1)}) fusion(bf16[2,4096,512]{2,1,0:T(8,128)(2,1)} %all-gather.5.cloned.1.call-done), kind=kLoop, calls=%fused_computation.64 | loop fusion | bytes 16777216 | tf_op jit(solution)/shard_map/slice | solution.py:467
  171.1 6.4 %copy.45 = bf16[1,4096,512]{1,2,0:T(8,128)(2,1)} copy(bf16[1,4096,512]{2,1,0:T(8,128)(2,1)} %get-tuple-element.12) | data formatting | bytes 8388608 | tf_op jit(solution)/shard_map/slice | solution.py:467
  177.6 26.6 %fusion.43 = (f32[128,8,3]{0,2,1:T(4,128)S(1)}, bf16[128,8,3,4096]{0,3,2,1:T(8,128)(2,1)}) fusion(bf16[4096,8,64,1]{0,2,3,1:T(8,128)(2,1)} %bitcast.58, pred[128,4096]{0,1:T(8,128)(4,1)S(1)} %fusion.9, bf16[128,8,3,32]{0,3,2,1:T(8,128)(2,1)S(1)} %bitcast.65, bf16[128,8,3,32]{0,3,2,1:T(8,128)(2,1)S(1)} %bitcast.64), kind=kOutput, calls=%fused_computation.65 | convolution fusion | flops 1686900736 | bytes 30289920 | tf_op jit(solution)/shard_map/sub | solution.py:477
  204.2 6.4 %copy.44 = bf16[1,4096,512]{1,2,0:T(8,128)(2,1)} copy(bf16[1,4096,512]{2,1,0:T(8,128)(2,1)} %get-tuple-element.13) | data formatting | bytes 8388608 | tf_op jit(solution)/shard_map/slice | solution.py:468
  210.6 13.2 %fusion.16 = bf16[128,8,3,64]{0,3,2,1:T(8,128)(2,1)S(1)} fusion(bf16[4096,8,64,1]{0,2,3,1:T(8,128)(2,1)} %bitcast.57, bf16[128,8,3,4096]{0,3,2,1:T(8,128)(2,1)} %get-tuple-element.23, f32[128,8,3]{0,2,1:T(4,128)S(1)} %get-tuple-element.22), kind=kOutput, calls=%fused_computation.16 | convolution fusion | flops 1611005952 | bytes 29765632 | tf_op jit(solution)/shard_map/tgrs,sgd->tgrd/dot_general | solution.py:479
  223.9 3.2 multiply_reduce_fusion
  227.2 0.9 multiply_convert_fusion.own
  228.0 37.9 %gather_rows.1.rows_in = bf16[16,128,1536]{2,1,0:T(8,128)(2,1)} custom-call(bf16[128,1536]{1,0:T(8,128)(2,1)} %multiply_convert_fusion.own), custom_call_target="tpu_custom_call" | custom-call | tf_op jit(solution)/shard_map/gather_rows/pallas_call | solution.py:168
  265.9 21.4 %experts.1.given = bf16[16,128,1536]{2,1,0:T(8,128)(2,1)} custom-call(f32[16,2,128]{2,1,0:T(2,128)} %get-tuple-element.19.ranks, f32[16,2,128]{2,1,0:T(2,128)} %get-tuple-element.18.gains, bf16[16,128,1536]{2,1,0:T(8,128)(2,1)} %gather_rows.1.rows_in, bf16[4,3,1536,128]{3,2,1,0:T(8,128)(2,1)} %all-gather.7.cloned.1.call-done.own, ...), custom_call_target="tpu_custom_call" | custom-call | tf_op jit(solution)/shard_map/experts/pallas_call | solution.py:378
  287.3 39.4 %scatter_sums.1 = f32[128,1536]{1,0:T(8,128)} custom-call(bf16[16,128,1536]{2,1,0:T(8,128)(2,1)} %experts.1.given), custom_call_target="tpu_custom_call" | custom-call | tf_op jit(solution)/shard_map/scatter_sums/pallas_call | solution.py:294
  326.7 2.0 add_convert_fusion
  (36 shorter events, 3.9 us)
Async XLA Ops:
  7.2 5.3 %copy-start = (bf16[1536,512]{1,0:T(8,128)(2,1)S(1)}, bf16[1536,512]{1,0:T(8,128)(2,1)}, u32[]{:S(2)}) copy-start(bf16[1536,512]{1,0:T(8,128)(2,1)} %param.14) | copy-start | bytes 4718596
  7.2 7.2 %copy-start.2 = (bf16[128,1536]{1,0:T(8,128)(2,1)S(1)}, bf16[128,1536]{1,0:T(8,128)(2,1)}, u32[]{:S(2)}) copy-start(bf16[128,1536]{1,0:T(8,128)(2,1)} %param.11) | copy-start | bytes 1179652
  7.2 7.2 %copy-start.4 = (f32[1536]{0:T(1024)S(1)}, f32[1536]{0:T(1024)}, u32[]{:S(2)}) copy-start(f32[1536]{0:T(1024)} %param.12) | copy-start | bytes 18436
  7.2 48.2 %all-gather.9.cloned.1.call-start = ((), (), s32[]{:S(2)}) async-start(), calls=%async_computation.2 | async-start | bytes 1081344 | tf_op jit(solution)/shard_map/all_gather | solution.py:429
  9.6 99.7 %all-gather.7.cloned.1.call-start = ((), (), s32[]{:S(2)}) async-start(), calls=%async_computation.1 | async-start | bytes 5898240 | tf_op jit(solution)/shard_map/all_gather | solution.py:430
  10.4 155.0 %all-gather.5.cloned.1.call-start = ((), (), s32[]{:S(2)}) async-start(), calls=%async_computation | async-start | bytes 8650752 | tf_op jit(solution)/shard_map/all_gather | solution.py:465
  14.4 7.9 %copy-start.6 = (s32[128]{0:T(128)S(1)}, s32[128]{0:T(128)}, u32[]{:S(2)}) copy-start(s32[128]{0:T(128)} %param.17) | copy-start | bytes 1540
  16.3 154.9 %copy-start.3 = (bf16[128,512]{1,0:T(8,128)(2,1)}, bf16[128,512]{1,0:T(8,128)(2,1)S(1)}, u32[]{:S(2)}) copy-start(bf16[128,512]{1,0:T(8,128)(2,1)S(1)} %convolution_convert_fusion) | copy-start | bytes 393220
  109.4 156.6 %collective-permute-start = (bf16[4,3,1536,128]{3,2,1,0:T(8,128)(2,1)}, bf16[4,3,1536,128]{3,2,1,0:T(8,128)(2,1)}, u32[]{:S(2)}, u32[]{:S(2)}) collective-permute-start(bf16[4,3,1536,128]{3,2,1,0:T(8,128)(2,1)} %all-gather.7.cloned.1.call-done.own), channel_id=1, source_target_pairs={{0,1},{1,0},{2,3},{3,2},{4,5},{5,4},{6,7},{7,6},{8,9},{9,8},{10,11... | collective-permute-start | bytes 14155784 | tf_op jit(solution)/shard_map/ppermute | solution.py:431
  223.9 3.3 copy-start.5
  265.9 62.7 %copy-start.1 = (bf16[1536,512]{1,0:T(8,128)(2,1)S(1)}, bf16[1536,512]{1,0:T(8,128)(2,1)}, u32[]{:S(2)}) copy-start(bf16[1536,512]{1,0:T(8,128)(2,1)} %param.14) | copy-start | bytes 4718596
Sparse Core Ops, SparseCore 0:
  10.3 45.0 all-gather.8
  57.1 52.2 all-gather.6
  112.2 53.0 all-gather.4

commit v2 on v1

--- a/solution.py
+++ b/solution.py
@@ -56,9 +56,13 @@
         return {"exp": self.chip(0, 0) * 2 + 1 - self.core}
 
 
-def greet(plane, with_partner=False):
+NEXT = ((0, 1), (0, -1), (1, 0), (-1, 0))
+OTHERS = tuple((dy, dx) for dy in range(SIDE) for dx in range(SIDE) if dy or dx)
+
+
+def greet(plane, places=NEXT, with_partner=False):
     barrier = pltpu.get_barrier_semaphore()
-    for dy, dx in ((0, 1), (0, -1), (1, 0), (-1, 0)):
+    for dy, dx in places:
         pl.semaphore_signal(
             barrier, inc=1, device_id=plane.device(dy, dx), device_id_type=pl.DeviceIdType.MESH
         )
@@ -66,7 +70,7 @@
         pl.semaphore_signal(
             barrier, inc=1, device_id=plane.partner(), device_id_type=pl.DeviceIdType.MESH
         )
-    pl.semaphore_wait(barrier, 5 if with_partner else 4)
+    pl.semaphore_wait(barrier, len(places) + int(with_partner))
 
 
 def turn(h, a, b):
@@ -76,9 +80,10 @@
 class Gather:
     COPIES = 20
 
-    def __init__(self, plane, own, slots, send, recv, rows, slot_of):
+    def __init__(self, plane, own, slots, send, recv, rows, slot_of, ready=None):
         self.plane, self.own, self.slots = plane, own, slots
         self.send, self.recv, self.rows, self.slot_of = send, recv, rows, slot_of
+        self.ready = ready or (lambda h, a, b: None)
 
     def span(self, h, part):
         half = self.rows // 2
@@ -129,10 +134,15 @@
             self.make(h, k, True).wait_recv()
             for t in then:
                 self.make(h, t, False).start()
+            (a, b), part, (da, db) = self.step(k)
+            if part != 0:
+                self.ready(h, a - da, b - db)
 
     def run(self):
         self.start(0, 1)
         self.start(4, 5)
+        self.ready(0, 0, 0)
+        self.ready(1, 0, 0)
         self.arrive(0, 2, 8, 9)
         self.arrive(1, 3, 12, 13)
         self.arrive(4, 6)
@@ -178,6 +188,201 @@
         compiler_params=pltpu.CompilerParams(collective_id=collective_id, has_side_effects=True),
         name="gather_rows",
     )(block)
+
+
+def gather_keys_values(block, tables, collective_id):
+    rows, width = block.shape
+
+    def kernel(own, given, slots, held, send, recv, give, take, lend, borrow, sems):
+        plane = Plane()
+        greet(plane, OTHERS, True)
+        here = plane.chip(0, 0)
+
+        def share(h, a, b, incoming=False):
+            place = turn(h, a, b)
+            half = pl.ds(h * (rows // 2), rows // 2)
+            core = 1 - plane.core if incoming else plane.core
+            there = slots.at[plane.chip(*place) * 2 + core, half]
+            at = h * CHIPS + (a % SIDE) * SIDE + b % SIDE
+            return pltpu.make_async_remote_copy(
+                src_ref=own.at[half] if (a, b) == (0, 0) and not incoming else there,
+                dst_ref=there,
+                send_sem=lend.at[at],
+                recv_sem=borrow.at[at],
+                device_id=plane.partner(),
+                device_id_type=pl.DeviceIdType.MESH,
+            )
+
+        def table(n, incoming):
+            dy, dx = OTHERS[n]
+            return pltpu.make_async_remote_copy(
+                src_ref=given.at[plane.chip(dy, dx)],
+                dst_ref=held.at[plane.chip(-dy, -dx) if incoming else here],
+                send_sem=give.at[n],
+                recv_sem=take.at[n],
+                device_id=plane.device(dy, dx),
+                device_id_type=pl.DeviceIdType.MESH,
+            )
+
+        gather = Gather(
+            plane,
+            own,
+            slots,
+            send,
+            recv,
+            rows,
+            lambda chip: chip * 2 + plane.core,
+            lambda h, a, b: share(h, a, b).start(),
+        )
+        mine = pltpu.make_async_copy(own, slots.at[here * 2 + plane.core], sems.at[0])
+        mine.start()
+        row = pltpu.make_async_copy(given.at[here], held.at[here], sems.at[1])
+        row.start()
+        gather.run()
+        for n in range(len(OTHERS)):
+            table(n, False).start()
+        gather.finish()
+        mine.wait()
+        row.wait()
+        for n in range(len(OTHERS)):
+            table(n, True).wait_recv()
+            table(n, False).wait_send()
+        for h in (0, 1):
+            for a in range(SIDE):
+                for b in range(SIDE):
+                    share(h, a, b, True).wait_recv()
+                    share(h, a, b).wait_send()
+
+    return pl.pallas_call(
+        kernel,
+        out_shape=(
+            jax.ShapeDtypeStruct((2 * CHIPS, rows, width), block.dtype),
+            jax.ShapeDtypeStruct(tables.shape, tables.dtype),
+        ),
+        in_specs=[pl.BlockSpec(memory_space=pltpu.VMEM)] * 2,
+        out_specs=(pl.BlockSpec(memory_space=pl.ANY), pl.BlockSpec(memory_space=pltpu.VMEM)),
+        scratch_shapes=[
+            pltpu.SemaphoreType.DMA((2 * Gather.COPIES,)),
+            pltpu.SemaphoreType.DMA((2 * Gather.COPIES,)),
+            pltpu.SemaphoreType.DMA((len(OTHERS),)),
+            pltpu.SemaphoreType.DMA((len(OTHERS),)),
+            pltpu.SemaphoreType.DMA((2 * CHIPS,)),
+            pltpu.SemaphoreType.DMA((2 * CHIPS,)),
+            pltpu.SemaphoreType.DMA((2,)),
+        ],
+        compiler_params=pltpu.CompilerParams(collective_id=collective_id, has_side_effects=True),
+        name="gather_keys_values",
+    )(block, tables)
+
+
+KEYS = 512
+PAIR = 6
+LOW = -1e30
+SCALE = HEAD_SIZE**-0.5 * 1.4426950408889634
+
+
+def attention_kernel(bounds, queries, keys, values, starts, out, packed, peak, total):
+    rows = queries.shape[0]
+    lane = lax.broadcasted_iota(jnp.int32, (rows, 128), 1)
+    low_half = lane < HEAD_SIZE
+    for n in range(PAIR):
+        tile = queries[:, (n // 2) * 128 : (n // 2 + 1) * 128].astype(jnp.float32)
+        group = n // 3
+        if n % 2 != group:
+            tile = pltpu.roll(tile, HEAD_SIZE, axis=1)
+        keep = low_half if group == 0 else jnp.logical_not(low_half)
+        packed[n * rows : (n + 1) * rows, :] = jnp.where(keep, tile, 0.0).astype(jnp.bfloat16)
+    peak[...] = jnp.full_like(peak, LOW)
+    total[...] = jnp.zeros_like(total)
+    first, last, inner, base = bounds[0], bounds[1], bounds[2], bounds[3]
+    half = PAIR // 2 * rows
+
+    def block(at, masked):
+        at = pl.multiple_of(at * KEYS, KEYS)
+        key = keys[pl.ds(at, KEYS), :]
+        value = values[pl.ds(at, KEYS), :]
+        key_lane = lax.broadcasted_iota(jnp.int32, (KEYS, 128), 1)
+        if masked:
+            key_pos = at + lax.broadcasted_iota(jnp.int32, (rows, KEYS), 1)
+            own_pos = base + lax.broadcasted_iota(jnp.int32, (rows, KEYS), 0)
+            valid = (key_pos >= starts[...]) & (key_pos <= own_pos)
+        for group in (0, 1):
+            span = pl.ds(group * half, half)
+            scores = lax.dot_general(
+                packed[span, :], key, (((1,), (1,)), ((), ())), preferred_element_type=jnp.float32
+            )
+            if masked:
+                scores = jnp.where(
+                    valid[None], scores.reshape(PAIR // 2, rows, KEYS), LOW
+                ).reshape(half, KEYS)
+            before = peak[span, :]
+            now = jnp.maximum(before, jnp.max(scores, axis=1, keepdims=True))
+            peak[span, :] = now
+            fade = jnp.exp2((before - now) * SCALE)
+            probs = jnp.exp2((scores - now[:, :1]) * SCALE).astype(jnp.bfloat16)
+            own_half = (key_lane < HEAD_SIZE) == (group == 0)
+            beside = jnp.where(own_half, value, jnp.ones_like(value))
+            total[span, :] = total[span, :] * fade + jnp.dot(
+                probs, beside, preferred_element_type=jnp.float32
+            )
+
+    def visit(at, carry):
+        edge = (at == last) | (at * KEYS < inner)
+
+        @pl.when(edge)
+        def _():
+            block(at, True)
+
+        @pl.when(jnp.logical_not(edge))
+        def _():
+            block(at, False)
+
+        return carry
+
+    lax.fori_loop(first, last + 1, visit, 0)
+
+    def head(n):
+        sums = total[n * rows : (n + 1) * rows, :]
+        result = sums / pltpu.roll(sums, HEAD_SIZE, axis=1)
+        if n % 2 != n // 3:
+            result = pltpu.roll(result, HEAD_SIZE, axis=1)
+        return result
+
+    for i in range(PAIR // 2):
+        out[:, i * 128 : (i + 1) * 128] = jnp.where(low_half, head(2 * i), head(2 * i + 1)).astype(
+            out.dtype
+        )
+
+
+def attend(queries, keys_values, prompt_start, base):
+    rows, width = queries.shape
+    span = PAIR * HEAD_SIZE
+    pairs = width // span
+    keys_values = keys_values.reshape(-1, keys_values.shape[-1])
+    length = keys_values.shape[0]
+    bounds = jnp.stack([prompt_start[0] // KEYS, base // KEYS, prompt_start[rows - 1], base])
+    return pl.pallas_call(
+        attention_kernel,
+        out_shape=jax.ShapeDtypeStruct((rows, width), jnp.bfloat16),
+        grid_spec=pltpu.PrefetchScalarGridSpec(
+            num_scalar_prefetch=1,
+            grid=(pairs,),
+            in_specs=[
+                pl.BlockSpec((rows, span), lambda p, _: (0, p)),
+                pl.BlockSpec((length, 128), lambda p, _: (0, p)),
+                pl.BlockSpec((length, 128), lambda p, _: (0, p + pairs)),
+                pl.BlockSpec((rows, 1), lambda p, _: (0, 0)),
+            ],
+            out_specs=pl.BlockSpec((rows, span), lambda p, _: (0, p)),
+            scratch_shapes=[
+                pltpu.VMEM((PAIR * rows, 128), jnp.bfloat16),
+                pltpu.VMEM((PAIR * rows, 128), jnp.float32),
+                pltpu.VMEM((PAIR * rows, 128), jnp.float32),
+            ],
+        ),
+        compiler_params=pltpu.CompilerParams(vmem_limit_bytes=60 << 20),
+        name="attention",
+    )(bounds.astype(jnp.int32), queries, keys_values, keys_values, prompt_start[:, None])
 
 
 class Scatter:
@@ -313,15 +518,16 @@
 BLOCKS = 4
 
 
-def expert_kernel(ranks, gains, rows_in, own, other, out, weights, picked, made, sems):
+def expert_kernel(tables, rows_in, own, other, out, weights, picked, made, sems):
     step = pl.program_id(0)
+    core = lax.rem(lax.axis_index("exp"), 2)
 
     def loads():
         for e, source in enumerate((own, other)):
             for r in range(4):
                 yield pltpu.make_async_copy(
                     source.at[r],
-                    weights.at[e, :, :, pl.ds(r * 128, 128)],
+                    weights.at[core if e == 0 else 1 - core, :, :, pl.ds(r * 128, 128)],
                     sems.at[e * 4 + r],
                 )
 
@@ -334,7 +540,7 @@
     slot = lax.broadcasted_iota(jnp.int32, (SLOTS, tokens), 0).astype(jnp.float32)
 
     def hits(j):
-        return jnp.concatenate([ranks[j, e : e + 1, :] == slot for e in (0, 1)], axis=0)
+        return jnp.concatenate([tables[j, 2 + e : 3 + e, :] == slot for e in (0, 1)], axis=0)
 
     for j in range(BLOCKS):
         choose = jnp.where(hits(j), 1.0, 0.0).astype(jnp.bfloat16)
@@ -358,7 +564,7 @@
         )
         for j in range(BLOCKS):
             gain = jnp.sum(
-                jnp.where(ranks[j, e : e + 1, :] == slot, gains[j, e : e + 1, :], 0.0),
+                jnp.where(tables[j, 2 + e : 3 + e, :] == slot, tables[j, e : e + 1, :], 0.0),
                 axis=1,
                 keepdims=True,
             )
@@ -373,15 +579,14 @@
         ).astype(jnp.bfloat16)
 
 
-def run_experts(ranks, gains, rows_in, own, other):
+def run_experts(tables, rows_in, own, other):
     chips, tokens, width = rows_in.shape
     return pl.pallas_call(
         expert_kernel,
         grid=(chips // BLOCKS,),
         out_shape=jax.ShapeDtypeStruct(rows_in.shape, jnp.bfloat16),
         in_specs=[
-            pl.BlockSpec((BLOCKS, 2, tokens), lambda i: (i, 0, 0)),
-            pl.BlockSpec((BLOCKS, 2, tokens), lambda i: (i, 0, 0)),
+            pl.BlockSpec((BLOCKS, 8, tokens), lambda i: (i, 0, 0)),
             pl.BlockSpec((BLOCKS, tokens, width), lambda i: (i, 0, 0)),
             pl.BlockSpec(memory_space=pl.ANY),
             pl.BlockSpec(memory_space=pl.ANY),
@@ -395,7 +600,7 @@
         ],
         compiler_params=pltpu.CompilerParams(vmem_limit_bytes=60 << 20),
         name="experts",
-    )(ranks, gains, rows_in, own, other)
+    )(tables, rows_in, own, other)
 
 
 def slot_tables(routes, route_weights):
@@ -405,7 +610,9 @@
     named = jnp.any(hit, axis=2)
     earlier = jnp.triu(jnp.ones((tokens, tokens), jnp.bfloat16), 1)
     ranks = jnp.dot(named.astype(jnp.bfloat16), earlier, preferred_element_type=jnp.float32)
-    return jnp.where(named, ranks, -1.0), gains
+    ranks = jnp.where(named, ranks, -1.0)
+    pairs = [t.reshape(CHIPS, 2, tokens) for t in (gains, ranks)]
+    return jnp.concatenate(pairs + [jnp.zeros((CHIPS, 4, tokens), jnp.float32)], axis=1)
 
 
 def shards(
@@ -423,21 +630,8 @@
 ):
     total_row_count = hidden.shape[0]
     lane_index = lax.axis_index("exp")
-    heads_per_group = QUERY_HEADS // KEY_VALUE_HEADS
-
-    tables = jnp.stack(slot_tables(routes, route_weights))
-    tables = lax.all_gather(tables, "exp", axis=0)
     weight_piece = lax.all_gather(expert_weights[0], "req", axis=0)
     weight_other = lax.ppermute(weight_piece, "exp", [(i, i ^ 1) for i in range(EXPERTS)])
-    tables = lax.dynamic_index_in_dim(
-        tables.reshape(CHIPS, 2, 2, CHIPS, 2, total_row_count),
-        lax.rem(lane_index, 2),
-        1,
-        keepdims=False,
-    )
-    tables = lax.dynamic_index_in_dim(tables, lax.div(lane_index, 2), 2, keepdims=False)
-    tables = jnp.where(lax.rem(lane_index, 2) == 0, tables, tables[:, :, ::-1])
-
     positions = lane_index * total_row_count + jnp.arange(total_row_count, dtype=jnp.int32)
     stream_offsets = positions - prompt_start
     inputs = hidden.astype(jnp.float32)
@@ -448,7 +642,7 @@
     query_rows_all = (
         rotary_embedding(query_rows_all, stream_offsets)
         .astype(jnp.bfloat16)
-        .reshape(total_row_count, KEY_VALUE_HEADS, heads_per_group, HEAD_SIZE)
+        .reshape(total_row_count, QUERY_HEADS * HEAD_SIZE)
     )
     shard_keys = jnp.dot(normalized_input, key_matrix, preferred_element_type=jnp.float32).reshape(
         total_row_count, KEY_VALUE_HEADS, HEAD_SIZE
@@ -461,37 +655,20 @@
     values_local = jnp.dot(
         normalized_input, value_matrix, preferred_element_type=jnp.float32
     ).astype(jnp.bfloat16)
-    stacked = jnp.stack([shard_keys, values_local])
-    key_value_slice = lax.all_gather(stacked, "exp", axis=1, tiled=True)
-    feature_width = key_value_slice.shape[1]
-    key_tile = key_value_slice[0].reshape(feature_width, KEY_VALUE_HEADS, HEAD_SIZE)
-    value_tile = key_value_slice[1].reshape(feature_width, KEY_VALUE_HEADS, HEAD_SIZE)
-    key_pos = jnp.arange(feature_width, dtype=jnp.int32)
-    scores = jnp.einsum(
-        "tgrd,sgd->tgrs", query_rows_all, key_tile, preferred_element_type=jnp.float32
-    ) * HEAD_SIZE ** (-0.5)
-    valid = (key_pos[None, :] >= prompt_start[:, None]) & (key_pos[None, :] <= positions[:, None])
-    valid = valid[:, None, None, :]
-    masked = jnp.where(valid, scores, jnp.float32(-1e30))
-    new_max = jnp.max(masked, axis=-1)
-    probs = jnp.where(valid, jnp.exp(masked - new_max[..., None]), jnp.float32(0.0))
-    totals = jnp.sum(probs, axis=-1)
-    attention_mixed = jnp.einsum(
-        "tgrs,sgd->tgrd", probs.astype(jnp.bfloat16), value_tile, preferred_element_type=jnp.float32
+    keys_values, tables = gather_keys_values(
+        jnp.concatenate([shard_keys, values_local], axis=1), slot_tables(routes, route_weights), 0
     )
-    attention = (
-        (attention_mixed / totals[..., None])
-        .reshape(total_row_count, QUERY_HEADS * HEAD_SIZE)
-        .astype(jnp.bfloat16)
+    attention = attend(
+        query_rows_all, keys_values, prompt_start, lane_index * total_row_count
     )
     residual = inputs + jnp.dot(attention, output_weight, preferred_element_type=jnp.float32)
     moe_in = rms_norm(residual, ffn_gain).astype(jnp.bfloat16)
 
     rows_in = gather_rows(moe_in, 1)
-    parts = run_experts(tables[:, 0], tables[:, 1], rows_in, weight_piece, weight_other)
+    parts = run_experts(tables, rows_in, weight_piece, weight_other)
     moe_sum = scatter_sums(parts, 2)
     layer_out = (residual + moe_sum).astype(jnp.bfloat16)
-    return (layer_out, stacked[0], stacked[1])
+    return (layer_out, shard_keys, values_local)
 
 
 def solution(mesh):

time: 337 us -> 276 us (0.82)
  waiting for transfers between devices: 141 us -> 57.8 us
  Pallas kernels: 98.6 us -> 177 us
  matrix products: 51.2 us -> 11.4 us
  local copies, waits for them, and re-layouts: 21 us -> 3.95 us
    all_gather x2 -> x0, waiting for transfers between devices: 88.7 us -> none  [the longest x1 56 us: shards(): key_value_slice = lax.all_gather(stacked, 'exp', axis=1, tiled=True)]
    pallas_call x0 -> x2, Pallas kernels: none -> 48.6 us  [the longest x1 39.2 us: gather_keys_values(): pl.pallas_call(kernel, out_shape=(jax.ShapeDtypeStruct((2 * CHIPS, rows,...]
    pallas_call x1, Pallas kernels: 37.9 us -> 69.9 us  [gather_rows(): pl.pallas_call(kernel, out_shape=jax.ShapeDtypeStruct((CHIPS, rows, width...]
    sub x1 -> x0, matrix products: 26.6 us -> none  [shards(): masked - new_max[..., None]]
    slice x3 -> x1, local copies, waits for them, and re-layouts: 18.6 us -> 1.38 us  [attend(): prompt_start[0] // KEYS]
    dot_general x1 -> x0, matrix products: 13.2 us -> none  [shards(): jnp.einsum('tgrs,sgd->tgrd', probs.astype(jnp.bfloat16), value_tile, pref...]
    all_gather x1, waiting for transfers between devices: 51.7 us -> 57.1 us  [shards(): weight_piece = lax.all_gather(expert_weights[0], 'req', axis=0)]
  transfers between devices with their start and end apart: 4 -> 2, of which waited for: 3 -> 1; matrix products, arithmetic and copies ran while one was open for 23% -> 8% of each run, Pallas kernels for 11% -> 43%
where the time goes in v2:
time: 276 us; the launch traced here: 275 us
  Pallas kernels  177 us (64%)
  waiting for transfers between devices  57.8 us (21%)
  between operations  16.9 us (6%)
  matrix products  11.4 us (4%)
  other arithmetic  7.84 us (3%)
  local copies, waits for them, and re-layouts  3.95 us (1%)
    pallas_call x1, Pallas kernels, gather_rows(): pl.pallas_call(kernel, out_shape=jax.ShapeDtypeStruct((CHIPS, rows, width...  69.9 us
    all_gather x1, waiting for transfers between devices, shards(): weight_piece = lax.all_gather(expert_weights[0], 'req', axis=0)  57.1 us
    pallas_call x1, Pallas kernels, gather_keys_values(): pl.pallas_call(kernel, out_shape=(jax.ShapeDtypeStruct((2 * CHIPS, rows,...  39.2 us
    pallas_call x1, Pallas kernels, scatter_sums(): pl.pallas_call(kernel, out_shape=jax.ShapeDtypeStruct((rows, width), jnp....  37.1 us
    pallas_call x1, Pallas kernels, run_experts(): pl.pallas_call(expert_kernel, grid=(chips // BLOCKS,), out_shape=jax.Shap...  21.3 us
    pallas_call x1, Pallas kernels, attend(): pl.pallas_call(attention_kernel, out_shape=jax.ShapeDtypeStruct((rows, wi...  9.42 us
  transfers between devices with their start and end apart: 2, of which 1 were waited for; matrix products, arithmetic and copies ran while one was open for 8% of the time, Pallas kernels for 43%

profile of v2, /device:TPU:0, one launch (start us, length us, event | category | flops | bytes accessed | tf_op | source)
XLA Modules:
  0.0 274.8 jit_solution(5320803959835982280)
XLA Ops:
  7.2 0.7 all-gather.2.cloned.1.call-update
  7.9 57.1 %all-gather.2.cloned.1.call-done.own = bf16[4,3,1536,128]{3,2,1,0:T(8,128)(2,1)} async-done(((bf16[1,3,1536,128]{3,2,1,0:T(8,128)(2,1)}), bf16[4,3,1536,128]{3,2,1,0:T(8,128)(2,1)}) %all-gather.2.cloned.1.call-update) | async-done | bytes 4718608 | tf_op jit(solution)/shard_map/all_gather | solution.py:633
  65.0 1.4 fusion.15
  69.0 1.4 copy.37.starts
  70.4 1.2 fusion
  71.6 0.7 subtract_convert_fusion.2
  72.3 0.1 multiply_cosine_fusion
  72.4 1.8 fusion.11
  74.3 0.1 copy.35
  74.4 4.4 %fusion.13 = f32[128,1536]{0,1:T(8,128)S(1)} fusion(bf16[1536,1536]{1,0:T(8,128)(2,1)} %param.13, bf16[128,1536]{1,0:T(8,128)(2,1)S(1)} %copy-done.1, f32[1536]{0:T(1024)S(1)} %copy-done.4, f32[128]{0:T(128)S(1)} %add_rsqrt_fusion.1), kind=kOutput, calls=%fused_computation.36 | convolution fusion | flops 604766208 | bytes 5904896 | tf_op jit(solution)/shard_map/dot_general | solution.py:639
  79.0 0.9 copy.36.queries
  80.1 1.8 convolution_convert_fusion
  82.0 0.8 pad_maximum_fusion.1.own
  82.7 0.1 convolution_select_fusion
  82.8 0.7 maximum_maximum_fusion.given
  83.6 39.2 %gather_keys_values.1 = (bf16[32,128,1024]{2,1,0:T(8,128)(2,1)}, f32[16,8,128]{2,1,0:T(8,128)}) custom-call(bf16[128,1024]{1,0:T(8,128)(2,1)} %pad_maximum_fusion.1.own, f32[16,8,128]{2,1,0:T(8,128)} %maximum_maximum_fusion.given), custom_call_target="tpu_custom_call" | custom-call | tf_op jit(solution)/shard_map/gather_keys_values/pallas_call | solution.py:256
  122.7 1.2 pad_add_fusion.bounds
  124.0 9.4 %attention.1 = bf16[128,1536]{1,0:T(8,128)(2,1)} custom-call(s32[4]{0:T(128)} %pad_add_fusion.bounds, bf16[128,1536]{1,0:T(8,128)(2,1)} %copy.36.queries, bf16[4096,1024]{1,0:T(8,128)(2,1)} %bitcast.18, bf16[4096,1024]{1,0:T(8,128)(2,1)} %bitcast.19, s32[128,1]{1,0:T(8,128)} %copy.37.starts), custom_call_target="tpu_custom_call" | custom-call | tf_op jit(solution)/shard_map/attention/pallas_call | solution.py:364
  133.4 3.3 %multiply_reduce_fusion = (f32[128]{0:T(128)S(1)}, f32[128,1536]{1,0:T(8,128)S(1)}) fusion(bf16[128,1536]{1,0:T(8,128)(2,1)} %attention.1, bf16[1536,1536]{1,0:T(8,128)(2,1)} %param.16, bf16[128,1536]{1,0:T(8,128)(2,1)S(1)} %copy-done.1), kind=kOutput, calls=%fused_computation.10 | convolution fusion | flops 604766080 | bytes 6291968 | tf_op jit(solution)/shard_map/dot_general | solution.py:664
  136.8 0.9 multiply_convert_fusion.own
  137.7 69.9 %gather_rows.1.rows_in = bf16[16,128,1536]{2,1,0:T(8,128)(2,1)} custom-call(bf16[128,1536]{1,0:T(8,128)(2,1)} %multiply_convert_fusion.own), custom_call_target="tpu_custom_call" | custom-call | tf_op jit(solution)/shard_map/gather_rows/pallas_call | solution.py:178
  207.6 21.3 %experts.1.given = bf16[16,128,1536]{2,1,0:T(8,128)(2,1)} custom-call(f32[16,8,128]{2,1,0:T(8,128)} %get-tuple-element.6.tables, bf16[16,128,1536]{2,1,0:T(8,128)(2,1)} %gather_rows.1.rows_in, bf16[4,3,1536,128]{3,2,1,0:T(8,128)(2,1)} %all-gather.2.cloned.1.call-done.own, bf16[4,3,1536,128]{3,2,1,0:T(8,128)(2,1)} %collective-permute-done.other), custom_call_target="tpu_custom_call" | custom-call | tf_op jit(solution)/shard_map/experts/pallas_call | solution.py:584
  228.9 37.1 %scatter_sums.1 = f32[128,1536]{1,0:T(8,128)} custom-call(bf16[16,128,1536]{2,1,0:T(8,128)(2,1)} %experts.1.given), custom_call_target="tpu_custom_call" | custom-call | tf_op jit(solution)/shard_map/scatter_sums/pallas_call | solution.py:499
  266.0 2.0 add_convert_fusion
  (30 shorter events, 0.5 us)
Async XLA Ops:
  7.2 65.3 %copy-start = (bf16[1536,512]{1,0:T(8,128)(2,1)S(1)}, bf16[1536,512]{1,0:T(8,128)(2,1)}, u32[]{:S(2)}) copy-start(bf16[1536,512]{1,0:T(8,128)(2,1)} %param.14) | copy-start | bytes 4718596
  7.2 67.2 %copy-start.1 = (bf16[128,1536]{1,0:T(8,128)(2,1)S(1)}, bf16[128,1536]{1,0:T(8,128)(2,1)}, u32[]{:S(2)}) copy-start(bf16[128,1536]{1,0:T(8,128)(2,1)} %param.11) | copy-start | bytes 1179652
  7.2 67.2 %copy-start.4 = (f32[1536]{0:T(1024)S(1)}, f32[1536]{0:T(1024)}, u32[]{:S(2)}) copy-start(f32[1536]{0:T(1024)} %param.12) | copy-start | bytes 18436
  7.2 57.8 %all-gather.2.cloned.1.call-start = ((), (), s32[]{:S(2)}) async-start(), calls=%async_computation | async-start | bytes 5898240 | tf_op jit(solution)/shard_map/all_gather | solution.py:633
  65.0 142.6 %collective-permute-start = (bf16[4,3,1536,128]{3,2,1,0:T(8,128)(2,1)}, bf16[4,3,1536,128]{3,2,1,0:T(8,128)(2,1)}, u32[]{:S(2)}, u32[]{:S(2)}) collective-permute-start(bf16[4,3,1536,128]{3,2,1,0:T(8,128)(2,1)} %all-gather.2.cloned.1.call-done.own), channel_id=1, source_target_pairs={{0,1},{1,0},{2,3},{3,2},{4,5},{5,4},{6,7},{7,6},{8,9},{9,8},{10,11... | collective-permute-start | bytes 14155784 | tf_op jit(solution)/shard_map/ppermute | solution.py:634
  74.2 5.7 %copy-start.5 = (s32[128,8]{0,1:T(8,128)S(1)}, s32[128,8]{0,1:T(8,128)}, u32[]{:S(2)}) copy-start(s32[128,8]{0,1:T(8,128)} %param.19) | copy-start | bytes 12292
  74.3 5.8 %copy-start.7 = (f32[128,8]{0,1:T(8,128)S(1)}, f32[128,8]{0,1:T(8,128)}, u32[]{:S(2)}) copy-start(f32[128,8]{0,1:T(8,128)} %param.20) | copy-start | bytes 12292
  74.4 7.5 %copy-start.2 = (bf16[128,512]{1,0:T(8,128)(2,1)}, bf16[128,512]{1,0:T(8,128)(2,1)S(1)}, u32[]{:S(2)}) copy-start(bf16[128,512]{1,0:T(8,128)(2,1)S(1)} %copy.35) | copy-start | bytes 393220
  81.9 51.5 %copy-start.3 = (bf16[128,512]{1,0:T(8,128)(2,1)}, bf16[128,512]{1,0:T(8,128)(2,1)S(1)}, u32[]{:S(2)}) copy-start(bf16[128,512]{1,0:T(8,128)(2,1)S(1)} %convolution_convert_fusion) | copy-start | bytes 393220
  133.4 3.4 %copy-start.6 = (f32[1536]{0:T(1024)S(1)}, f32[1536]{0:T(1024)}, u32[]{:S(2)}) copy-start(f32[1536]{0:T(1024)} %param.18) | copy-start | bytes 18436
Sparse Core Ops, SparseCore 0:
  9.7 55.3 all-gather.1

commit v3 on v1

--- a/solution.py
+++ b/solution.py
@@ -55,18 +55,33 @@
     def partner(self):
         return {"exp": self.chip(0, 0) * 2 + 1 - self.core}
 
-
-def greet(plane, with_partner=False):
+    def mirror(self, same_core):
+        core = self.core if same_core else 1 - self.core
+        return {"exp": (CHIPS - 1 - self.chip(0, 0)) * 2 + core}
+
+
+NEXT = ((0, 1), (0, -1), (1, 0), (-1, 0))
+OTHERS = tuple((dy, dx) for dy in range(SIDE) for dx in range(SIDE) if dy or dx)
+
+
+def greet(plane, places=NEXT, devices=()):
     barrier = pltpu.get_barrier_semaphore()
-    for dy, dx in ((0, 1), (0, -1), (1, 0), (-1, 0)):
+    for device in [plane.device(dy, dx) for dy, dx in places] + list(devices):
         pl.semaphore_signal(
-            barrier, inc=1, device_id=plane.device(dy, dx), device_id_type=pl.DeviceIdType.MESH
-        )
-    if with_partner:
-        pl.semaphore_signal(
-            barrier, inc=1, device_id=plane.partner(), device_id_type=pl.DeviceIdType.MESH
-        )
-    pl.semaphore_wait(barrier, 5 if with_partner else 4)
+            barrier, inc=1, device_id=device, device_id_type=pl.DeviceIdType.MESH
+        )
+    pl.semaphore_wait(barrier, len(places) + len(devices))
+
+
+def remote(src, dst, send, recv, device):
+    return pltpu.make_async_remote_copy(
+        src_ref=src,
+        dst_ref=dst,
+        send_sem=send,
+        recv_sem=recv,
+        device_id=device,
+        device_id_type=pl.DeviceIdType.MESH,
+    )
 
 
 def turn(h, a, b):
@@ -152,32 +167,363 @@
                 self.make(h, k, False).wait_send()
 
 
-def gather_rows(block, collective_id):
+def gather_rows(block, weights, collective_id):
     rows, width = block.shape
 
-    def kernel(own, slots, send, recv, mine_sem):
+    def kernel(own, given, slots, other, send, recv, sems):
         plane = Plane()
-        greet(plane)
+        greet(plane, NEXT, [plane.partner()])
+        swap = remote(given, other, sems.at[1], sems.at[2], plane.partner())
         gather = Gather(plane, own, slots, send, recv, rows, lambda chip: chip)
-        mine = pltpu.make_async_copy(own, slots.at[plane.chip(0, 0)], mine_sem)
+        mine = pltpu.make_async_copy(own, slots.at[plane.chip(0, 0)], sems.at[0])
         mine.start()
+        swap.start()
         gather.run()
         gather.finish()
         mine.wait()
+        swap.wait()
 
     return pl.pallas_call(
         kernel,
-        out_shape=jax.ShapeDtypeStruct((CHIPS, rows, width), block.dtype),
-        in_specs=[pl.BlockSpec(memory_space=pltpu.VMEM)],
-        out_specs=pl.BlockSpec(memory_space=pl.ANY),
+        out_shape=(
+            jax.ShapeDtypeStruct((CHIPS, rows, width), block.dtype),
+            jax.ShapeDtypeStruct(weights.shape, weights.dtype),
+        ),
+        in_specs=[
+            pl.BlockSpec(memory_space=pltpu.VMEM),
+            pl.BlockSpec(memory_space=pl.ANY),
+        ],
+        out_specs=(pl.BlockSpec(memory_space=pl.ANY), pl.BlockSpec(memory_space=pl.ANY)),
         scratch_shapes=[
             pltpu.SemaphoreType.DMA((2 * Gather.COPIES,)),
             pltpu.SemaphoreType.DMA((2 * Gather.COPIES,)),
-            pltpu.SemaphoreType.DMA,
+            pltpu.SemaphoreType.DMA((3,)),
         ],
         compiler_params=pltpu.CompilerParams(collective_id=collective_id, has_side_effects=True),
         name="gather_rows",
-    )(block)
+    )(block, weights)
+
+
+KEYS = 512
+PAIR = 6
+PAIR_WIDTH = PAIR * HEAD_SIZE
+LOW = -1e30
+SCALE = HEAD_SIZE**-0.5 * 1.4426950408889634
+ACROSS = (0, -1, 1, 2)
+
+
+def attention_kernel(
+    queries, pairs, starts, given,
+    out, held,
+    near, store, asked, begin, packed, peak, total, bias, done,
+    give, take, x_send, x_recv, y_send, y_recv, q_send, q_recv, o_send, o_recv, sems,
+):
+    plane = Plane()
+    core, odd = plane.core, lax.rem(plane.x, 2)
+    here = plane.chip(0, 0)
+    rows = queries.shape[0]
+    friends = [plane.partner(), plane.mirror(True), plane.mirror(False)]
+    greet(plane, OTHERS, [friends[0], friends[2]])
+
+    mine = 2 * core + odd
+    theirs = [2 * (1 - core) + odd, 2 * core + 1 - odd, 2 * (1 - core) + 1 - odd]
+    slots = [core, 2 + core, 2 + core]
+    from_slots = [1 - core, 2 + core, 2 + 1 - core]
+
+    def lanes(at, size):
+        return pl.ds(pl.multiple_of(at * size, size), size)
+
+    swap = remote(
+        pairs.at[:, lanes(1 - core, 512)], near, sems.at[0], sems.at[1], friends[0]
+    )
+
+    def source(h, parity):
+        if h == 0:
+            return pairs.at[:, lanes(2 * core + parity, 256)]
+        return near.at[:, lanes(parity, 256)]
+
+    def slot(h, dy, dx, part=None):
+        low = (core if h == 0 else 1 - core) * rows
+        size = rows
+        if part is not None:
+            size = rows // 2
+            low = low + part * size
+        return store.at[plane.chip(dy, dx), pl.ds(pl.multiple_of(low, size), size)]
+
+    def keep(h):
+        return pltpu.make_async_copy(source(h, odd), slot(h, 0, 0), sems.at[2 + h])
+
+    def across(h, n, incoming=False):
+        dx = (1, -1, 2)[n]
+        return remote(
+            source(h, odd if n == 2 else 1 - odd),
+            slot(h, 0, -dx if incoming else 0),
+            x_send.at[3 * h + n],
+            x_recv.at[3 * h + n],
+            plane.device(0, dx),
+        )
+
+    def along(h, i, n, incoming=False):
+        dx = ACROSS[i]
+        at, part, dy = ((0, None, 1), (0, None, -1), (-1, 0, 1), (1, 1, -1))[n]
+        place = slot(h, at - dy if incoming else at, dx, part)
+        src = source(h, odd) if (i == 0 and n < 2) else place
+        if i == 0 and n < 2 and not incoming:
+            place = slot(h, 0, 0)
+        k = (h * 4 + i) * 4 + n
+        return remote(src, place, y_send.at[k], y_recv.at[k], plane.device(dy, 0))
+
+    def ask(n, incoming=False):
+        at = from_slots[n] if incoming else slots[n]
+        return remote(
+            queries.at[:, lanes(theirs[n], PAIR_WIDTH)],
+            asked.at[at],
+            q_send.at[n],
+            q_recv.at[n],
+            friends[n],
+        )
+
+    def tell(n, incoming=False):
+        at = from_slots[n] if incoming else slots[n]
+        return remote(starts, begin.at[at], q_send.at[3 + n], q_recv.at[3 + n], friends[n])
+
+    def table(n, incoming=False):
+        dy, dx = OTHERS[n]
+        return remote(
+            given.at[plane.chip(dy, dx)],
+            held.at[plane.chip(-dy, -dx) if incoming else here],
+            give.at[n],
+            take.at[n],
+            plane.device(dy, dx),
+        )
+
+    own_asked = pltpu.make_async_copy(
+        queries.at[:, lanes(mine, PAIR_WIDTH)], asked.at[core], sems.at[4]
+    )
+    own_begin = pltpu.make_async_copy(starts, begin.at[core], sems.at[5])
+    own_table = pltpu.make_async_copy(given.at[here], held.at[here], sems.at[6])
+
+    swap.start()
+    for h in (0, 1):
+        if h == 1:
+            ask(0).start()
+            tell(0).start()
+            own_asked.start()
+            own_begin.start()
+            own_table.start()
+            swap.wait_recv()
+        keep(h).start()
+        for n in range(3):
+            across(h, n).start()
+        along(h, 0, 0).start()
+        along(h, 0, 1).start()
+    for n in (1, 2):
+        ask(n).start()
+        tell(n).start()
+    for n in range(3):
+        i = (1, 2, 3)[n]
+        for h in (0, 1):
+            across(h, n, True).wait_recv()
+            along(h, i, 0).start()
+            along(h, i, 1).start()
+    for n in range(len(OTHERS)):
+        table(n).start()
+
+    own_asked.wait()
+    own_begin.wait()
+    for n in range(3):
+        ask(n, True).wait_recv()
+        tell(n, True).wait_recv()
+    for h in (0, 1):
+        keep(h).wait()
+
+    lane = lax.broadcasted_iota(jnp.int32, (rows, 128), 1)
+    low_half = lane < HEAD_SIZE
+    for which in (0, 1):
+        for side in (0, 1):
+            for n in range(PAIR):
+                tile = asked[2 * which + side, :, (n // 2) * 128 : (n // 2 + 1) * 128].astype(
+                    jnp.float32
+                )
+                group = n // 3
+                if n % 2 != group:
+                    tile = pltpu.roll(tile, HEAD_SIZE, axis=1)
+                own_half = low_half if group == 0 else jnp.logical_not(low_half)
+                at = (n * 2 + side) * rows
+                packed[which, at : at + rows, :] = jnp.where(own_half, tile, 0.0).astype(
+                    jnp.bfloat16
+                )
+    peak[...] = jnp.full_like(peak, LOW)
+    total[...] = jnp.zeros_like(total)
+    half = PAIR * rows
+
+    def visit(which, chip):
+        stream_chip = jnp.where(which == 0, here, CHIPS - 1 - here)
+        at = chip * (2 * rows)
+        for side in (0, 1):
+            first = jnp.broadcast_to(begin[2 * which + side, 0:1, :], (rows, rows)).T
+            first = jnp.concatenate([first] * (KEYS // rows), axis=1).astype(jnp.int32)
+            key_pos = at + lax.broadcasted_iota(jnp.int32, (rows, KEYS), 1)
+            own_pos = (2 * stream_chip + side) * rows + lax.broadcasted_iota(
+                jnp.int32, (rows, KEYS), 0
+            )
+            bias[side * rows : (side + 1) * rows, :] = jnp.where(
+                (key_pos >= first) & (key_pos <= own_pos), 0.0, LOW
+            )
+        tile = store[pl.ds(chip, 2)].reshape(KEYS, 256)
+        key, value = tile[:, :128], tile[:, 128:]
+        key_lane = lax.broadcasted_iota(jnp.int32, (KEYS, 128), 1)
+        for group in (0, 1):
+            span = pl.ds(group * half, half)
+            scores = lax.dot_general(
+                packed[which, span, :],
+                key,
+                (((1,), (1,)), ((), ())),
+                preferred_element_type=jnp.float32,
+            )
+            scores = (scores.reshape(PAIR // 2, 2 * rows, KEYS) + bias[...][None]).reshape(
+                half, KEYS
+            )
+            before = peak[which, span, :]
+            now = jnp.maximum(before, jnp.max(scores, axis=1, keepdims=True))
+            peak[which, span, :] = now
+            fade = jnp.exp2((before - now) * SCALE)
+            wide = jnp.concatenate([now] * (KEYS // 128), axis=1)
+            probs = jnp.exp2((scores - wide) * SCALE).astype(jnp.bfloat16)
+            own_half = (key_lane < HEAD_SIZE) == (group == 0)
+            beside = jnp.where(own_half, value, jnp.ones_like(value))
+            total[which, span, :] = total[which, span, :] * fade + jnp.dot(
+                probs, beside, preferred_element_type=jnp.float32
+            )
+
+    def phase(step, carry):
+        @pl.when(step == 1)
+        def _():
+            for i in range(4):
+                for n in (0, 1):
+                    for h in (0, 1):
+                        along(h, i, n, True).wait_recv()
+                        along(h, i, n + 2).start()
+
+        @pl.when(step == 3)
+        def _():
+            for i in range(4):
+                for n in (2, 3):
+                    for h in (0, 1):
+                        along(h, i, n, True).wait_recv()
+
+        dy = jnp.where(step == 0, 0, jnp.where(step == 1, SIDE - 1, step - 1))
+        dy = jnp.where(step == 3, 2, dy)
+        row = lax.rem(plane.y + dy, SIDE) * SIDE
+
+        def one(t, carry):
+            which = lax.div(t, 2)
+            chip = row + 2 * lax.rem(t, 2)
+            limit = jnp.where(which == 0, here, CHIPS - 1 - here)
+
+            @pl.when(chip <= limit)
+            def _():
+                visit(which, chip)
+
+            return carry
+
+        return lax.fori_loop(0, 4, one, carry)
+
+    lax.fori_loop(0, 4, phase, 0)
+
+    def answer(which, side):
+        def head(n):
+            at = (n * 2 + side) * rows
+            sums = total[which, at : at + rows, :]
+            result = sums / pltpu.roll(sums, HEAD_SIZE, axis=1)
+            if n % 2 != n // 3:
+                result = pltpu.roll(result, HEAD_SIZE, axis=1)
+            return result
+
+        return [
+            jnp.where(low_half, head(2 * i), head(2 * i + 1)).astype(out.dtype)
+            for i in range(PAIR // 2)
+        ]
+
+    for which in (1, 0):
+        for side in (0, 1):
+            for i, piece in enumerate(answer(which, side)):
+                done[2 * which + side, :, i * 128 : (i + 1) * 128] = piece
+
+    def reply(n, incoming=False):
+        return remote(
+            done.at[from_slots[n]],
+            out.at[:, lanes(theirs[n] if incoming else mine, PAIR_WIDTH)],
+            o_send.at[n],
+            o_recv.at[n],
+            friends[n],
+        )
+
+    for n in (1, 2, 0):
+        reply(n).start()
+    own_reply = pltpu.make_async_copy(
+        done.at[core], out.at[:, lanes(mine, PAIR_WIDTH)], sems.at[7]
+    )
+    own_reply.start()
+
+    swap.wait_send()
+    own_table.wait()
+    for h in (0, 1):
+        for n in range(3):
+            across(h, n).wait_send()
+        for i in range(4):
+            for n in range(4):
+                along(h, i, n).wait_send()
+    for n in range(3):
+        ask(n).wait_send()
+        tell(n).wait_send()
+    for n in range(len(OTHERS)):
+        table(n, True).wait_recv()
+        table(n).wait_send()
+    own_reply.wait()
+    for n in range(3):
+        reply(n, True).wait_recv()
+        reply(n).wait_send()
+
+
+def attend(queries, pairs, starts, tables, collective_id):
+    rows, width = queries.shape
+    dma = pltpu.SemaphoreType.DMA
+    return pl.pallas_call(
+        attention_kernel,
+        out_shape=(
+            jax.ShapeDtypeStruct((rows, width), jnp.bfloat16),
+            jax.ShapeDtypeStruct(tables.shape, tables.dtype),
+        ),
+        in_specs=[pl.BlockSpec(memory_space=pltpu.VMEM)] * 4,
+        out_specs=(pl.BlockSpec(memory_space=pltpu.VMEM),) * 2,
+        scratch_shapes=[
+            pltpu.VMEM((rows, 512), jnp.bfloat16),
+            pltpu.VMEM((CHIPS, 2 * rows, 256), jnp.bfloat16),
+            pltpu.VMEM((4, rows, PAIR_WIDTH), jnp.bfloat16),
+            pltpu.VMEM((4, 8, rows), jnp.float32),
+            pltpu.VMEM((2, 2 * PAIR * rows, 128), jnp.bfloat16),
+            pltpu.VMEM((2, 2 * PAIR * rows, 128), jnp.float32),
+            pltpu.VMEM((2, 2 * PAIR * rows, 128), jnp.float32),
+            pltpu.VMEM((2 * rows, KEYS), jnp.float32),
+            pltpu.VMEM((4, rows, PAIR_WIDTH), jnp.bfloat16),
+            dma((len(OTHERS),)),
+            dma((len(OTHERS),)),
+            dma((6,)),
+            dma((6,)),
+            dma((32,)),
+            dma((32,)),
+            dma((6,)),
+            dma((6,)),
+            dma((3,)),
+            dma((3,)),
+            dma((8,)),
+        ],
+        compiler_params=pltpu.CompilerParams(
+            collective_id=collective_id, has_side_effects=True, vmem_limit_bytes=60 << 20
+        ),
+        name="attention",
+    )(queries, pairs, starts, tables)
 
 
 class Scatter:
@@ -313,15 +659,16 @@
 BLOCKS = 4
 
 
-def expert_kernel(ranks, gains, rows_in, own, other, out, weights, picked, made, sems):
+def expert_kernel(tables, rows_in, own, other, out, weights, picked, made, sems):
     step = pl.program_id(0)
+    core = lax.rem(lax.axis_index("exp"), 2)
 
     def loads():
         for e, source in enumerate((own, other)):
             for r in range(4):
                 yield pltpu.make_async_copy(
                     source.at[r],
-                    weights.at[e, :, :, pl.ds(r * 128, 128)],
+                    weights.at[core if e == 0 else 1 - core, :, :, pl.ds(r * 128, 128)],
                     sems.at[e * 4 + r],
                 )
 
@@ -334,7 +681,7 @@
     slot = lax.broadcasted_iota(jnp.int32, (SLOTS, tokens), 0).astype(jnp.float32)
 
     def hits(j):
-        return jnp.concatenate([ranks[j, e : e + 1, :] == slot for e in (0, 1)], axis=0)
+        return jnp.concatenate([tables[j, 2 + e : 3 + e, :] == slot for e in (0, 1)], axis=0)
 
     for j in range(BLOCKS):
         choose = jnp.where(hits(j), 1.0, 0.0).astype(jnp.bfloat16)
@@ -358,7 +705,7 @@
         )
         for j in range(BLOCKS):
             gain = jnp.sum(
-                jnp.where(ranks[j, e : e + 1, :] == slot, gains[j, e : e + 1, :], 0.0),
+                jnp.where(tables[j, 2 + e : 3 + e, :] == slot, tables[j, e : e + 1, :], 0.0),
                 axis=1,
                 keepdims=True,
             )
@@ -373,15 +720,14 @@
         ).astype(jnp.bfloat16)
 
 
-def run_experts(ranks, gains, rows_in, own, other):
+def run_experts(tables, rows_in, own, other):
     chips, tokens, width = rows_in.shape
     return pl.pallas_call(
         expert_kernel,
         grid=(chips // BLOCKS,),
         out_shape=jax.ShapeDtypeStruct(rows_in.shape, jnp.bfloat16),
         in_specs=[
-            pl.BlockSpec((BLOCKS, 2, tokens), lambda i: (i, 0, 0)),
-            pl.BlockSpec((BLOCKS, 2, tokens), lambda i: (i, 0, 0)),
+            pl.BlockSpec((BLOCKS, 8, tokens), lambda i: (i, 0, 0)),
             pl.BlockSpec((BLOCKS, tokens, width), lambda i: (i, 0, 0)),
             pl.BlockSpec(memory_space=pl.ANY),
             pl.BlockSpec(memory_space=pl.ANY),
@@ -395,7 +741,7 @@
         ],
         compiler_params=pltpu.CompilerParams(vmem_limit_bytes=60 << 20),
         name="experts",
-    )(ranks, gains, rows_in, own, other)
+    )(tables, rows_in, own, other)
 
 
 def slot_tables(routes, route_weights):
@@ -405,7 +751,9 @@
     named = jnp.any(hit, axis=2)
     earlier = jnp.triu(jnp.ones((tokens, tokens), jnp.bfloat16), 1)
     ranks = jnp.dot(named.astype(jnp.bfloat16), earlier, preferred_element_type=jnp.float32)
-    return jnp.where(named, ranks, -1.0), gains
+    ranks = jnp.where(named, ranks, -1.0)
+    pairs = [t.reshape(CHIPS, 2, tokens) for t in (gains, ranks)]
+    return jnp.concatenate(pairs + [jnp.zeros((CHIPS, 4, tokens), jnp.float32)], axis=1)
 
 
 def shards(
@@ -423,21 +771,7 @@
 ):
     total_row_count = hidden.shape[0]
     lane_index = lax.axis_index("exp")
-    heads_per_group = QUERY_HEADS // KEY_VALUE_HEADS
-
-    tables = jnp.stack(slot_tables(routes, route_weights))
-    tables = lax.all_gather(tables, "exp", axis=0)
     weight_piece = lax.all_gather(expert_weights[0], "req", axis=0)
-    weight_other = lax.ppermute(weight_piece, "exp", [(i, i ^ 1) for i in range(EXPERTS)])
-    tables = lax.dynamic_index_in_dim(
-        tables.reshape(CHIPS, 2, 2, CHIPS, 2, total_row_count),
-        lax.rem(lane_index, 2),
-        1,
-        keepdims=False,
-    )
-    tables = lax.dynamic_index_in_dim(tables, lax.div(lane_index, 2), 2, keepdims=False)
-    tables = jnp.where(lax.rem(lane_index, 2) == 0, tables, tables[:, :, ::-1])
-
     positions = lane_index * total_row_count + jnp.arange(total_row_count, dtype=jnp.int32)
     stream_offsets = positions - prompt_start
     inputs = hidden.astype(jnp.float32)
@@ -448,7 +782,7 @@
     query_rows_all = (
         rotary_embedding(query_rows_all, stream_offsets)
         .astype(jnp.bfloat16)
-        .reshape(total_row_count, KEY_VALUE_HEADS, heads_per_group, HEAD_SIZE)
+        .reshape(total_row_count, QUERY_HEADS * HEAD_SIZE)
     )
     shard_keys = jnp.dot(normalized_input, key_matrix, preferred_element_type=jnp.float32).reshape(
         total_row_count, KEY_VALUE_HEADS, HEAD_SIZE
@@ -461,37 +795,26 @@
     values_local = jnp.dot(
         normalized_input, value_matrix, preferred_element_type=jnp.float32
     ).astype(jnp.bfloat16)
-    stacked = jnp.stack([shard_keys, values_local])
-    key_value_slice = lax.all_gather(stacked, "exp", axis=1, tiled=True)
-    feature_width = key_value_slice.shape[1]
-    key_tile = key_value_slice[0].reshape(feature_width, KEY_VALUE_HEADS, HEAD_SIZE)
-    value_tile = key_value_slice[1].reshape(feature_width, KEY_VALUE_HEADS, HEAD_SIZE)
-    key_pos = jnp.arange(feature_width, dtype=jnp.int32)
-    scores = jnp.einsum(
-        "tgrd,sgd->tgrs", query_rows_all, key_tile, preferred_element_type=jnp.float32
-    ) * HEAD_SIZE ** (-0.5)
-    valid = (key_pos[None, :] >= prompt_start[:, None]) & (key_pos[None, :] <= positions[:, None])
-    valid = valid[:, None, None, :]
-    masked = jnp.where(valid, scores, jnp.float32(-1e30))
-    new_max = jnp.max(masked, axis=-1)
-    probs = jnp.where(valid, jnp.exp(masked - new_max[..., None]), jnp.float32(0.0))
-    totals = jnp.sum(probs, axis=-1)
-    attention_mixed = jnp.einsum(
-        "tgrs,sgd->tgrd", probs.astype(jnp.bfloat16), value_tile, preferred_element_type=jnp.float32
-    )
-    attention = (
-        (attention_mixed / totals[..., None])
-        .reshape(total_row_count, QUERY_HEADS * HEAD_SIZE)
-        .astype(jnp.bfloat16)
+    pairs = jnp.concatenate(
+        [
+            side[:, p * 128 : (p + 1) * 128]
+            for p in range(KEY_VALUE_HEADS // 2)
+            for side in (shard_keys, values_local)
+        ],
+        axis=1,
+    )
+    starts = jnp.broadcast_to(prompt_start.astype(jnp.float32)[None], (8, total_row_count))
+    attention, tables = attend(
+        query_rows_all, pairs, starts, slot_tables(routes, route_weights), 0
     )
     residual = inputs + jnp.dot(attention, output_weight, preferred_element_type=jnp.float32)
     moe_in = rms_norm(residual, ffn_gain).astype(jnp.bfloat16)
 
-    rows_in = gather_rows(moe_in, 1)
-    parts = run_experts(tables[:, 0], tables[:, 1], rows_in, weight_piece, weight_other)
+    rows_in, weight_other = gather_rows(moe_in, weight_piece, 1)
+    parts = run_experts(tables, rows_in, weight_piece, weight_other)
     moe_sum = scatter_sums(parts, 2)
     layer_out = (residual + moe_sum).astype(jnp.bfloat16)
-    return (layer_out, stacked[0], stacked[1])
+    return (layer_out, shard_keys, values_local)
 
 
 def solution(mesh):

time: 337 us -> 182 us (0.54)
  waiting for transfers between devices: 141 us -> 0.68 us
  Pallas kernels: 98.6 us -> 146 us
  matrix products: 51.2 us -> 11.5 us
  local copies, waits for them, and re-layouts: 21 us -> 1.88 us
    all_gather x2 -> x0, waiting for transfers between devices: 88.7 us -> none  [the longest x1 56 us: shards(): key_value_slice = lax.all_gather(stacked, 'exp', axis=1, tiled=True)]
    all_gather x1, waiting for transfers between devices: 51.7 us -> 0.01 us  [shards(): weight_piece = lax.all_gather(expert_weights[0], 'req', axis=0)]
    pallas_call x1 -> x2, Pallas kernels: 37.9 us -> 85.5 us  [the longest x1 47.3 us: attend(): pl.pallas_call(attention_kernel, out_shape=(jax.ShapeDtypeStruct((rows, w...]
    sub x1 -> x0, matrix products: 26.6 us -> none  [shards(): masked - new_max[..., None]]
    slice x3 -> x0, local copies, waits for them, and re-layouts: 18.6 us -> none  [the longest x2 12.2 us: shards(): key_value_slice[0].reshape(feature_width, KEY_VALUE_HEADS, HEAD_SIZE)]
    dot_general x1 -> x0, matrix products: 13.2 us -> none  [shards(): jnp.einsum('tgrs,sgd->tgrd', probs.astype(jnp.bfloat16), value_tile, pref...]
  transfers between devices with their start and end apart: 4 -> 1, of which waited for: 3 -> 0; matrix products, arithmetic and copies ran while one was open for 23% -> 10% of each run, Pallas kernels for 11% -> 26%
where the time goes in v3:
time: 182 us; the launch traced here: 181 us
  Pallas kernels  146 us (80%)
  between operations  14.3 us (8%)
  matrix products  11.5 us (6%)
  other arithmetic  5.89 us (3%)
  local copies, waits for them, and re-layouts  1.88 us (1%)
    pallas_call x1, Pallas kernels, attend(): pl.pallas_call(attention_kernel, out_shape=(jax.ShapeDtypeStruct((rows, w...  47.3 us
    pallas_call x1, Pallas kernels, scatter_sums(): pl.pallas_call(kernel, out_shape=jax.ShapeDtypeStruct((rows, width), jnp....  39.5 us
    pallas_call x1, Pallas kernels, gather_rows(): pl.pallas_call(kernel, out_shape=(jax.ShapeDtypeStruct((CHIPS, rows, widt...  38.2 us
    pallas_call x1, Pallas kernels, run_experts(): pl.pallas_call(expert_kernel, grid=(chips // BLOCKS,), out_shape=jax.Shap...  21.3 us
    dot_general x1, matrix products, shards(): jnp.dot(normalized_input, query_weight, preferred_element_type=jnp.float32)  4.4 us
  transfers between devices with their start and end apart: 1, of which 0 were waited for; matrix products, arithmetic and copies ran while one was open for 10% of the time, Pallas kernels for 26%

profile of v3, /device:TPU:0, one launch (start us, length us, event | category | flops | bytes accessed | tf_op | source)
XLA Modules:
  0.0 180.6 jit_solution(13777160729897926732)
XLA Ops:
  7.2 0.0 copy-start
  7.2 0.0 all-gather.2.cloned.1.call-start
  7.2 0.7 all-gather.2.cloned.1.call-update
  8.0 1.2 fusion
  9.1 0.7 fusion.15
  9.9 0.1 multiply_cosine_fusion
  10.0 1.8 fusion.11
  11.9 0.1 copy.38
  12.0 4.4 %fusion.13 = f32[128,1536]{0,1:T(8,128)S(1)} fusion(bf16[1536,1536]{1,0:T(8,128)(2,1)} %param.13, bf16[128,1536]{1,0:T(8,128)(2,1)S(1)} %copy-done.1, f32[1536]{0:T(1024)S(1)} %copy-done.5, f32[128]{0:T(128)S(1)} %add_rsqrt_fusion.1), kind=kOutput, calls=%fused_computation.42 | convolution fusion | flops 604766208 | bytes 5904896 | tf_op jit(solution)/shard_map/dot_general | solution.py:779
  16.4 0.1 subtract_convert_fusion
  16.6 0.9 copy.42.queries
  17.5 0.1 pad.2.clone
  17.6 0.1 fusion.3
  17.7 0.1 convolution_select_fusion
  17.9 1.8 %convolution_convert_fusion = bf16[128,512]{1,0:T(8,128)(2,1)S(1)} fusion(bf16[1536,512]{1,0:T(8,128)(2,1)} %param.15, bf16[128,1536]{1,0:T(8,128)(2,1)S(1)} %copy-done.1, f32[1536]{0:T(1024)S(1)} %copy-done.5, f32[128]{0:T(128)S(1)} %add_rsqrt_fusion.1), kind=kOutput, calls=%fused_computation.3 | convolution fusion | flops 202178560 | bytes 2103808 | tf_op jit(solution)/shard_map/dot_general | solution.py:795
  19.9 0.7 maximum_maximum_fusion.given
  20.6 0.6 broadcast_in_dim.20.starts
  21.2 47.3 %attention.1 = (bf16[128,1536]{1,0:T(8,128)(2,1)}, f32[16,8,128]{2,1,0:T(8,128)}) custom-call(bf16[128,1536]{1,0:T(8,128)(2,1)} %copy.42.queries, bf16[128,1024]{1,0:T(8,128)(2,1)} %copy-done.3, f32[8,128]{1,0:T(8,128)} %broadcast_in_dim.20.starts, f32[16,8,128]{2,1,0:T(8,128)} %maximum_maximum_fusion.given), custom_call_target="tpu_custom_call" | custom-call | tf_op jit(solution)/shard_map/attention/pallas_call | solution.py:492
  68.4 3.3 %multiply_reduce_fusion = (f32[128]{0:T(128)S(1)}, f32[128,1536]{1,0:T(8,128)S(1)}) fusion(bf16[128,1536]{1,0:T(8,128)(2,1)} %get-tuple-element.7, bf16[1536,1536]{1,0:T(8,128)(2,1)} %param.16, bf16[128,1536]{1,0:T(8,128)(2,1)S(1)} %copy-done.1), kind=kOutput, calls=%fused_computation.10 | convolution fusion | flops 604766080 | bytes 6291968 | tf_op jit(solution)/shard_map/dot_general | solution.py:810
  71.8 0.9 multiply_convert_fusion.own
  72.7 38.2 %gather_rows.1 = (bf16[16,128,1536]{2,1,0:T(8,128)(2,1)}, bf16[4,3,1536,128]{3,2,1,0:T(8,128)(2,1)}) custom-call(bf16[128,1536]{1,0:T(8,128)(2,1)} %multiply_convert_fusion.own, bf16[4,3,1536,128]{3,2,1,0:T(8,128)(2,1)} %all-gather.2.cloned.1.call-done.given.own), custom_call_target="tpu_custom_call" | custom-call | tf_op jit(solution)/shard_map/gather_rows/pallas_call | solution.py:186
  110.9 21.3 %experts.1.given = bf16[16,128,1536]{2,1,0:T(8,128)(2,1)} custom-call(f32[16,8,128]{2,1,0:T(8,128)} %get-tuple-element.8.tables, bf16[16,128,1536]{2,1,0:T(8,128)(2,1)} %get-tuple-element.9.rows_in, bf16[4,3,1536,128]{3,2,1,0:T(8,128)(2,1)} %all-gather.2.cloned.1.call-done.given.own, bf16[4,3,1536,128]{3,2,1,0:T(8,128)(2,1)} %get-tuple-element.10.other), custom_call_target="tpu_custom_call" | custom-call | tf_op jit(solution)/shard_map/experts/pallas_call | solution.py:725
  132.2 39.5 %scatter_sums.1 = f32[128,1536]{1,0:T(8,128)} custom-call(bf16[16,128,1536]{2,1,0:T(8,128)(2,1)} %experts.1.given), custom_call_target="tpu_custom_call" | custom-call | tf_op jit(solution)/shard_map/scatter_sums/pallas_call | solution.py:640
  171.8 2.0 %add_convert_fusion = bf16[128,1536]{1,0:T(8,128)(2,1)} fusion(f32[128,1536]{1,0:T(8,128)S(1)} %get-tuple-element.29, f32[128,1536]{1,0:T(8,128)} %scatter_sums.1), kind=kLoop, calls=%fused_computation.8 | loop fusion | flops 393216 | bytes 1966080 | tf_op jit(solution)/shard_map/convert_element_type | solution.py:816
  (34 shorter events, 0.3 us)
Async XLA Ops:
  7.2 2.8 %copy-start = (bf16[1536,512]{1,0:T(8,128)(2,1)S(1)}, bf16[1536,512]{1,0:T(8,128)(2,1)}, u32[]{:S(2)}) copy-start(bf16[1536,512]{1,0:T(8,128)(2,1)} %param.14) | copy-start | bytes 4718596
  7.2 4.8 %copy-start.1 = (bf16[128,1536]{1,0:T(8,128)(2,1)S(1)}, bf16[128,1536]{1,0:T(8,128)(2,1)}, u32[]{:S(2)}) copy-start(bf16[128,1536]{1,0:T(8,128)(2,1)} %param.11) | copy-start | bytes 1179652
  7.2 4.8 %copy-start.5 = (f32[1536]{0:T(1024)S(1)}, f32[1536]{0:T(1024)}, u32[]{:S(2)}) copy-start(f32[1536]{0:T(1024)} %param.12) | copy-start | bytes 18436
  7.2 65.5 %all-gather.2.cloned.1.call-start = ((), (), s32[]{:S(2)}) async-start(), calls=%async_computation | async-start | bytes 5898240 | tf_op jit(solution)/shard_map/all_gather | solution.py:774
  11.8 5.8 %copy-start.6 = (s32[128,8]{0,1:T(8,128)S(1)}, s32[128,8]{0,1:T(8,128)}, u32[]{:S(2)}) copy-start(s32[128,8]{0,1:T(8,128)} %param.19) | copy-start | bytes 12292
  11.9 5.8 %copy-start.8 = (f32[128,8]{0,1:T(8,128)S(1)}, f32[128,8]{0,1:T(8,128)}, u32[]{:S(2)}) copy-start(f32[128,8]{0,1:T(8,128)} %param.20) | copy-start | bytes 12292
  12.0 7.8 %copy-start.2 = (bf16[128,512]{1,0:T(8,128)(2,1)}, bf16[128,512]{1,0:T(8,128)(2,1)S(1)}, u32[]{:S(2)}) copy-start(bf16[128,512]{1,0:T(8,128)(2,1)S(1)} %copy.38) | copy-start | bytes 393220
  17.9 53.9 %copy-start.7 = (f32[1536]{0:T(1024)S(1)}, f32[1536]{0:T(1024)}, u32[]{:S(2)}) copy-start(f32[1536]{0:T(1024)} %param.18) | copy-start | bytes 18436
  19.7 91.2 %copy-start.4 = (bf16[128,512]{1,0:T(8,128)(2,1)}, bf16[128,512]{1,0:T(8,128)(2,1)S(1)}, u32[]{:S(2)}) copy-start(bf16[128,512]{1,0:T(8,128)(2,1)S(1)} %convolution_convert_fusion) | copy-start | bytes 393220
  19.9 1.3 copy-start.3
Sparse Core Ops, SparseCore 0:
  9.7 55.3 all-gather.1

commit v4 on v3

--- a/solution.py
+++ b/solution.py
@@ -51,6 +51,9 @@
 
     def device(self, dy, dx):
         return {"exp": self.chip(dy, dx) * 2 + self.core}
+
+    def level(self, dz):
+        return {"req": lax.rem(lax.axis_index("req") + dz + SIDE, SIDE)}
 
     def partner(self):
         return {"exp": self.chip(0, 0) * 2 + 1 - self.core}
@@ -213,17 +216,17 @@
 
 
 def attention_kernel(
-    queries, pairs, starts, given,
-    out, held,
+    queries, pairs, starts, given, weights,
+    out, held, gathered, partners,
     near, store, asked, begin, packed, peak, total, bias, done,
-    give, take, x_send, x_recv, y_send, y_recv, q_send, q_recv, o_send, o_recv, sems,
+    give, take, x_send, x_recv, y_send, y_recv, q_send, q_recv, o_send, o_recv, w_send, w_recv, sems,
 ):
     plane = Plane()
     core, odd = plane.core, lax.rem(plane.x, 2)
     here = plane.chip(0, 0)
     rows = queries.shape[0]
     friends = [plane.partner(), plane.mirror(True), plane.mirror(False)]
-    greet(plane, OTHERS, [friends[0], friends[2]])
+    greet(plane, OTHERS, [friends[0], friends[2], plane.level(1), plane.level(-1)])
 
     mine = 2 * core + odd
     theirs = [2 * (1 - core) + odd, 2 * core + 1 - odd, 2 * (1 - core) + 1 - odd]
@@ -296,6 +299,23 @@
             take.at[n],
             plane.device(dy, dx),
         )
+
+    def slice_copy(n):
+        if n < 2:
+            return remote(
+                weights, gathered.at[n], w_send.at[n], w_recv.at[n], plane.level((1, -1)[n])
+            )
+        if n < 4:
+            size = weights.shape[1] // 2
+            part = pl.ds((n - 2) * size, size)
+            return remote(
+                gathered.at[n - 2, :, part],
+                gathered.at[2, :, part],
+                w_send.at[n],
+                w_recv.at[n],
+                plane.level((1, -1)[n - 2]),
+            )
+        return remote(weights, partners, w_send.at[n], w_recv.at[n], friends[0])
 
     own_asked = pltpu.make_async_copy(
         queries.at[:, lanes(mine, PAIR_WIDTH)], asked.at[core], sems.at[4]
@@ -328,6 +348,8 @@
             along(h, i, 1).start()
     for n in range(len(OTHERS)):
         table(n).start()
+    for n in (0, 1, 4):
+        slice_copy(n).start()
 
     own_asked.wait()
     own_begin.wait()
@@ -411,6 +433,9 @@
                 for n in (2, 3):
                     for h in (0, 1):
                         along(h, i, n, True).wait_recv()
+            for n in (0, 1):
+                slice_copy(n).wait_recv()
+                slice_copy(n + 2).start()
 
         dy = jnp.where(step == 0, 0, jnp.where(step == 1, SIDE - 1, step - 1))
         dy = jnp.where(step == 3, 2, dy)
@@ -484,9 +509,13 @@
     for n in range(3):
         reply(n, True).wait_recv()
         reply(n).wait_send()
-
-
-def attend(queries, pairs, starts, tables, collective_id):
+    for n in (2, 3, 4):
+        slice_copy(n).wait_recv()
+    for n in range(5):
+        slice_copy(n).wait_send()
+
+
+def attend(queries, pairs, starts, tables, weights, collective_id):
     rows, width = queries.shape
     dma = pltpu.SemaphoreType.DMA
     return pl.pallas_call(
@@ -494,9 +523,12 @@
         out_shape=(
             jax.ShapeDtypeStruct((rows, width), jnp.bfloat16),
             jax.ShapeDtypeStruct(tables.shape, tables.dtype),
+            jax.ShapeDtypeStruct((3, *weights.shape), weights.dtype),
+            jax.ShapeDtypeStruct(weights.shape, weights.dtype),
         ),
-        in_specs=[pl.BlockSpec(memory_space=pltpu.VMEM)] * 4,
-        out_specs=(pl.BlockSpec(memory_space=pltpu.VMEM),) * 2,
+        in_specs=[pl.BlockSpec(memory_space=pltpu.VMEM)] * 4 + [pl.BlockSpec(memory_space=pl.ANY)],
+        out_specs=(pl.BlockSpec(memory_space=pltpu.VMEM),) * 2
+        + (pl.BlockSpec(memory_space=pl.ANY),) * 2,
         scratch_shapes=[
             pltpu.VMEM((rows, 512), jnp.bfloat16),
             pltpu.VMEM((CHIPS, 2 * rows, 256), jnp.bfloat16),
@@ -517,13 +549,15 @@
             dma((6,)),
             dma((3,)),
             dma((3,)),
+            dma((5,)),
+            dma((5,)),
             dma((8,)),
         ],
         compiler_params=pltpu.CompilerParams(
             collective_id=collective_id, has_side_effects=True, vmem_limit_bytes=60 << 20
         ),
         name="attention",
-    )(queries, pairs, starts, tables)
+    )(queries, pairs, starts, tables, weights)
 
 
 class Scatter:
@@ -659,15 +693,15 @@
 BLOCKS = 4
 
 
-def expert_kernel(tables, rows_in, own, other, out, weights, picked, made, sems):
+def expert_kernel(tables, rows_in, own, own_rest, other, other_rest, out, weights, picked, made, sems):
     step = pl.program_id(0)
     core = lax.rem(lax.axis_index("exp"), 2)
 
     def loads():
-        for e, source in enumerate((own, other)):
+        for e, (first, rest) in enumerate(((own, own_rest), (other, other_rest))):
             for r in range(4):
                 yield pltpu.make_async_copy(
-                    source.at[r],
+                    first if r == 0 else rest.at[r - 1],
                     weights.at[core if e == 0 else 1 - core, :, :, pl.ds(r * 128, 128)],
                     sems.at[e * 4 + r],
                 )
@@ -720,7 +754,7 @@
         ).astype(jnp.bfloat16)
 
 
-def run_experts(tables, rows_in, own, other):
+def run_experts(tables, rows_in, *weights):
     chips, tokens, width = rows_in.shape
     return pl.pallas_call(
         expert_kernel,
@@ -729,9 +763,8 @@
         in_specs=[
             pl.BlockSpec((BLOCKS, 8, tokens), lambda i: (i, 0, 0)),
             pl.BlockSpec((BLOCKS, tokens, width), lambda i: (i, 0, 0)),
-            pl.BlockSpec(memory_space=pl.ANY),
-            pl.BlockSpec(memory_space=pl.ANY),
-        ],
+        ]
+        + [pl.BlockSpec(memory_space=pl.ANY)] * 4,
         out_specs=pl.BlockSpec((BLOCKS, tokens, width), lambda i: (i, 0, 0)),
         scratch_shapes=[
             pltpu.VMEM((2, 3, width, FF), jnp.bfloat16),
@@ -741,7 +774,7 @@
         ],
         compiler_params=pltpu.CompilerParams(vmem_limit_bytes=60 << 20),
         name="experts",
-    )(tables, rows_in, own, other)
+    )(tables, rows_in, *weights)
 
 
 def slot_tables(routes, route_weights):
@@ -771,7 +804,6 @@
 ):
     total_row_count = hidden.shape[0]
     lane_index = lax.axis_index("exp")
-    weight_piece = lax.all_gather(expert_weights[0], "req", axis=0)
     positions = lane_index * total_row_count + jnp.arange(total_row_count, dtype=jnp.int32)
     stream_offsets = positions - prompt_start
     inputs = hidden.astype(jnp.float32)
@@ -804,14 +836,15 @@
         axis=1,
     )
     starts = jnp.broadcast_to(prompt_start.astype(jnp.float32)[None], (8, total_row_count))
-    attention, tables = attend(
-        query_rows_all, pairs, starts, slot_tables(routes, route_weights), 0
+    own = expert_weights[0]
+    attention, tables, own_rest, other = attend(
+        query_rows_all, pairs, starts, slot_tables(routes, route_weights), own, 0
     )
     residual = inputs + jnp.dot(attention, output_weight, preferred_element_type=jnp.float32)
     moe_in = rms_norm(residual, ffn_gain).astype(jnp.bfloat16)
 
-    rows_in, weight_other = gather_rows(moe_in, weight_piece, 1)
-    parts = run_experts(tables, rows_in, weight_piece, weight_other)
+    rows_in, other_rest = gather_rows(moe_in, own_rest, 1)
+    parts = run_experts(tables, rows_in, own, own_rest, other, other_rest)
     moe_sum = scatter_sums(parts, 2)
     layer_out = (residual + moe_sum).astype(jnp.bfloat16)
     return (layer_out, shard_keys, values_local)

time: 182 us -> 179 us (0.984)
  between operations: 14.3 us -> 0.9 us
  Pallas kernels: 146 us -> 157 us
    pallas_call x1, Pallas kernels: 47.3 us -> 58.4 us  [attend(): pl.pallas_call(attention_kernel, out_shape=(jax.ShapeDtypeStruct((rows, w...]
  transfers between devices with their start and end apart: 1 -> 0, of which waited for: 0 -> 0; matrix products, arithmetic and copies ran while one was open for 10% -> 0% of each run, Pallas kernels for 26% -> 0%
where the time goes in v4:
time: 179 us
  Pallas kernels  157 us (88%)
  matrix products  11.7 us (7%)
  other arithmetic  7.42 us (4%)
  local copies, waits for them, and re-layouts  1.87 us (1%)
    pallas_call x1, Pallas kernels, attend(): pl.pallas_call(attention_kernel, out_shape=(jax.ShapeDtypeStruct((rows, w...  58.4 us
    pallas_call x1, Pallas kernels, scatter_sums(): pl.pallas_call(kernel, out_shape=jax.ShapeDtypeStruct((rows, width), jnp....  40.4 us
    pallas_call x1, Pallas kernels, gather_rows(): pl.pallas_call(kernel, out_shape=(jax.ShapeDtypeStruct((CHIPS, rows, widt...  37 us
    pallas_call x1, Pallas kernels, run_experts(): pl.pallas_call(expert_kernel, grid=(chips // BLOCKS,), out_shape=jax.Shap...  21.3 us
    dot_general x1, matrix products, shards(): jnp.dot(normalized_input, query_weight, preferred_element_type=jnp.float32)  4.42 us

profile of v4, /device:TPU:0, one launch (start us, length us, event | category | flops | bytes accessed | tf_op | source)
XLA Modules:
  0.0 178.9 jit_solution(3605607285798292502)
XLA Ops:
  0.6 0.0 copy-start
  0.7 1.3 fusion
  2.0 0.1 pad.2.clone
  2.1 0.7 fusion.15
  2.8 0.6 broadcast_in_dim.20.starts
  3.4 0.7 fusion.3
  4.1 0.1 convolution_select_fusion
  4.3 0.8 select_reduce_fusion
  5.0 0.7 maximum_maximum_fusion.given
  5.7 0.1 multiply_cosine_fusion
  5.9 1.4 convolution_convert_fusion
  7.3 0.0 copy-start.4
  7.3 2.4 %fusion.11 = f32[128,512]{0,1:T(8,128)S(1)} fusion(bf16[1536,512]{1,0:T(8,128)(2,1)} %param.14, bf16[128,1536]{1,0:T(8,128)(2,1)} %param.11, f32[1536]{0:T(1024)} %param.12, f32[128]{0:T(128)S(1)} %add_rsqrt_fusion.1), kind=kOutput, calls=%fused_computation.41 | convolution fusion | flops 202113024 | bytes 2234880 | tf_op jit(solution)/shard_map/dot_general | solution.py:819
  9.7 0.1 copy.28
  10.1 4.4 %fusion.13 = f32[128,1536]{0,1:T(8,128)S(1)} fusion(bf16[1536,1536]{1,0:T(8,128)(2,1)} %param.13, bf16[128,1536]{1,0:T(8,128)(2,1)S(1)} %copy-done.1, f32[1536]{0:T(1024)S(1)} %copy-done.5, f32[128]{0:T(128)S(1)} %add_rsqrt_fusion.1), kind=kOutput, calls=%fused_computation.42 | convolution fusion | flops 604766208 | bytes 5904896 | tf_op jit(solution)/shard_map/dot_general | solution.py:811
  14.5 0.1 subtract_convert_fusion
  14.7 0.9 copy.32.queries
  15.6 58.4 %attention.1 = (bf16[128,1536]{1,0:T(8,128)(2,1)}, f32[16,8,128]{2,1,0:T(8,128)}, bf16[3,3,1536,128]{3,2,1,0:T(8,128)(2,1)}, bf16[3,1536,128]{2,1,0:T(8,128)(2,1)}) custom-call(bf16[128,1536]{1,0:T(8,128)(2,1)} %copy.32.queries, bf16[128,1024]{1,0:T(8,128)(2,1)} %copy-done.3, f32[8,128]{1,0:T(8,128)} %broadcast_in_dim.20.starts, ...), custom_call_target="tpu_custom_call" | custom-call | tf_op jit(solution)/shard_map/attention/pallas_call | solution.py:521
  74.0 3.3 %multiply_reduce_fusion = (f32[128]{0:T(128)S(1)}, f32[128,1536]{1,0:T(8,128)S(1)}) fusion(bf16[128,1536]{1,0:T(8,128)(2,1)} %get-tuple-element.9, bf16[1536,1536]{1,0:T(8,128)(2,1)} %param.16, bf16[128,1536]{1,0:T(8,128)(2,1)S(1)} %copy-done.1), kind=kOutput, calls=%fused_computation.10 | convolution fusion | flops 604766080 | bytes 6291968 | tf_op jit(solution)/shard_map/dot_general | solution.py:843
  77.4 0.9 multiply_convert_fusion.own
  78.2 37.0 %gather_rows.1 = (bf16[16,128,1536]{2,1,0:T(8,128)(2,1)}, bf16[3,3,1536,128]{3,2,1,0:T(8,128)(2,1)}) custom-call(bf16[128,1536]{1,0:T(8,128)(2,1)} %multiply_convert_fusion.own, bf16[3,3,1536,128]{3,2,1,0:T(8,128)(2,1)} %get-tuple-element.11.given.own_rest), custom_call_target="tpu_custom_call" | custom-call | tf_op jit(solution)/shard_map/gather_rows/pallas_call | solution.py:189
  115.3 21.3 %experts.1.given = bf16[16,128,1536]{2,1,0:T(8,128)(2,1)} custom-call(f32[16,8,128]{2,1,0:T(8,128)} %get-tuple-element.10.tables, bf16[16,128,1536]{2,1,0:T(8,128)(2,1)} %get-tuple-element.12.rows_in, bf16[3,1536,128]{2,1,0:T(8,128)(2,1)} %bitcast.14, bf16[3,3,1536,128]{3,2,1,0:T(8,128)(2,1)} %get-tuple-element.11.given.own_rest, ...), custom_call_target="tpu_custom_call" | custom-call | tf_op jit(solution)/shard_map/experts/pallas_call | solution.py:759
  136.5 40.4 %scatter_sums.1 = f32[128,1536]{1,0:T(8,128)} custom-call(bf16[16,128,1536]{2,1,0:T(8,128)(2,1)} %experts.1.given), custom_call_target="tpu_custom_call" | custom-call | tf_op jit(solution)/shard_map/scatter_sums/pallas_call | solution.py:674
  177.0 2.0 %add_convert_fusion = bf16[128,1536]{1,0:T(8,128)(2,1)} fusion(f32[128,1536]{1,0:T(8,128)S(1)} %get-tuple-element.30, f32[128,1536]{1,0:T(8,128)} %scatter_sums.1), kind=kLoop, calls=%fused_computation.8 | loop fusion | flops 393216 | bytes 1966080 | tf_op jit(solution)/shard_map/convert_element_type | solution.py:849
  (27 shorter events, 0.3 us)
Async XLA Ops:
  0.6 5.2 %copy-start = (bf16[1536,512]{1,0:T(8,128)(2,1)S(1)}, bf16[1536,512]{1,0:T(8,128)(2,1)}, u32[]{:S(2)}) copy-start(bf16[1536,512]{1,0:T(8,128)(2,1)} %param.15) | copy-start | bytes 4718596
  0.6 9.4 %copy-start.1 = (bf16[128,1536]{1,0:T(8,128)(2,1)S(1)}, bf16[128,1536]{1,0:T(8,128)(2,1)}, u32[]{:S(2)}) copy-start(bf16[128,1536]{1,0:T(8,128)(2,1)} %param.11) | copy-start | bytes 1179652
  0.7 9.4 %copy-start.5 = (f32[1536]{0:T(1024)S(1)}, f32[1536]{0:T(1024)}, u32[]{:S(2)}) copy-start(f32[1536]{0:T(1024)} %param.12) | copy-start | bytes 18436
  7.3 7.2 %copy-start.4 = (bf16[128,512]{1,0:T(8,128)(2,1)}, bf16[128,512]{1,0:T(8,128)(2,1)S(1)}, u32[]{:S(2)}) copy-start(bf16[128,512]{1,0:T(8,128)(2,1)S(1)} %convolution_convert_fusion) | copy-start | bytes 393220
  9.9 4.8 %copy-start.2 = (bf16[128,512]{1,0:T(8,128)(2,1)}, bf16[128,512]{1,0:T(8,128)(2,1)S(1)}, u32[]{:S(2)}) copy-start(bf16[128,512]{1,0:T(8,128)(2,1)S(1)} %copy.28) | copy-start | bytes 393220
  10.1 4.6 %copy-start.3 = (bf16[128,1024]{1,0:T(8,128)(2,1)}, bf16[128,1024]{1,0:T(8,128)(2,1)S(1)}, u32[]{:S(2)}) copy-start(bf16[128,1024]{1,0:T(8,128)(2,1)S(1)} %slice_dynamic-update-slice_fusion.pairs) | copy-start | bytes 786436
  74.0 3.4 %copy-start.6 = (f32[1536]{0:T(1024)S(1)}, f32[1536]{0:T(1024)}, u32[]{:S(2)}) copy-start(f32[1536]{0:T(1024)} %param.18) | copy-start | bytes 18436

commit v5 on v4

--- a/solution.py
+++ b/solution.py
@@ -85,126 +85,6 @@
         device_id=device,
         device_id_type=pl.DeviceIdType.MESH,
     )
-
-
-def turn(h, a, b):
-    return (b, a) if h == 0 else (a, b)
-
-
-class Gather:
-    COPIES = 20
-
-    def __init__(self, plane, own, slots, send, recv, rows, slot_of):
-        self.plane, self.own, self.slots = plane, own, slots
-        self.send, self.recv, self.rows, self.slot_of = send, recv, rows, slot_of
-
-    def span(self, h, part):
-        half = self.rows // 2
-        if part is None:
-            return pl.ds(h * half, half)
-        return pl.ds(h * half + part * (half // 2), half // 2)
-
-    def step(self, k):
-        if k < 4:
-            return (
-                ((0, 0), None, (1, 0)),
-                ((0, 0), None, (-1, 0)),
-                ((-1, 0), 0, (1, 0)),
-                ((1, 0), 1, (-1, 0)),
-            )[k]
-        a = (0, -1, 1, 2)[(k - 4) // 4]
-        return (
-            ((a, 0), None, (0, 1)),
-            ((a, 0), None, (0, -1)),
-            ((a, -1), 0, (0, 1)),
-            ((a, 1), 1, (0, -1)),
-        )[(k - 4) % 4]
-
-    def make(self, h, k, incoming):
-        (a, b), part, (da, db) = self.step(k)
-        span = self.span(h, part)
-        if incoming:
-            a, b = a - da, b - db
-        slot = self.slot_of(self.plane.chip(*turn(h, a, b)))
-        there = self.slots.at[slot, span]
-        here = self.own.at[span] if (a, b) == (0, 0) else there
-        return pltpu.make_async_remote_copy(
-            src_ref=here,
-            dst_ref=there,
-            send_sem=self.send.at[h * self.COPIES + k],
-            recv_sem=self.recv.at[h * self.COPIES + k],
-            device_id=self.plane.device(*turn(h, da, db)),
-            device_id_type=pl.DeviceIdType.MESH,
-        )
-
-    def start(self, *ks):
-        for k in ks:
-            for h in (0, 1):
-                self.make(h, k, False).start()
-
-    def arrive(self, k, *then):
-        for h in (0, 1):
-            self.make(h, k, True).wait_recv()
-            for t in then:
-                self.make(h, t, False).start()
-
-    def run(self):
-        self.start(0, 1)
-        self.start(4, 5)
-        self.arrive(0, 2, 8, 9)
-        self.arrive(1, 3, 12, 13)
-        self.arrive(4, 6)
-        self.arrive(5, 7)
-        self.arrive(2)
-        self.arrive(3, 16, 17)
-        for base in (8, 12, 16):
-            self.arrive(base, base + 2)
-            self.arrive(base + 1, base + 3)
-        for base in (4, 8, 12, 16):
-            self.arrive(base + 2)
-            self.arrive(base + 3)
-
-    def finish(self):
-        for h in (0, 1):
-            for k in range(self.COPIES):
-                self.make(h, k, False).wait_send()
-
-
-def gather_rows(block, weights, collective_id):
-    rows, width = block.shape
-
-    def kernel(own, given, slots, other, send, recv, sems):
-        plane = Plane()
-        greet(plane, NEXT, [plane.partner()])
-        swap = remote(given, other, sems.at[1], sems.at[2], plane.partner())
-        gather = Gather(plane, own, slots, send, recv, rows, lambda chip: chip)
-        mine = pltpu.make_async_copy(own, slots.at[plane.chip(0, 0)], sems.at[0])
-        mine.start()
-        swap.start()
-        gather.run()
-        gather.finish()
-        mine.wait()
-        swap.wait()
-
-    return pl.pallas_call(
-        kernel,
-        out_shape=(
-            jax.ShapeDtypeStruct((CHIPS, rows, width), block.dtype),
-            jax.ShapeDtypeStruct(weights.shape, weights.dtype),
-        ),
-        in_specs=[
-            pl.BlockSpec(memory_space=pltpu.VMEM),
-            pl.BlockSpec(memory_space=pl.ANY),
-        ],
-        out_specs=(pl.BlockSpec(memory_space=pl.ANY), pl.BlockSpec(memory_space=pl.ANY)),
-        scratch_shapes=[
-            pltpu.SemaphoreType.DMA((2 * Gather.COPIES,)),
-            pltpu.SemaphoreType.DMA((2 * Gather.COPIES,)),
-            pltpu.SemaphoreType.DMA((3,)),
-        ],
-        compiler_params=pltpu.CompilerParams(collective_id=collective_id, has_side_effects=True),
-        name="gather_rows",
-    )(block, weights)
 
 
 KEYS = 512
@@ -324,6 +204,8 @@
     own_table = pltpu.make_async_copy(given.at[here], held.at[here], sems.at[6])
 
     swap.start()
+    for n in (0, 1, 4):
+        slice_copy(n).start()
     for h in (0, 1):
         if h == 1:
             ask(0).start()
@@ -348,8 +230,6 @@
             along(h, i, 1).start()
     for n in range(len(OTHERS)):
         table(n).start()
-    for n in (0, 1, 4):
-        slice_copy(n).start()
 
     own_asked.wait()
     own_begin.wait()
@@ -427,15 +307,18 @@
                         along(h, i, n, True).wait_recv()
                         along(h, i, n + 2).start()
 
+        @pl.when(step == 2)
+        def _():
+            for n in (0, 1):
+                slice_copy(n).wait_recv()
+                slice_copy(n + 2).start()
+
         @pl.when(step == 3)
         def _():
             for i in range(4):
                 for n in (2, 3):
                     for h in (0, 1):
                         along(h, i, n, True).wait_recv()
-            for n in (0, 1):
-                slice_copy(n).wait_recv()
-                slice_copy(n + 2).start()
 
         dy = jnp.where(step == 0, 0, jnp.where(step == 1, SIDE - 1, step - 1))
         dy = jnp.where(step == 3, 2, dy)
@@ -560,221 +443,327 @@
     )(queries, pairs, starts, tables, weights)
 
 
-class Scatter:
-    COPIES = 20
-
-    def __init__(self, plane, parts, hold, send, recv, rows):
-        self.plane, self.parts, self.hold = plane, parts, hold
-        self.send, self.recv, self.rows = send, recv, rows
-
-    def span(self, h, part):
-        half = self.rows // 2
-        if part is None:
-            return pl.ds(h * half, half)
-        return pl.ds(h * half + part * (half // 2), half // 2)
-
-    def step(self, k):
-        if k < 16:
-            q = (2, 1, 3, 0)[k // 4]
-            return (
-                ((2, q), 0, (1, 0)),
-                ((2, q), 1, (-1, 0)),
-                ((1, q), None, (1, 0)),
-                ((3, q), None, (-1, 0)),
-            )[k % 4]
-        return (
-            ((0, 2), 0, (0, 1)),
-            ((0, 2), 1, (0, -1)),
-            ((0, 1), None, (0, 1)),
-            ((0, 3), None, (0, -1)),
-        )[k % 4]
-
-    def make(self, h, k):
-        (a, b), part, (da, db) = self.step(k)
-        span = self.span(h, part)
-        size = self.rows // 2 if part is None else self.rows // 4
-        return pltpu.make_async_remote_copy(
-            src_ref=self.parts.at[self.plane.chip(*turn(h, a, b)), span],
-            dst_ref=self.hold.at[h, k, pl.ds(0, size)],
-            send_sem=self.send.at[h * self.COPIES + k],
-            recv_sem=self.recv.at[h * self.COPIES + k],
-            device_id=self.plane.device(*turn(h, da, db)),
-            device_id_type=pl.DeviceIdType.MESH,
-        )
-
-    def start(self, k):
-        for h in (0, 1):
-            self.make(h, k).start()
-
-    def add(self, h, k, place, part):
-        size = self.rows // 4
-        at = (self.plane.chip(*turn(h, *place)), self.span(h, part))
-        self.parts[at] = (
-            self.parts[at].astype(jnp.float32)
-            + self.hold[h, k, pl.ds(0, size)].astype(jnp.float32)
-        ).astype(jnp.bfloat16)
-
-    def relay(self, base, near, far):
-        for h in (0, 1):
-            self.make(h, base).wait_recv()
-            self.add(h, base, near, 0)
-            self.make(h, base + 2).start()
-        for h in (0, 1):
-            self.make(h, base + 1).wait_recv()
-            self.add(h, base + 1, far, 1)
-            self.make(h, base + 3).start()
-
-    def total(self, h, base, place):
-        self.make(h, base + 2).wait_recv()
-        self.make(h, base + 3).wait_recv()
-        at = (self.plane.chip(*turn(h, *place)), self.span(h, None))
-        return (
-            self.parts[at].astype(jnp.float32)
-            + self.hold[h, base + 2].astype(jnp.float32)
-            + self.hold[h, base + 3].astype(jnp.float32)
-        )
-
-    def run(self, out):
-        for i in range(4):
-            self.start(4 * i)
-            self.start(4 * i + 1)
-        for i, q in enumerate((2, 1, 3, 0)):
-            self.relay(4 * i, (1, q), (3, q))
-        for i, q in enumerate((2, 1, 3, 0)):
-            for h in (0, 1):
-                at = (self.plane.chip(*turn(h, 0, q)), self.span(h, None))
-                self.parts[at] = self.total(h, 4 * i, (0, q)).astype(jnp.bfloat16)
-            if i == 0:
-                self.start(16)
-                self.start(17)
-            if i == 2:
-                self.relay(16, (0, 1), (0, 3))
-        for h in (0, 1):
-            out[self.span(h, None)] = self.total(h, 16, (0, 0))
-
-    def finish(self):
-        for h in (0, 1):
-            for k in range(self.COPIES):
-                self.make(h, k).wait_send()
-
-
-def scatter_sums(parts, collective_id):
-    _, rows, width = parts.shape
-
-    def kernel(given, out, held, hold, send, recv, in_sem):
-        load = pltpu.make_async_copy(given, held, in_sem)
+BLOCKS = 4
+GROUPS = (
+    ((0, 0), (2, 0), (0, -1), (0, 1)),
+    ((-1, 0), (1, 0), (-1, -1), (-1, 1)),
+    ((-1, 2), (1, 2), (1, -1), (1, 1)),
+    ((0, 2), (2, 2), (2, -1), (2, 1)),
+)
+TWO = (0, 2)
+ENDS = (-1, 1)
+
+
+def experts_kernel(
+    own, residual, tables, first, rest, other,
+    out,
+    rows_in, sums, weights, picked, made, hold_q, hold_r, hold_p, hold_d,
+    g_send, g_recv, q_send, q_recv, r_send, r_recv, p_send, p_recv, d_send, d_recv,
+    w_send, w_recv, load_sems,
+):
+    plane = Plane()
+    core = plane.core
+    rows, width = own.shape
+    part_rows = rows // 2
+    even = lax.rem(plane.y + plane.x, 2) == 0
+
+    def turned(o, t):
+        return jnp.where(even, t, o), jnp.where(even, o, t)
+
+    def place(at):
+        return plane.chip(*turned(*at))
+
+    def device(o, t):
+        return plane.device(*turned(o, t))
+
+    def part(n):
+        return pl.ds(n * part_rows, part_rows)
+
+    greet(plane, NEXT, [plane.partner()])
+
+    def gather(k, src, dst, to):
+        return remote(src, dst, g_send.at[k], g_recv.at[k], to)
+
+    def emit(n, incoming=False):
+        d = (1, -1)[n]
+        at = (0, -d) if incoming else (0, 0)
+        return gather(n, own, rows_in.at[place(at)], device(d, 0))
+
+    def pass_on(n, incoming=False):
+        at = (2, 0) if incoming else (0, ENDS[n])
+        ref = rows_in.at[place(at), part(n)]
+        return gather(2 + n, ref, ref, device(0, -ENDS[n]))
+
+    def spread(group, j, n, incoming=False):
+        d = (1, -1)[n]
+        if group == 0:
+            at = (-d, TWO[j]) if incoming else (TWO[j], 0)
+            to = device(0, d)
+        else:
+            at = (ENDS[j], -d) if incoming else (0, ENDS[j])
+            to = device(d, 0)
+        ref = rows_in.at[place(at)]
+        src = own if at == (0, 0) else ref
+        return gather(4 + group * 8 + j * 4 + n, src, ref, to)
+
+    def relay(group, j, n, incoming=False):
+        if group == 0:
+            at = (TWO[j], 2) if incoming else (ENDS[n], TWO[j])
+            to = device(-ENDS[n], 0)
+        else:
+            at = (2, ENDS[j]) if incoming else (ENDS[j], ENDS[n])
+            to = device(0, -ENDS[n])
+        ref = rows_in.at[place(at), part(n)]
+        return gather(4 + group * 8 + j * 4 + 2 + n, ref, ref, to)
+
+    def lanes(r):
+        return pl.ds(r * 128, 128)
+
+    def loads():
+        sources = [(first, core, 0), (other, 1 - core, 0)]
+        sources += [(rest.at[r], core, r + 1) for r in range(3)]
+        for n, (src, e, r) in enumerate(sources):
+            yield pltpu.make_async_copy(src, weights.at[e, :, :, lanes(r)], load_sems.at[n])
+        yield pltpu.make_async_copy(own, rows_in.at[place((0, 0))], load_sems.at[5])
+
+    def swap(r, incoming=False):
+        e = 1 - core if incoming else core
+        return remote(
+            rest.at[r],
+            weights.at[e, :, :, lanes(r + 1)],
+            w_send.at[r],
+            w_recv.at[r],
+            plane.partner(),
+        )
+
+    for n in (0, 1):
+        emit(n).start()
+    for r in range(3):
+        swap(r).start()
+    for n in (0, 1):
+        spread(0, 0, n).start()
+    for load in loads():
         load.start()
-        plane = Plane()
-        greet(plane)
+    for j in (0, 1):
+        emit(j, True).wait_recv()
+        pass_on(j).start()
+        for n in (0, 1):
+            spread(1, j, n).start()
+    for n in (0, 1):
+        pass_on(n, True).wait_recv()
+    for n in (0, 1):
+        spread(0, 1, n).start()
+    for load in loads():
         load.wait()
-        scatter = Scatter(plane, held, hold, send, recv, rows)
-        scatter.run(out)
-        scatter.finish()
-
+    for r in range(3):
+        swap(r, True).wait_recv()
+
+    def far(group, j):
+        return (TWO[j], 2) if group == 0 else (2, ENDS[j])
+
+    def near(group, j, side):
+        return (ENDS[side], TWO[j]) if group == 0 else (ENDS[j], ENDS[side])
+
+    def line(group, along_first):
+        return (lambda d: device(d, 0)) if (group == 0) == along_first else (lambda d: device(0, d))
+
+    def give_far(group, j, n):
+        k = group * 4 + j * 2 + n
+        return remote(
+            sums.at[place(far(group, j)), part(n)],
+            hold_q.at[k],
+            q_send.at[k],
+            q_recv.at[k],
+            line(group, False)(ENDS[n]),
+        )
+
+    def give_near(group, j, side, late):
+        k = group * 4 + j * 2 + side
+        span = part(side if late else 1 - side)
+        return remote(
+            sums.at[place(near(group, j, side)), span],
+            hold_r.at[k, span],
+            r_send.at[2 * k + late],
+            r_recv.at[2 * k + late],
+            line(group, True)(ENDS[side]),
+        )
+
+    def give_across(n):
+        return remote(
+            sums.at[place((2, 0)), part(n)],
+            hold_p.at[n],
+            p_send.at[n],
+            p_recv.at[n],
+            device(ENDS[n], 0),
+        )
+
+    def give_back(side, late):
+        span = part(side if late else 1 - side)
+        return remote(
+            sums.at[place((0, ENDS[side])), span],
+            hold_d.at[side, span],
+            d_send.at[2 * side + late],
+            d_recv.at[2 * side + late],
+            device(0, ENDS[side]),
+        )
+
+    PAIRS = [(group, j) for j in (0, 1) for group in (0, 1)]
+    slot = lax.broadcasted_iota(jnp.int32, (SLOTS, rows), 0).astype(jnp.float32)
+
+    def group_step(g, carry):
+        for when, j in ((1, 0), (2, 1)):
+
+            @pl.when(g == when)
+            def _():
+                for n in (0, 1):
+                    for group in (0, 1):
+                        spread(group, j, n, True).wait_recv()
+                        relay(group, j, n).start()
+
+        @pl.when(g == 3)
+        def _():
+            for group, j in PAIRS:
+                for n in (0, 1):
+                    relay(group, j, n, True).wait_recv()
+            for group, j in PAIRS:
+                for side in (0, 1):
+                    give_near(group, j, side, 0).start()
+
+        ids = []
+        for j in range(BLOCKS):
+            at = place(GROUPS[3][j])
+            for k in range(3):
+                at = jnp.where(g == k, place(GROUPS[k][j]), at)
+            ids.append(at)
+
+        def hits(j, e):
+            return tables[ids[j], 2 + e : 3 + e, :] == slot
+
+        def choice(j):
+            both = jnp.concatenate([hits(j, 0), hits(j, 1)], axis=0)
+            return jnp.where(both, 1.0, 0.0).astype(jnp.bfloat16)
+
+        for j in range(BLOCKS):
+            picked[j] = jnp.dot(
+                choice(j), rows_in[ids[j]], preferred_element_type=jnp.float32
+            ).astype(jnp.bfloat16)
+        for e in (0, 1):
+            chosen = picked[:, e * SLOTS : (e + 1) * SLOTS, :].reshape(BLOCKS * SLOTS, width)
+            gate = jnp.dot(chosen, weights[e, 0], preferred_element_type=jnp.float32)
+            up = jnp.dot(chosen, weights[e, 1], preferred_element_type=jnp.float32)
+            units = (gate / (1.0 + jnp.exp(-gate)) * up).astype(jnp.bfloat16)
+            result = lax.dot_general(
+                units, weights[e, 2], (((1,), (1,)), ((), ())), preferred_element_type=jnp.float32
+            )
+            for j in range(BLOCKS):
+                gain = jnp.sum(
+                    jnp.where(hits(j, e), tables[ids[j], e : e + 1, :], 0.0),
+                    axis=1,
+                    keepdims=True,
+                )
+                made[j, e * SLOTS : (e + 1) * SLOTS, :] = (
+                    result[j * SLOTS : (j + 1) * SLOTS, :] * gain
+                ).astype(jnp.bfloat16)
+        for j in range(BLOCKS):
+            sums[ids[j]] = lax.dot_general(
+                choice(j), made[j], (((0,), (0,)), ((), ())), preferred_element_type=jnp.float32
+            ).astype(jnp.bfloat16)
+        return carry
+
+    lax.fori_loop(0, len(GROUPS), group_step, 0)
+
+    for group, j in PAIRS:
+        for n in (0, 1):
+            give_far(group, j, n).start()
+
+    def add(at, held):
+        sums[at] = (sums[at].astype(jnp.float32) + held.astype(jnp.float32)).astype(jnp.bfloat16)
+
+    for group, j in PAIRS:
+        for side in (0, 1):
+            k = group * 4 + j * 2 + side
+            give_far(group, j, side).wait_recv()
+            add((place(near(group, j, side)), part(side)), hold_q[k])
+            give_near(group, j, side, 1).start()
+
+    def total(group, j):
+        for side in (0, 1):
+            for late in (0, 1):
+                give_near(group, j, side, late).wait_recv()
+        at = place((TWO[j], 0) if group == 0 else (0, ENDS[j]))
+        k = group * 4 + j * 2
+        return at, (
+            sums[at].astype(jnp.float32)
+            + hold_r[k].astype(jnp.float32)
+            + hold_r[k + 1].astype(jnp.float32)
+        )
+
+    at, value = total(0, 1)
+    sums[at] = value.astype(jnp.bfloat16)
+    for n in (0, 1):
+        give_across(n).start()
+    for side in (0, 1):
+        at, value = total(1, side)
+        sums[at] = value.astype(jnp.bfloat16)
+        give_back(side, 0).start()
+    _, value = total(0, 0)
+    out_sum = value + residual[...]
+    for side in (0, 1):
+        give_across(side).wait_recv()
+        add((place((0, ENDS[side])), part(side)), hold_p[side])
+        give_back(side, 1).start()
+    for side in (0, 1):
+        for late in (0, 1):
+            give_back(side, late).wait_recv()
+    out[...] = (
+        out_sum + hold_d[0].astype(jnp.float32) + hold_d[1].astype(jnp.float32)
+    ).astype(out.dtype)
+
+    for n in (0, 1):
+        emit(n).wait_send()
+        pass_on(n).wait_send()
+        give_across(n).wait_send()
+        for late in (0, 1):
+            give_back(n, late).wait_send()
+    for r in range(3):
+        swap(r).wait_send()
+    for group, j in PAIRS:
+        for n in (0, 1):
+            spread(group, j, n).wait_send()
+            relay(group, j, n).wait_send()
+            give_far(group, j, n).wait_send()
+            for late in (0, 1):
+                give_near(group, j, n, late).wait_send()
+
+
+def run_experts(block, residual, tables, weights, collective_id):
+    rows, width = block.shape
+    dma = pltpu.SemaphoreType.DMA
+    vmem = pl.BlockSpec(memory_space=pltpu.VMEM)
+    pairs = [dma((n,)) for n in (20, 8, 16, 2, 4, 3) for _ in (0, 1)]
     return pl.pallas_call(
-        kernel,
-        out_shape=jax.ShapeDtypeStruct((rows, width), jnp.float32),
-        in_specs=[pl.BlockSpec(memory_space=pl.ANY)],
-        out_specs=pl.BlockSpec(memory_space=pltpu.VMEM),
+        experts_kernel,
+        out_shape=jax.ShapeDtypeStruct(block.shape, block.dtype),
+        in_specs=[vmem] * 3 + [pl.BlockSpec(memory_space=pl.ANY)] * 3,
+        out_specs=vmem,
         scratch_shapes=[
             pltpu.VMEM((CHIPS, rows, width), jnp.bfloat16),
-            pltpu.VMEM((2, Scatter.COPIES, rows // 2, width), jnp.bfloat16),
-            pltpu.SemaphoreType.DMA((2 * Scatter.COPIES,)),
-            pltpu.SemaphoreType.DMA((2 * Scatter.COPIES,)),
-            pltpu.SemaphoreType.DMA,
+            pltpu.VMEM((CHIPS, rows, width), jnp.bfloat16),
+            pltpu.VMEM((2, 3, width, FF), jnp.bfloat16),
+            pltpu.VMEM((BLOCKS, 2 * SLOTS, width), jnp.bfloat16),
+            pltpu.VMEM((BLOCKS, 2 * SLOTS, width), jnp.bfloat16),
+            pltpu.VMEM((8, rows // 2, width), jnp.bfloat16),
+            pltpu.VMEM((8, rows, width), jnp.bfloat16),
+            pltpu.VMEM((2, rows // 2, width), jnp.bfloat16),
+            pltpu.VMEM((2, rows, width), jnp.bfloat16),
+            *pairs,
+            dma((6,)),
         ],
         compiler_params=pltpu.CompilerParams(
             collective_id=collective_id, has_side_effects=True, vmem_limit_bytes=60 << 20
         ),
-        name="scatter_sums",
-    )(parts)
-
-
-BLOCKS = 4
-
-
-def expert_kernel(tables, rows_in, own, own_rest, other, other_rest, out, weights, picked, made, sems):
-    step = pl.program_id(0)
-    core = lax.rem(lax.axis_index("exp"), 2)
-
-    def loads():
-        for e, (first, rest) in enumerate(((own, own_rest), (other, other_rest))):
-            for r in range(4):
-                yield pltpu.make_async_copy(
-                    first if r == 0 else rest.at[r - 1],
-                    weights.at[core if e == 0 else 1 - core, :, :, pl.ds(r * 128, 128)],
-                    sems.at[e * 4 + r],
-                )
-
-    @pl.when(step == 0)
-    def _():
-        for load in loads():
-            load.start()
-
-    tokens = rows_in.shape[1]
-    slot = lax.broadcasted_iota(jnp.int32, (SLOTS, tokens), 0).astype(jnp.float32)
-
-    def hits(j):
-        return jnp.concatenate([tables[j, 2 + e : 3 + e, :] == slot for e in (0, 1)], axis=0)
-
-    for j in range(BLOCKS):
-        choose = jnp.where(hits(j), 1.0, 0.0).astype(jnp.bfloat16)
-        picked[j] = jnp.dot(choose, rows_in[j], preferred_element_type=jnp.float32).astype(
-            jnp.bfloat16
-        )
-
-    @pl.when(step == 0)
-    def _():
-        for load in loads():
-            load.wait()
-
-    width = rows_in.shape[2]
-    for e in (0, 1):
-        rows = picked[:, e * SLOTS : (e + 1) * SLOTS, :].reshape(BLOCKS * SLOTS, width)
-        gate = jnp.dot(rows, weights[e, 0], preferred_element_type=jnp.float32)
-        up = jnp.dot(rows, weights[e, 1], preferred_element_type=jnp.float32)
-        units = (gate / (1.0 + jnp.exp(-gate)) * up).astype(jnp.bfloat16)
-        result = lax.dot_general(
-            units, weights[e, 2], (((1,), (1,)), ((), ())), preferred_element_type=jnp.float32
-        )
-        for j in range(BLOCKS):
-            gain = jnp.sum(
-                jnp.where(tables[j, 2 + e : 3 + e, :] == slot, tables[j, e : e + 1, :], 0.0),
-                axis=1,
-                keepdims=True,
-            )
-            made[j, e * SLOTS : (e + 1) * SLOTS, :] = (
-                result[j * SLOTS : (j + 1) * SLOTS, :] * gain
-            ).astype(jnp.bfloat16)
-
-    for j in range(BLOCKS):
-        choose = jnp.where(hits(j), 1.0, 0.0).astype(jnp.bfloat16)
-        out[j] = lax.dot_general(
-            choose, made[j], (((0,), (0,)), ((), ())), preferred_element_type=jnp.float32
-        ).astype(jnp.bfloat16)
-
-
-def run_experts(tables, rows_in, *weights):
-    chips, tokens, width = rows_in.shape
-    return pl.pallas_call(
-        expert_kernel,
-        grid=(chips // BLOCKS,),
-        out_shape=jax.ShapeDtypeStruct(rows_in.shape, jnp.bfloat16),
-        in_specs=[
-            pl.BlockSpec((BLOCKS, 8, tokens), lambda i: (i, 0, 0)),
-            pl.BlockSpec((BLOCKS, tokens, width), lambda i: (i, 0, 0)),
-        ]
-        + [pl.BlockSpec(memory_space=pl.ANY)] * 4,
-        out_specs=pl.BlockSpec((BLOCKS, tokens, width), lambda i: (i, 0, 0)),
-        scratch_shapes=[
-            pltpu.VMEM((2, 3, width, FF), jnp.bfloat16),
-            pltpu.VMEM((BLOCKS, 2 * SLOTS, width), jnp.bfloat16),
-            pltpu.VMEM((BLOCKS, 2 * SLOTS, width), jnp.bfloat16),
-            pltpu.SemaphoreType.DMA((8,)),
-        ],
-        compiler_params=pltpu.CompilerParams(vmem_limit_bytes=60 << 20),
         name="experts",
-    )(tables, rows_in, *weights)
+    )(block, residual, tables, *weights)
 
 
 def slot_tables(routes, route_weights):
@@ -843,10 +832,7 @@
     residual = inputs + jnp.dot(attention, output_weight, preferred_element_type=jnp.float32)
     moe_in = rms_norm(residual, ffn_gain).astype(jnp.bfloat16)
 
-    rows_in, other_rest = gather_rows(moe_in, own_rest, 1)
-    parts = run_experts(tables, rows_in, own, own_rest, other, other_rest)
-    moe_sum = scatter_sums(parts, 2)
-    layer_out = (residual + moe_sum).astype(jnp.bfloat16)
+    layer_out = run_experts(moe_in, residual, tables, (own, own_rest, other), 1)
     return (layer_out, shard_keys, values_local)
 
 

time: 179 us -> 160 us (0.89)
  Pallas kernels: 157 us -> 135 us
  local copies, waits for them, and re-layouts: 1.87 us -> 6.72 us
  other arithmetic: 7.42 us -> 5.57 us
    pallas_call x3 -> x1, Pallas kernels: 98.7 us -> 82.5 us  [run_experts(): pl.pallas_call(experts_kernel, out_shape=jax.ShapeDtypeStruct(block.shape...]
    pallas_call x1, Pallas kernels: 58.4 us -> 52.4 us  [attend(): pl.pallas_call(attention_kernel, out_shape=(jax.ShapeDtypeStruct((rows, w...]
    unnamed x21 -> x30, local copies, waits for them, and re-layouts: 0.14 us -> 4.24 us
    convert_element_type x1 -> x0, other arithmetic: 1.96 us -> none  [shards(): layer_out = (residual + moe_sum).astype(jnp.bfloat16)]
where the time goes in v5:
time: 160 us; the launch traced here: 159 us
  Pallas kernels  135 us (84%)
  matrix products  10.8 us (7%)
  local copies, waits for them, and re-layouts  6.72 us (4%)
  other arithmetic  5.57 us (3%)
    pallas_call x1, Pallas kernels, run_experts(): pl.pallas_call(experts_kernel, out_shape=jax.ShapeDtypeStruct(block.shape...  82.5 us
    pallas_call x1, Pallas kernels, attend(): pl.pallas_call(attention_kernel, out_shape=(jax.ShapeDtypeStruct((rows, w...  52.4 us
    dot_general x1, matrix products, shards(): jnp.dot(normalized_input, query_weight, preferred_element_type=jnp.float32)  4.44 us
    unnamed x30, local copies, waits for them, and re-layouts  4.24 us
    dot_general x1, matrix products, shards(): jnp.dot(attention, output_weight, preferred_element_type=jnp.float32)  3.34 us

profile of v5, /device:TPU:0, one launch (start us, length us, event | category | flops | bytes accessed | tf_op | source)
XLA Modules:
  0.0 158.9 jit_solution(7120137129612295353)
XLA Ops:
  0.7 1.3 fusion
  2.0 0.1 pad.2.clone
  2.1 0.7 fusion.15
  2.8 0.6 broadcast_in_dim.20.starts
  3.4 0.7 fusion.3
  4.2 0.1 convolution_select_fusion
  4.3 0.8 select_reduce_fusion
  5.1 0.7 maximum_maximum_fusion.given
  5.8 0.1 multiply_cosine_fusion
  5.9 2.1 %convolution_convert_fusion = bf16[128,512]{1,0:T(8,128)(2,1)} fusion(bf16[1536,512]{1,0:T(8,128)(2,1)S(1)} %copy-done, bf16[128,1536]{1,0:T(8,128)(2,1)} %param.11, f32[1536]{0:T(1024)} %param.12, f32[128]{0:T(128)S(1)} %add_rsqrt_fusion.1), kind=kOutput, calls=%fused_computation.3 | convolution fusion | flops 202178560 | bytes 2103808 | tf_op jit(solution)/shard_map/dot_general | solution.py:816
  8.0 0.8 fusion.11
  8.9 0.1 copy.28
  9.0 0.8 slice_dynamic-update-slice_fusion.6
  9.9 0.8 slice_dynamic-update-slice_fusion.4
  10.6 0.8 slice_dynamic-update-slice_fusion.2
  11.4 0.8 slice_dynamic-update-slice_fusion.pairs
  12.2 4.4 %fusion.13 = f32[128,1536]{0,1:T(8,128)S(1)} fusion(bf16[1536,1536]{1,0:T(8,128)(2,1)} %param.13, bf16[128,1536]{1,0:T(8,128)(2,1)S(1)} %copy-done.2, f32[1536]{0:T(1024)} %param.12, f32[128]{0:T(128)} %copy-done.10), kind=kOutput, calls=%fused_computation.41 | convolution fusion | flops 604766208 | bytes 5904896 | tf_op jit(solution)/shard_map/dot_general | solution.py:800
  16.7 0.1 subtract_convert_fusion
  16.9 0.9 copy.32.queries
  17.8 52.4 %attention.1 = (bf16[128,1536]{1,0:T(8,128)(2,1)}, f32[16,8,128]{2,1,0:T(8,128)}, bf16[3,3,1536,128]{3,2,1,0:T(8,128)(2,1)}, bf16[3,1536,128]{2,1,0:T(8,128)(2,1)}) custom-call(bf16[128,1536]{1,0:T(8,128)(2,1)} %copy.32.queries, bf16[128,1024]{1,0:T(8,128)(2,1)} %copy-done.5, f32[8,128]{1,0:T(8,128)} %broadcast_in_dim.20.starts, ...), custom_call_target="tpu_custom_call" | custom-call | tf_op jit(solution)/shard_map/attention/pallas_call | solution.py:404
  70.2 3.3 %multiply_reduce_fusion = (f32[128]{0:T(128)S(1)}, f32[128,1536]{1,0:T(8,128)S(1)}) fusion(bf16[128,1536]{1,0:T(8,128)(2,1)} %get-tuple-element.7, bf16[1536,1536]{1,0:T(8,128)(2,1)} %param.16, bf16[128,1536]{1,0:T(8,128)(2,1)S(1)} %copy-done.2), kind=kOutput, calls=%fused_computation.9 | convolution fusion | flops 604766080 | bytes 6291968 | tf_op jit(solution)/shard_map/dot_general | solution.py:832
  73.6 1.0 multiply_convert_fusion.own
  74.6 82.5 %experts.1 = bf16[128,1536]{1,0:T(8,128)(2,1)} custom-call(bf16[128,1536]{1,0:T(8,128)(2,1)} %multiply_convert_fusion.own, f32[128,1536]{1,0:T(8,128)} %copy-done.1, f32[16,8,128]{2,1,0:T(8,128)} %get-tuple-element.8.tables, bf16[3,1536,128]{2,1,0:T(8,128)(2,1)} %bitcast.14, bf16[3,3,1536,128]{3,2,1,0:T(8,128)(2,1)} %get-tuple-element.9.rest, ...), custom_call_target="tpu_custom_call" | custom-call | tf_op jit(solution)/shard_map/experts/pallas_call | solution.py:744
  157.1 1.8 %copy.44 = bf16[128,1536]{1,0:T(8,128)(2,1)} copy(bf16[128,1536]{1,0:T(8,128)(2,1)} %experts.1) | data formatting | bytes 786432
  (33 shorter events, 0.2 us)
Async XLA Ops:
  0.6 5.3 %copy-start = (bf16[1536,512]{1,0:T(8,128)(2,1)S(1)}, bf16[1536,512]{1,0:T(8,128)(2,1)}, u32[]{:S(2)}) copy-start(bf16[1536,512]{1,0:T(8,128)(2,1)} %param.15) | copy-start | bytes 4718596
  0.6 7.4 %copy-start.2 = (bf16[128,1536]{1,0:T(8,128)(2,1)S(1)}, bf16[128,1536]{1,0:T(8,128)(2,1)}, u32[]{:S(2)}) copy-start(bf16[128,1536]{1,0:T(8,128)(2,1)} %param.11) | copy-start | bytes 1179652
  0.7 7.4 %copy-start.3 = (bf16[1536,512]{1,0:T(8,128)(2,1)S(1)}, bf16[1536,512]{1,0:T(8,128)(2,1)}, u32[]{:S(2)}) copy-start(bf16[1536,512]{1,0:T(8,128)(2,1)} %param.14) | copy-start | bytes 4718596
  0.7 7.3 %copy-start.8 = (f32[1536]{0:T(1024)S(1)}, f32[1536]{0:T(1024)}, u32[]{:S(2)}) copy-start(f32[1536]{0:T(1024)} %param.12) | copy-start | bytes 18436
  2.0 6.8 %copy-start.10 = (f32[128]{0:T(128)}, f32[128]{0:T(128)S(1)}, u32[]{:S(2)}) copy-start(f32[128]{0:T(128)S(1)} %add_rsqrt_fusion.1) | copy-start | bytes 1540
  5.9 2.9 %copy-start.6 = (f32[128,32]{0,1:T(8,128)}, f32[128,32]{0,1:T(8,128)S(1)}, u32[]{:S(2)}) copy-start(f32[128,32]{0,1:T(8,128)S(1)} %get-tuple-element.22) | copy-start | bytes 49156
  9.0 7.7 %copy-start.4 = (bf16[128,512]{1,0:T(8,128)(2,1)}, bf16[128,512]{1,0:T(8,128)(2,1)S(1)}, u32[]{:S(2)}) copy-start(bf16[128,512]{1,0:T(8,128)(2,1)S(1)} %copy.28) | copy-start | bytes 393220
  12.2 4.5 %copy-start.5 = (bf16[128,1024]{1,0:T(8,128)(2,1)}, bf16[128,1024]{1,0:T(8,128)(2,1)S(1)}, u32[]{:S(2)}) copy-start(bf16[128,1024]{1,0:T(8,128)(2,1)S(1)} %slice_dynamic-update-slice_fusion.pairs) | copy-start | bytes 786436
  12.2 4.5 %copy-start.7 = (f32[128,32]{0,1:T(8,128)S(1)}, f32[128,32]{0,1:T(8,128)}, u32[]{:S(2)}) copy-start(f32[128,32]{0,1:T(8,128)} %copy-done.6) | copy-start | bytes 49156
  70.2 3.4 %copy-start.9 = (f32[1536]{0:T(1024)S(1)}, f32[1536]{0:T(1024)}, u32[]{:S(2)}) copy-start(f32[1536]{0:T(1024)} %param.18) | copy-start | bytes 18436
  73.6 1.0 copy-start.1

commit v6 on v5

--- a/solution.py
+++ b/solution.py
@@ -19,25 +19,6 @@
 epsilon = 1e-05
 
 
-def rms_norm(values, gain):
-    mean_square = jnp.mean(values * values, axis=-1, keepdims=True)
-    return values * lax.rsqrt(mean_square + epsilon) * gain
-
-
-def rotary_embedding(heads_in, stream_offsets):
-    half = heads_in.shape[-1] // 2
-    freqs = 10000.0 ** (-jnp.arange(half, dtype=jnp.float32) / half)
-    angle = stream_offsets.astype(jnp.float32)[:, None] * freqs[None, :]
-    cosine = jnp.cos(angle)[:, None, :]
-    sine = jnp.sin(angle)[:, None, :]
-    first_half = heads_in[..., :half]
-    second_half = heads_in[..., half:]
-    return jnp.concatenate(
-        [first_half * cosine - second_half * sine, second_half * cosine + first_half * sine],
-        axis=-1,
-    )
-
-
 class Plane:
     def __init__(self):
         me = lax.axis_index("exp")
@@ -63,17 +44,18 @@
         return {"exp": (CHIPS - 1 - self.chip(0, 0)) * 2 + core}
 
 
-NEXT = ((0, 1), (0, -1), (1, 0), (-1, 0))
 OTHERS = tuple((dy, dx) for dy in range(SIDE) for dx in range(SIDE) if dy or dx)
 
 
-def greet(plane, places=NEXT, devices=()):
+def greet(plane):
     barrier = pltpu.get_barrier_semaphore()
-    for device in [plane.device(dy, dx) for dy, dx in places] + list(devices):
+    devices = [plane.device(dy, dx) for dy, dx in OTHERS]
+    devices += [plane.partner(), plane.mirror(False), plane.level(1), plane.level(-1)]
+    for device in devices:
         pl.semaphore_signal(
             barrier, inc=1, device_id=device, device_id_type=pl.DeviceIdType.MESH
         )
-    pl.semaphore_wait(barrier, len(places) + len(devices))
+    return lambda: pl.semaphore_wait(barrier, len(devices))
 
 
 def remote(src, dst, send, recv, device):
@@ -95,18 +77,16 @@
 ACROSS = (0, -1, 1, 2)
 
 
-def attention_kernel(
-    queries, pairs, starts, given, weights,
-    out, held, gathered, partners,
+def attention_section(
+    plane, weight_copy, project_keys, project_queries, make_tables,
+    queries, pairs, starts, given, out, held,
     near, store, asked, begin, packed, peak, total, bias, done,
-    give, take, x_send, x_recv, y_send, y_recv, q_send, q_recv, o_send, o_recv, w_send, w_recv, sems,
+    give, take, x_send, x_recv, y_send, y_recv, q_send, q_recv, o_send, o_recv, sems,
 ):
-    plane = Plane()
     core, odd = plane.core, lax.rem(plane.x, 2)
     here = plane.chip(0, 0)
     rows = queries.shape[0]
     friends = [plane.partner(), plane.mirror(True), plane.mirror(False)]
-    greet(plane, OTHERS, [friends[0], friends[2], plane.level(1), plane.level(-1)])
 
     mine = 2 * core + odd
     theirs = [2 * (1 - core) + odd, 2 * core + 1 - odd, 2 * (1 - core) + 1 - odd]
@@ -180,37 +160,17 @@
             plane.device(dy, dx),
         )
 
-    def slice_copy(n):
-        if n < 2:
-            return remote(
-                weights, gathered.at[n], w_send.at[n], w_recv.at[n], plane.level((1, -1)[n])
-            )
-        if n < 4:
-            size = weights.shape[1] // 2
-            part = pl.ds((n - 2) * size, size)
-            return remote(
-                gathered.at[n - 2, :, part],
-                gathered.at[2, :, part],
-                w_send.at[n],
-                w_recv.at[n],
-                plane.level((1, -1)[n - 2]),
-            )
-        return remote(weights, partners, w_send.at[n], w_recv.at[n], friends[0])
-
     own_asked = pltpu.make_async_copy(
         queries.at[:, lanes(mine, PAIR_WIDTH)], asked.at[core], sems.at[4]
     )
     own_begin = pltpu.make_async_copy(starts, begin.at[core], sems.at[5])
     own_table = pltpu.make_async_copy(given.at[here], held.at[here], sems.at[6])
 
+    project_keys()
     swap.start()
-    for n in (0, 1, 4):
-        slice_copy(n).start()
     for h in (0, 1):
         if h == 1:
-            ask(0).start()
-            tell(0).start()
-            own_asked.start()
+            make_tables()
             own_begin.start()
             own_table.start()
             swap.wait_recv()
@@ -219,6 +179,10 @@
             across(h, n).start()
         along(h, 0, 0).start()
         along(h, 0, 1).start()
+    project_queries()
+    own_asked.start()
+    ask(0).start()
+    tell(0).start()
     for n in (1, 2):
         ask(n).start()
         tell(n).start()
@@ -310,8 +274,9 @@
         @pl.when(step == 2)
         def _():
             for n in (0, 1):
-                slice_copy(n).wait_recv()
-                slice_copy(n + 2).start()
+                weight_copy(n, True).wait_recv()
+                weight_copy(2 + n).start()
+                weight_copy(5 + n).start()
 
         @pl.when(step == 3)
         def _():
@@ -392,55 +357,6 @@
     for n in range(3):
         reply(n, True).wait_recv()
         reply(n).wait_send()
-    for n in (2, 3, 4):
-        slice_copy(n).wait_recv()
-    for n in range(5):
-        slice_copy(n).wait_send()
-
-
-def attend(queries, pairs, starts, tables, weights, collective_id):
-    rows, width = queries.shape
-    dma = pltpu.SemaphoreType.DMA
-    return pl.pallas_call(
-        attention_kernel,
-        out_shape=(
-            jax.ShapeDtypeStruct((rows, width), jnp.bfloat16),
-            jax.ShapeDtypeStruct(tables.shape, tables.dtype),
-            jax.ShapeDtypeStruct((3, *weights.shape), weights.dtype),
-            jax.ShapeDtypeStruct(weights.shape, weights.dtype),
-        ),
-        in_specs=[pl.BlockSpec(memory_space=pltpu.VMEM)] * 4 + [pl.BlockSpec(memory_space=pl.ANY)],
-        out_specs=(pl.BlockSpec(memory_space=pltpu.VMEM),) * 2
-        + (pl.BlockSpec(memory_space=pl.ANY),) * 2,
-        scratch_shapes=[
-            pltpu.VMEM((rows, 512), jnp.bfloat16),
-            pltpu.VMEM((CHIPS, 2 * rows, 256), jnp.bfloat16),
-            pltpu.VMEM((4, rows, PAIR_WIDTH), jnp.bfloat16),
-            pltpu.VMEM((4, 8, rows), jnp.float32),
-            pltpu.VMEM((2, 2 * PAIR * rows, 128), jnp.bfloat16),
-            pltpu.VMEM((2, 2 * PAIR * rows, 128), jnp.float32),
-            pltpu.VMEM((2, 2 * PAIR * rows, 128), jnp.float32),
-            pltpu.VMEM((2 * rows, KEYS), jnp.float32),
-            pltpu.VMEM((4, rows, PAIR_WIDTH), jnp.bfloat16),
-            dma((len(OTHERS),)),
-            dma((len(OTHERS),)),
-            dma((6,)),
-            dma((6,)),
-            dma((32,)),
-            dma((32,)),
-            dma((6,)),
-            dma((6,)),
-            dma((3,)),
-            dma((3,)),
-            dma((5,)),
-            dma((5,)),
-            dma((8,)),
-        ],
-        compiler_params=pltpu.CompilerParams(
-            collective_id=collective_id, has_side_effects=True, vmem_limit_bytes=60 << 20
-        ),
-        name="attention",
-    )(queries, pairs, starts, tables, weights)
 
 
 BLOCKS = 4
@@ -454,15 +370,11 @@
 ENDS = (-1, 1)
 
 
-def experts_kernel(
-    own, residual, tables, first, rest, other,
-    out,
+def experts_section(
+    plane, weight_copy, own, residual, tables, out,
     rows_in, sums, weights, picked, made, hold_q, hold_r, hold_p, hold_d,
-    g_send, g_recv, q_send, q_recv, r_send, r_recv, p_send, p_recv, d_send, d_recv,
-    w_send, w_recv, load_sems,
+    g_send, g_recv, q_send, q_recv, r_send, r_recv, p_send, p_recv, d_send, d_recv, sem,
 ):
-    plane = Plane()
-    core = plane.core
     rows, width = own.shape
     part_rows = rows // 2
     even = lax.rem(plane.y + plane.x, 2) == 0
@@ -478,8 +390,6 @@
 
     def part(n):
         return pl.ds(n * part_rows, part_rows)
-
-    greet(plane, NEXT, [plane.partner()])
 
     def gather(k, src, dst, to):
         return remote(src, dst, g_send.at[k], g_recv.at[k], to)
@@ -516,34 +426,15 @@
         ref = rows_in.at[place(at), part(n)]
         return gather(4 + group * 8 + j * 4 + 2 + n, ref, ref, to)
 
-    def lanes(r):
-        return pl.ds(r * 128, 128)
-
-    def loads():
-        sources = [(first, core, 0), (other, 1 - core, 0)]
-        sources += [(rest.at[r], core, r + 1) for r in range(3)]
-        for n, (src, e, r) in enumerate(sources):
-            yield pltpu.make_async_copy(src, weights.at[e, :, :, lanes(r)], load_sems.at[n])
-        yield pltpu.make_async_copy(own, rows_in.at[place((0, 0))], load_sems.at[5])
-
-    def swap(r, incoming=False):
-        e = 1 - core if incoming else core
-        return remote(
-            rest.at[r],
-            weights.at[e, :, :, lanes(r + 1)],
-            w_send.at[r],
-            w_recv.at[r],
-            plane.partner(),
-        )
-
+    mine = pltpu.make_async_copy(own, rows_in.at[place((0, 0))], sem)
     for n in (0, 1):
         emit(n).start()
-    for r in range(3):
-        swap(r).start()
     for n in (0, 1):
         spread(0, 0, n).start()
-    for load in loads():
-        load.start()
+    mine.start()
+    for n in (2, 3):
+        weight_copy(n, True).wait_recv()
+    weight_copy(7).start()
     for j in (0, 1):
         emit(j, True).wait_recv()
         pass_on(j).start()
@@ -553,10 +444,9 @@
         pass_on(n, True).wait_recv()
     for n in (0, 1):
         spread(0, 1, n).start()
-    for load in loads():
-        load.wait()
-    for r in range(3):
-        swap(r, True).wait_recv()
+    mine.wait()
+    for n in (4, 5, 6, 7):
+        weight_copy(n, True).wait_recv()
 
     def far(group, j):
         return (TWO[j], 2) if group == 0 else (2, ENDS[j])
@@ -725,8 +615,8 @@
         give_across(n).wait_send()
         for late in (0, 1):
             give_back(n, late).wait_send()
-    for r in range(3):
-        swap(r).wait_send()
+    for n in range(8):
+        weight_copy(n).wait_send()
     for group, j in PAIRS:
         for n in (0, 1):
             spread(group, j, n).wait_send()
@@ -736,46 +626,235 @@
                 give_near(group, j, n, late).wait_send()
 
 
-def run_experts(block, residual, tables, weights, collective_id):
-    rows, width = block.shape
+def normed(values, gain):
+    mean_square = jnp.mean(values * values, axis=1, keepdims=True)
+    return (values * lax.rsqrt(mean_square + epsilon) * gain).astype(jnp.bfloat16)
+
+
+def layer_kernel(
+    hidden, attn_gain, wq, wk, wv, wo, prompt_start, cosine, sine, ffn_gain, routes, route_weights,
+    first,
+    out, key_cache, value_cache,
+    query_w, key_w, value_w, output_w, own_in, residual,
+    queries, pairs, starts, given, attention, tables,
+    near, store, asked, begin, packed, peak, total, bias, done,
+    rows_in, sums, weights, picked, made, hold_q, hold_r, hold_p, hold_d,
+    *sems,
+):
+    attention_sems, expert_sems, (w_send, w_recv, load_sems, row_sem) = (
+        sems[:11],
+        sems[11:21],
+        sems[21:],
+    )
+    plane = Plane()
+    core = plane.core
+    rows, width = hidden.shape
+    arrived = greet(plane)
+
+    def lanes(r):
+        return pl.ds(r * 128, 128)
+
+    def weight_copy(n, incoming=False):
+        half = width // 2
+        e = 1 - core if incoming and n >= 4 else core
+        if n < 2:
+            src, dst = first, weights.at[e, :, :, lanes(1 + n)]
+            to = plane.level((1, -1)[n])
+        elif n < 4:
+            span = pl.ds((n - 2) * half, half)
+            src = weights.at[e, :, span, lanes(n - 1)]
+            dst = weights.at[e, :, span, lanes(3)]
+            to = plane.level((1, -1)[n - 2])
+        else:
+            dst = weights.at[e, :, :, lanes(n - 4)]
+            src = first if n == 4 else dst
+            to = plane.partner()
+        return remote(src, dst, w_send.at[n], w_recv.at[n], to)
+
+    loads = [
+        pltpu.make_async_copy(src, dst, load_sems.at[n])
+        for n, (src, dst) in enumerate(
+            (
+                (wk, key_w),
+                (wv, value_w),
+                (wq, query_w),
+                (wo, output_w),
+                (first, weights.at[core, :, :, lanes(0)]),
+            )
+        )
+    ]
+    for load in loads:
+        load.start()
+    own_in[...] = normed(hidden[...].astype(jnp.float32), attn_gain[...])
+    arrived()
+    for n in (0, 1, 4):
+        weight_copy(n).start()
+
+    lane = lax.broadcasted_iota(jnp.int32, (rows, 128), 1)
+    first_half = lax.rem(lane, HEAD_SIZE) < HEAD_SIZE // 2
+
+    def rotated(tile):
+        other = jnp.where(
+            first_half,
+            pltpu.roll(tile, 128 - HEAD_SIZE // 2, axis=1),
+            pltpu.roll(tile, HEAD_SIZE // 2, axis=1),
+        )
+        return (tile * cosine[...] + other * sine[...]).astype(jnp.bfloat16)
+
+    def project_keys():
+        starts[...] = jnp.broadcast_to(prompt_start[...].astype(jnp.float32), starts.shape)
+        loads[0].wait()
+        keys = jnp.dot(own_in[...], key_w[...], preferred_element_type=jnp.float32)
+        loads[1].wait()
+        values = jnp.dot(
+            own_in[...], value_w[...], preferred_element_type=jnp.float32
+        ).astype(jnp.bfloat16)
+        value_cache[...] = values
+        for p in range(KEY_VALUE_HEADS // 2):
+            at = slice(p * 128, (p + 1) * 128)
+            tile = rotated(keys[:, at])
+            key_cache[:, at] = tile
+            pairs[:, p * 256 : p * 256 + 128] = tile
+            pairs[:, p * 256 + 128 : (p + 1) * 256] = values[:, at]
+
+    def project_queries():
+        loads[2].wait()
+        for c in range(3):
+            part = jnp.dot(
+                own_in[...],
+                query_w[:, c * 512 : (c + 1) * 512],
+                preferred_element_type=jnp.float32,
+            )
+            for p in range(4):
+                at = c * 512 + p * 128
+                queries[:, at : at + 128] = rotated(part[:, p * 128 : (p + 1) * 128])
+
+    def make_tables():
+        expert = lax.broadcasted_iota(jnp.int32, (EXPERTS, rows), 0)
+        gains = jnp.zeros((EXPERTS, rows), jnp.float32)
+        named = jnp.zeros((EXPERTS, rows), jnp.float32)
+        for j in range(TOP):
+            hit = routes[j : j + 1, :] == expert
+            gains = gains + jnp.where(hit, route_weights[j : j + 1, :], 0.0)
+            named = named + jnp.where(hit, 1.0, 0.0)
+        earlier = lax.broadcasted_iota(jnp.int32, (rows, rows), 0) < lax.broadcasted_iota(
+            jnp.int32, (rows, rows), 1
+        )
+        ranks = jnp.dot(
+            named.astype(jnp.bfloat16),
+            jnp.where(earlier, 1.0, 0.0).astype(jnp.bfloat16),
+            preferred_element_type=jnp.float32,
+        )
+        ranks = jnp.where(named > 0.0, ranks, -1.0)
+        given[...] = jnp.zeros_like(given)
+        for c in range(CHIPS):
+            given[c, 0:2, :] = gains[2 * c : 2 * c + 2, :]
+            given[c, 2:4, :] = ranks[2 * c : 2 * c + 2, :]
+
+    attention_section(
+        plane, weight_copy, project_keys, project_queries, make_tables,
+        queries, pairs, starts, given, attention, tables,
+        near, store, asked, begin, packed, peak, total, bias, done,
+        *attention_sems,
+    )
+
+    loads[3].wait()
+    for c in range(3):
+        at = slice(c * 512, (c + 1) * 512)
+        residual[:, at] = hidden[:, at].astype(jnp.float32) + jnp.dot(
+            attention[...], output_w[:, at], preferred_element_type=jnp.float32
+        )
+    own_in[...] = normed(residual[...], ffn_gain[...])
+    loads[4].wait()
+
+    experts_section(
+        plane, weight_copy, own_in, residual, tables, out,
+        rows_in, sums, weights, picked, made, hold_q, hold_r, hold_p, hold_d,
+        *expert_sems, row_sem,
+    )
+
+
+def run_layer(hidden, attn_gain, wq, wk, wv, wo, starts, trig, ffn_gain, routes, gains, first):
+    rows, width = hidden.shape
+    cache = wk.shape[1]
     dma = pltpu.SemaphoreType.DMA
     vmem = pl.BlockSpec(memory_space=pltpu.VMEM)
-    pairs = [dma((n,)) for n in (20, 8, 16, 2, 4, 3) for _ in (0, 1)]
+    hbm = pl.BlockSpec(memory_space=pl.ANY)
+
+    def brief(*shape):
+        return pltpu.VMEM(shape, jnp.bfloat16)
+
+    def full(*shape):
+        return pltpu.VMEM(shape, jnp.float32)
+
+    others = len(OTHERS)
+    counts = (others, 6, 32, 6, 3)
+    attention_sems = [dma((n,)) for n in counts for _ in (0, 1)] + [dma((8,))]
+    expert_sems = [dma((n,)) for n in (20, 8, 16, 2, 4) for _ in (0, 1)]
+    both = 2 * PAIR * rows
     return pl.pallas_call(
-        experts_kernel,
-        out_shape=jax.ShapeDtypeStruct(block.shape, block.dtype),
-        in_specs=[vmem] * 3 + [pl.BlockSpec(memory_space=pl.ANY)] * 3,
-        out_specs=vmem,
+        layer_kernel,
+        out_shape=(
+            jax.ShapeDtypeStruct((rows, width), jnp.bfloat16),
+            jax.ShapeDtypeStruct((rows, cache), jnp.bfloat16),
+            jax.ShapeDtypeStruct((rows, cache), jnp.bfloat16),
+        ),
+        in_specs=[vmem, vmem, hbm, hbm, hbm, hbm] + [vmem] * 6 + [hbm],
+        out_specs=(vmem,) * 3,
         scratch_shapes=[
-            pltpu.VMEM((CHIPS, rows, width), jnp.bfloat16),
-            pltpu.VMEM((CHIPS, rows, width), jnp.bfloat16),
-            pltpu.VMEM((2, 3, width, FF), jnp.bfloat16),
-            pltpu.VMEM((BLOCKS, 2 * SLOTS, width), jnp.bfloat16),
-            pltpu.VMEM((BLOCKS, 2 * SLOTS, width), jnp.bfloat16),
-            pltpu.VMEM((8, rows // 2, width), jnp.bfloat16),
-            pltpu.VMEM((8, rows, width), jnp.bfloat16),
-            pltpu.VMEM((2, rows // 2, width), jnp.bfloat16),
-            pltpu.VMEM((2, rows, width), jnp.bfloat16),
-            *pairs,
-            dma((6,)),
+            brief(*wq.shape),
+            brief(*wk.shape),
+            brief(*wv.shape),
+            brief(*wo.shape),
+            brief(rows, width),
+            full(rows, width),
+            brief(rows, width),
+            brief(rows, 2 * cache),
+            full(8, rows),
+            full(CHIPS, 8, rows),
+            brief(rows, width),
+            full(CHIPS, 8, rows),
+            brief(rows, 512),
+            brief(CHIPS, 2 * rows, 256),
+            brief(4, rows, PAIR_WIDTH),
+            full(4, 8, rows),
+            brief(2, both, 128),
+            full(2, both, 128),
+            full(2, both, 128),
+            full(2 * rows, KEYS),
+            brief(4, rows, PAIR_WIDTH),
+            brief(CHIPS, rows, width),
+            brief(CHIPS, rows, width),
+            brief(2, 3, width, FF),
+            brief(BLOCKS, 2 * SLOTS, width),
+            brief(BLOCKS, 2 * SLOTS, width),
+            brief(8, rows // 2, width),
+            brief(8, rows, width),
+            brief(2, rows // 2, width),
+            brief(2, rows, width),
+            *attention_sems,
+            *expert_sems,
+            dma((8,)),
+            dma((8,)),
+            dma((5,)),
+            dma,
         ],
         compiler_params=pltpu.CompilerParams(
-            collective_id=collective_id, has_side_effects=True, vmem_limit_bytes=60 << 20
+            collective_id=0, has_side_effects=True, vmem_limit_bytes=63 << 20
         ),
-        name="experts",
-    )(block, residual, tables, *weights)
-
-
-def slot_tables(routes, route_weights):
-    tokens = routes.shape[0]
-    hit = routes[None] == jnp.arange(EXPERTS, dtype=jnp.int32)[:, None, None]
-    gains = jnp.sum(jnp.where(hit, route_weights[None], 0.0), axis=2)
-    named = jnp.any(hit, axis=2)
-    earlier = jnp.triu(jnp.ones((tokens, tokens), jnp.bfloat16), 1)
-    ranks = jnp.dot(named.astype(jnp.bfloat16), earlier, preferred_element_type=jnp.float32)
-    ranks = jnp.where(named, ranks, -1.0)
-    pairs = [t.reshape(CHIPS, 2, tokens) for t in (gains, ranks)]
-    return jnp.concatenate(pairs + [jnp.zeros((CHIPS, 4, tokens), jnp.float32)], axis=1)
+        name="layer",
+    )(
+        hidden, attn_gain, wq, wk, wv, wo, starts, *trig, ffn_gain, routes, gains, first
+    )
+
+
+def rotation_tables(offsets):
+    half = HEAD_SIZE // 2
+    freqs = 10000.0 ** (-jnp.arange(half, dtype=jnp.float32) / half)
+    freqs = jnp.tile(freqs, 128 // half)
+    sign = jnp.where(jnp.arange(128) % HEAD_SIZE < half, -1.0, 1.0)
+    angle = offsets.astype(jnp.float32)[:, None] * freqs[None, :]
+    return jnp.cos(angle), jnp.sin(angle) * sign[None, :]
 
 
 def shards(
@@ -791,49 +870,22 @@
     route_weights,
     expert_weights,
 ):
-    total_row_count = hidden.shape[0]
-    lane_index = lax.axis_index("exp")
-    positions = lane_index * total_row_count + jnp.arange(total_row_count, dtype=jnp.int32)
-    stream_offsets = positions - prompt_start
-    inputs = hidden.astype(jnp.float32)
-    normalized_input = rms_norm(inputs, attn_gain).astype(jnp.bfloat16)
-    query_rows_all = jnp.dot(
-        normalized_input, query_weight, preferred_element_type=jnp.float32
-    ).reshape(total_row_count, QUERY_HEADS, HEAD_SIZE)
-    query_rows_all = (
-        rotary_embedding(query_rows_all, stream_offsets)
-        .astype(jnp.bfloat16)
-        .reshape(total_row_count, QUERY_HEADS * HEAD_SIZE)
+    rows = hidden.shape[0]
+    positions = lax.axis_index("exp") * rows + jnp.arange(rows, dtype=jnp.int32)
+    return run_layer(
+        hidden,
+        attn_gain[None],
+        query_weight,
+        key_matrix,
+        value_matrix,
+        output_weight,
+        prompt_start[None],
+        rotation_tables(positions - prompt_start),
+        ffn_gain[None],
+        routes.T,
+        route_weights.T,
+        expert_weights[0],
     )
-    shard_keys = jnp.dot(normalized_input, key_matrix, preferred_element_type=jnp.float32).reshape(
-        total_row_count, KEY_VALUE_HEADS, HEAD_SIZE
-    )
-    shard_keys = (
-        rotary_embedding(shard_keys, stream_offsets)
-        .astype(jnp.bfloat16)
-        .reshape(total_row_count, KEY_VALUE_HEADS * HEAD_SIZE)
-    )
-    values_local = jnp.dot(
-        normalized_input, value_matrix, preferred_element_type=jnp.float32
-    ).astype(jnp.bfloat16)
-    pairs = jnp.concatenate(
-        [
-            side[:, p * 128 : (p + 1) * 128]
-            for p in range(KEY_VALUE_HEADS // 2)
-            for side in (shard_keys, values_local)
-        ],
-        axis=1,
-    )
-    starts = jnp.broadcast_to(prompt_start.astype(jnp.float32)[None], (8, total_row_count))
-    own = expert_weights[0]
-    attention, tables, own_rest, other = attend(
-        query_rows_all, pairs, starts, slot_tables(routes, route_weights), own, 0
-    )
-    residual = inputs + jnp.dot(attention, output_weight, preferred_element_type=jnp.float32)
-    moe_in = rms_norm(residual, ffn_gain).astype(jnp.bfloat16)
-
-    layer_out = run_experts(moe_in, residual, tables, (own, own_rest, other), 1)
-    return (layer_out, shard_keys, values_local)
 
 
 def solution(mesh):

time: 160 us -> 143 us (0.89)
  matrix products: 10.8 us -> 0 us
  other arithmetic: 5.57 us -> 1.64 us
  Pallas kernels: 135 us -> 133 us
    dot_general x5 -> x0, matrix products: 10.8 us -> none  [the longest x1 4.44 us: shards(): jnp.dot(normalized_input, query_weight, preferred_element_type=jnp.float32)]
    pallas_call x2 -> x1, Pallas kernels: 135 us -> 133 us  [run_layer(): pl.pallas_call(layer_kernel, out_shape=(jax.ShapeDtypeStruct((rows, width...]
    reduce_sum x2 -> x0, other arithmetic: 2.06 us -> none  [the longest x1 1.31 us: rms_norm(): mean_square = jnp.mean(values * values, axis=-1, keepdims=True)]
    broadcast_in_dim x2, local copies, waits for them, and re-layouts: 0.59 us -> 2.58 us  [the longest x1 1.3 us: shards(): attn_gain[None]]
    unnamed x30 -> x3, local copies, waits for them, and re-layouts: 4.24 us -> 4.9 us
where the time goes in v6:
time: 143 us
  Pallas kernels  133 us (93%)
  local copies, waits for them, and re-layouts  7.56 us (5%)
  other arithmetic  1.64 us (1%)
    pallas_call x1, Pallas kernels, run_layer(): pl.pallas_call(layer_kernel, out_shape=(jax.ShapeDtypeStruct((rows, width...  133 us
    unnamed x3, local copies, waits for them, and re-layouts  4.9 us

profile of v6, /device:TPU:0, one launch (start us, length us, event | category | flops | bytes accessed | tf_op | source)
XLA Modules:
  0.0 142.6 jit_solution(6941643637731251040)
XLA Ops:
  0.6 0.7 subtract_convert_fusion
  1.3 0.1 mul.28
  1.4 1.3 broadcast_in_dim.19.attn_gain
  2.7 1.3 broadcast_in_dim.23.ffn_gain
  4.0 1.0 fusion
  5.0 132.8 %layer.1 = (bf16[128,1536]{1,0:T(8,128)(2,1)}, bf16[128,512]{1,0:T(8,128)(2,1)}, bf16[128,512]{1,0:T(8,128)(2,1)}) custom-call(bf16[128,1536]{1,0:T(8,128)(2,1)} %hidden.1, f32[1,1536]{1,0:T(1,128)} %broadcast_in_dim.19.attn_gain, bf16[1536,1536]{1,0:T(8,128)(2,1)} %wq.1, bf16[1536,512]{1,0:T(8,128)(2,1)} %wk.1, bf16[1536,512]{1,0:T(8,128)(2,1)} %wv.1, ...), custom_call_target="tpu_custom_call" | custom-call | tf_op jit(solution)/shard_map/layer/pallas_call | solution.py:795
  137.7 1.8 %copy.17 = bf16[128,1536]{1,0:T(8,128)(2,1)} copy(bf16[128,1536]{1,0:T(8,128)(2,1)} %get-tuple-element.8) | data formatting | bytes 786432
  139.5 1.6 %copy.18 = bf16[128,512]{1,0:T(8,128)(2,1)} copy(bf16[128,512]{1,0:T(8,128)(2,1)} %get-tuple-element.9) | data formatting | bytes 262144
  141.1 1.6 %copy.19 = bf16[128,512]{1,0:T(8,128)(2,1)} copy(bf16[128,512]{1,0:T(8,128)(2,1)} %get-tuple-element.10) | data formatting | bytes 262144
  (3 shorter events, 0.0 us)

commit v7 on v6

--- a/solution.py
+++ b/solution.py
@@ -39,18 +39,26 @@
     def partner(self):
         return {"exp": self.chip(0, 0) * 2 + 1 - self.core}
 
-    def mirror(self, same_core):
-        core = self.core if same_core else 1 - self.core
-        return {"exp": (CHIPS - 1 - self.chip(0, 0)) * 2 + core}
-
-
+    def friend(self, dx, dc):
+        x = lax.rem(self.x + dx + SIDE, SIDE)
+        y = self.y if dx % 2 == 0 else SIDE - 1 - self.y
+        core = 1 - self.core if dc else self.core
+        return y * SIDE + x, core, 2 * x + core
+
+    def friend_device(self, dx, dc):
+        chip, core, _ = self.friend(dx, dc)
+        return {"exp": chip * 2 + core}
+
+
+FRIENDS = tuple((dx, dc) for dx in range(SIDE) for dc in (0, 1) if dx or dc)
 OTHERS = tuple((dy, dx) for dy in range(SIDE) for dx in range(SIDE) if dy or dx)
 
 
 def greet(plane):
     barrier = pltpu.get_barrier_semaphore()
     devices = [plane.device(dy, dx) for dy, dx in OTHERS]
-    devices += [plane.partner(), plane.mirror(False), plane.level(1), plane.level(-1)]
+    devices += [plane.friend_device(dx, 1) for dx in range(SIDE)]
+    devices += [plane.level(1), plane.level(-1)]
     for device in devices:
         pl.semaphore_signal(
             barrier, inc=1, device_id=device, device_id_type=pl.DeviceIdType.MESH
@@ -70,8 +78,8 @@
 
 
 KEYS = 512
-PAIR = 6
-PAIR_WIDTH = PAIR * HEAD_SIZE
+HEADS = QUERY_HEADS // KEY_VALUE_HEADS
+ASK = 256
 LOW = -1e30
 SCALE = HEAD_SIZE**-0.5 * 1.4426950408889634
 ACROSS = (0, -1, 1, 2)
@@ -80,30 +88,26 @@
 def attention_section(
     plane, weight_copy, project_keys, project_queries, make_tables,
     queries, pairs, starts, given, out, held,
-    near, store, asked, begin, packed, peak, total, bias, done,
+    near, store, asked, begin, packed, peak, total, bias, done, replies,
     give, take, x_send, x_recv, y_send, y_recv, q_send, q_recv, o_send, o_recv, sems,
 ):
-    core, odd = plane.core, lax.rem(plane.x, 2)
+    core = plane.core
     here = plane.chip(0, 0)
     rows = queries.shape[0]
-    friends = [plane.partner(), plane.mirror(True), plane.mirror(False)]
-
-    mine = 2 * core + odd
-    theirs = [2 * (1 - core) + odd, 2 * core + 1 - odd, 2 * (1 - core) + 1 - odd]
-    slots = [core, 2 + core, 2 + core]
-    from_slots = [1 - core, 2 + core, 2 + 1 - core]
+    mine = 2 * plane.x + core
 
     def lanes(at, size):
         return pl.ds(pl.multiple_of(at * size, size), size)
 
     swap = remote(
-        pairs.at[:, lanes(1 - core, 512)], near, sems.at[0], sems.at[1], friends[0]
+        pairs.at[:, lanes(1 - core, 512)], near, sems.at[0], sems.at[1], plane.partner()
     )
 
-    def source(h, parity):
+    def source(h, dx):
+        x = lax.rem(plane.x + dx + SIDE, SIDE)
         if h == 0:
-            return pairs.at[:, lanes(2 * core + parity, 256)]
-        return near.at[:, lanes(parity, 256)]
+            return pairs.at[:, lanes(SIDE * core + x, 128)]
+        return near.at[:, lanes(x, 128)]
 
     def slot(h, dy, dx, part=None):
         low = (core if h == 0 else 1 - core) * rows
@@ -114,12 +118,12 @@
         return store.at[plane.chip(dy, dx), pl.ds(pl.multiple_of(low, size), size)]
 
     def keep(h):
-        return pltpu.make_async_copy(source(h, odd), slot(h, 0, 0), sems.at[2 + h])
+        return pltpu.make_async_copy(source(h, 0), slot(h, 0, 0), sems.at[2 + h])
 
     def across(h, n, incoming=False):
         dx = (1, -1, 2)[n]
         return remote(
-            source(h, odd if n == 2 else 1 - odd),
+            source(h, dx),
             slot(h, 0, -dx if incoming else 0),
             x_send.at[3 * h + n],
             x_recv.at[3 * h + n],
@@ -130,25 +134,36 @@
         dx = ACROSS[i]
         at, part, dy = ((0, None, 1), (0, None, -1), (-1, 0, 1), (1, 1, -1))[n]
         place = slot(h, at - dy if incoming else at, dx, part)
-        src = source(h, odd) if (i == 0 and n < 2) else place
+        src = source(h, 0) if (i == 0 and n < 2) else place
         if i == 0 and n < 2 and not incoming:
             place = slot(h, 0, 0)
         k = (h * 4 + i) * 4 + n
         return remote(src, place, y_send.at[k], y_recv.at[k], plane.device(dy, 0))
 
+    def other(n, incoming):
+        dx, dc = FRIENDS[n]
+        return plane.friend(-dx if incoming else dx, dc)[2]
+
+    def asking(head):
+        return pl.ds(pl.multiple_of(lax.div(3 * head, 2) * 128, 128), ASK)
+
     def ask(n, incoming=False):
-        at = from_slots[n] if incoming else slots[n]
         return remote(
-            queries.at[:, lanes(theirs[n], PAIR_WIDTH)],
-            asked.at[at],
+            queries.at[:, asking(other(n, False))],
+            asked.at[other(n, True) if incoming else mine],
             q_send.at[n],
             q_recv.at[n],
-            friends[n],
+            plane.friend_device(*FRIENDS[n]),
         )
 
     def tell(n, incoming=False):
-        at = from_slots[n] if incoming else slots[n]
-        return remote(starts, begin.at[at], q_send.at[3 + n], q_recv.at[3 + n], friends[n])
+        return remote(
+            starts,
+            begin.at[other(n, True) if incoming else mine],
+            q_send.at[len(FRIENDS) + n],
+            q_recv.at[len(FRIENDS) + n],
+            plane.friend_device(*FRIENDS[n]),
+        )
 
     def table(n, incoming=False):
         dy, dx = OTHERS[n]
@@ -161,9 +176,9 @@
         )
 
     own_asked = pltpu.make_async_copy(
-        queries.at[:, lanes(mine, PAIR_WIDTH)], asked.at[core], sems.at[4]
+        queries.at[:, asking(mine)], asked.at[mine], sems.at[4]
     )
-    own_begin = pltpu.make_async_copy(starts, begin.at[core], sems.at[5])
+    own_begin = pltpu.make_async_copy(starts, begin.at[mine], sems.at[5])
     own_table = pltpu.make_async_copy(given.at[here], held.at[here], sems.at[6])
 
     project_keys()
@@ -181,9 +196,7 @@
         along(h, 0, 1).start()
     project_queries()
     own_asked.start()
-    ask(0).start()
-    tell(0).start()
-    for n in (1, 2):
+    for n in range(len(FRIENDS)):
         ask(n).start()
         tell(n).start()
     for n in range(3):
@@ -197,34 +210,42 @@
 
     own_asked.wait()
     own_begin.wait()
-    for n in range(3):
+    for n in range(len(FRIENDS)):
         ask(n, True).wait_recv()
         tell(n, True).wait_recv()
     for h in (0, 1):
         keep(h).wait()
 
     lane = lax.broadcasted_iota(jnp.int32, (rows, 128), 1)
-    low_half = lane < HEAD_SIZE
-    for which in (0, 1):
+    low = lane < HEAD_SIZE
+    upper = core == 1
+    for which in range(SIDE):
         for side in (0, 1):
-            for n in range(PAIR):
-                tile = asked[2 * which + side, :, (n // 2) * 128 : (n // 2 + 1) * 128].astype(
-                    jnp.float32
-                )
-                group = n // 3
-                if n % 2 != group:
-                    tile = pltpu.roll(tile, HEAD_SIZE, axis=1)
-                own_half = low_half if group == 0 else jnp.logical_not(low_half)
+            tiles = [
+                asked[2 * which + side, :, i * 128 : (i + 1) * 128].astype(jnp.float32)
+                for i in (0, 1)
+            ]
+            turned = [pltpu.roll(tile, HEAD_SIZE, axis=1) for tile in tiles]
+            heads = (
+                jnp.where(upper, turned[0], tiles[0]),
+                jnp.where(upper, tiles[1], turned[0]),
+                jnp.where(upper, turned[1], tiles[1]),
+            )
+            for n in range(HEADS):
                 at = (n * 2 + side) * rows
-                packed[which, at : at + rows, :] = jnp.where(own_half, tile, 0.0).astype(
+                packed[which, at : at + rows, :] = jnp.where(low, heads[n], 0.0).astype(
                     jnp.bfloat16
                 )
     peak[...] = jnp.full_like(peak, LOW)
     total[...] = jnp.zeros_like(total)
-    half = PAIR * rows
+    both = 2 * HEADS * rows
+
+    def member(which):
+        flip = lax.rem(plane.x + which, 2)
+        return jnp.where(flip == 0, plane.y, SIDE - 1 - plane.y) * SIDE + which
 
     def visit(which, chip):
-        stream_chip = jnp.where(which == 0, here, CHIPS - 1 - here)
+        stream_chip = member(which)
         at = chip * (2 * rows)
         for side in (0, 1):
             first = jnp.broadcast_to(begin[2 * which + side, 0:1, :], (rows, rows)).T
@@ -236,31 +257,22 @@
             bias[side * rows : (side + 1) * rows, :] = jnp.where(
                 (key_pos >= first) & (key_pos <= own_pos), 0.0, LOW
             )
-        tile = store[pl.ds(chip, 2)].reshape(KEYS, 256)
-        key, value = tile[:, :128], tile[:, 128:]
-        key_lane = lax.broadcasted_iota(jnp.int32, (KEYS, 128), 1)
-        for group in (0, 1):
-            span = pl.ds(group * half, half)
-            scores = lax.dot_general(
-                packed[which, span, :],
-                key,
-                (((1,), (1,)), ((), ())),
-                preferred_element_type=jnp.float32,
-            )
-            scores = (scores.reshape(PAIR // 2, 2 * rows, KEYS) + bias[...][None]).reshape(
-                half, KEYS
-            )
-            before = peak[which, span, :]
-            now = jnp.maximum(before, jnp.max(scores, axis=1, keepdims=True))
-            peak[which, span, :] = now
-            fade = jnp.exp2((before - now) * SCALE)
-            wide = jnp.concatenate([now] * (KEYS // 128), axis=1)
-            probs = jnp.exp2((scores - wide) * SCALE).astype(jnp.bfloat16)
-            own_half = (key_lane < HEAD_SIZE) == (group == 0)
-            beside = jnp.where(own_half, value, jnp.ones_like(value))
-            total[which, span, :] = total[which, span, :] * fade + jnp.dot(
-                probs, beside, preferred_element_type=jnp.float32
-            )
+        tile = store[pl.ds(chip, 2)].reshape(KEYS, 128)
+        scores = lax.dot_general(
+            packed[which], tile, (((1,), (1,)), ((), ())), preferred_element_type=jnp.float32
+        )
+        scores = (scores.reshape(HEADS, 2 * rows, KEYS) + bias[...][None]).reshape(both, KEYS)
+        before = peak[which]
+        now = jnp.maximum(before, jnp.max(scores, axis=1, keepdims=True))
+        peak[which] = now
+        fade = jnp.exp2((before - now) * SCALE)
+        wide = jnp.concatenate([now] * (KEYS // 128), axis=1)
+        probs = jnp.exp2((scores - wide) * SCALE).astype(jnp.bfloat16)
+        value_lane = lax.broadcasted_iota(jnp.int32, (KEYS, 128), 1) >= HEAD_SIZE
+        beside = jnp.where(value_lane, tile, jnp.ones_like(tile))
+        total[which] = total[which] * fade + jnp.dot(
+            probs, beside, preferred_element_type=jnp.float32
+        )
 
     def phase(step, carry):
         @pl.when(step == 1)
@@ -271,13 +283,6 @@
                         along(h, i, n, True).wait_recv()
                         along(h, i, n + 2).start()
 
-        @pl.when(step == 2)
-        def _():
-            for n in (0, 1):
-                weight_copy(n, True).wait_recv()
-                weight_copy(2 + n).start()
-                weight_copy(5 + n).start()
-
         @pl.when(step == 3)
         def _():
             for i in range(4):
@@ -292,52 +297,48 @@
         def one(t, carry):
             which = lax.div(t, 2)
             chip = row + 2 * lax.rem(t, 2)
-            limit = jnp.where(which == 0, here, CHIPS - 1 - here)
-
-            @pl.when(chip <= limit)
+            @pl.when(chip <= member(which))
             def _():
                 visit(which, chip)
 
             return carry
 
-        return lax.fori_loop(0, 4, one, carry)
+        return lax.fori_loop(0, 2 * SIDE, one, carry)
 
     lax.fori_loop(0, 4, phase, 0)
 
-    def answer(which, side):
-        def head(n):
-            at = (n * 2 + side) * rows
-            sums = total[which, at : at + rows, :]
-            result = sums / pltpu.roll(sums, HEAD_SIZE, axis=1)
-            if n % 2 != n // 3:
-                result = pltpu.roll(result, HEAD_SIZE, axis=1)
-            return result
-
-        return [
-            jnp.where(low_half, head(2 * i), head(2 * i + 1)).astype(out.dtype)
-            for i in range(PAIR // 2)
-        ]
-
-    for which in (1, 0):
+    for which in range(SIDE):
         for side in (0, 1):
-            for i, piece in enumerate(answer(which, side)):
-                done[2 * which + side, :, i * 128 : (i + 1) * 128] = piece
+            high, turned = [], []
+            for n in range(HEADS):
+                at = (n * 2 + side) * rows
+                sums_here = total[which, at : at + rows, :]
+                high.append(sums_here / pltpu.roll(sums_here, HEAD_SIZE, axis=1))
+                turned.append(pltpu.roll(high[n], HEAD_SIZE, axis=1))
+            answer = (
+                jnp.where(upper, high[0], jnp.where(low, turned[0], high[1])),
+                jnp.where(upper, jnp.where(low, turned[1], high[2]), turned[2]),
+            )
+            for i in (0, 1):
+                done[2 * which + side, :, i * 128 : (i + 1) * 128] = answer[i].astype(jnp.bfloat16)
 
     def reply(n, incoming=False):
         return remote(
-            done.at[from_slots[n]],
-            out.at[:, lanes(theirs[n] if incoming else mine, PAIR_WIDTH)],
+            done.at[other(n, False)],
+            replies.at[other(n, True) if incoming else mine],
             o_send.at[n],
             o_recv.at[n],
-            friends[n],
-        )
-
-    for n in (1, 2, 0):
+            plane.friend_device(*FRIENDS[n]),
+        )
+
+    for n in range(len(FRIENDS)):
         reply(n).start()
-    own_reply = pltpu.make_async_copy(
-        done.at[core], out.at[:, lanes(mine, PAIR_WIDTH)], sems.at[7]
-    )
+    own_reply = pltpu.make_async_copy(done.at[mine], replies.at[mine], sems.at[7])
     own_reply.start()
+    for n in (0, 1):
+        weight_copy(n, True).wait_recv()
+        weight_copy(2 + n).start()
+        weight_copy(5 + n).start()
 
     swap.wait_send()
     own_table.wait()
@@ -347,16 +348,23 @@
         for i in range(4):
             for n in range(4):
                 along(h, i, n).wait_send()
-    for n in range(3):
+    for n in range(len(FRIENDS)):
         ask(n).wait_send()
         tell(n).wait_send()
     for n in range(len(OTHERS)):
         table(n, True).wait_recv()
         table(n).wait_send()
     own_reply.wait()
-    for n in range(3):
+    for n in range(len(FRIENDS)):
         reply(n, True).wait_recv()
         reply(n).wait_send()
+    for p in range(KEY_VALUE_HEADS // 2):
+        even, odd = replies[2 * p], replies[2 * p + 1]
+        out[:, p * 384 : p * 384 + 128] = even[:, :128]
+        out[:, p * 384 + 128 : p * 384 + 256] = jnp.where(
+            low, even[:, 128:].astype(jnp.float32), odd[:, :128].astype(jnp.float32)
+        ).astype(jnp.bfloat16)
+        out[:, p * 384 + 256 : p * 384 + 384] = odd[:, 128:]
 
 
 BLOCKS = 4
@@ -432,9 +440,6 @@
     for n in (0, 1):
         spread(0, 0, n).start()
     mine.start()
-    for n in (2, 3):
-        weight_copy(n, True).wait_recv()
-    weight_copy(7).start()
     for j in (0, 1):
         emit(j, True).wait_recv()
         pass_on(j).start()
@@ -444,6 +449,9 @@
         pass_on(n, True).wait_recv()
     for n in (0, 1):
         spread(0, 1, n).start()
+    for n in (2, 3):
+        weight_copy(n, True).wait_recv()
+    weight_copy(7).start()
     mine.wait()
     for n in (4, 5, 6, 7):
         weight_copy(n, True).wait_recv()
@@ -628,7 +636,7 @@
 
 def normed(values, gain):
     mean_square = jnp.mean(values * values, axis=1, keepdims=True)
-    return (values * lax.rsqrt(mean_square + epsilon) * gain).astype(jnp.bfloat16)
+    return (values * lax.rsqrt(mean_square + epsilon) * gain[None]).astype(jnp.bfloat16)
 
 
 def layer_kernel(
@@ -637,7 +645,7 @@
     out, key_cache, value_cache,
     query_w, key_w, value_w, output_w, own_in, residual,
     queries, pairs, starts, given, attention, tables,
-    near, store, asked, begin, packed, peak, total, bias, done,
+    near, store, asked, begin, packed, peak, total, bias, done, replies,
     rows_in, sums, weights, picked, made, hold_q, hold_r, hold_p, hold_d,
     *sems,
 ):
@@ -699,23 +707,27 @@
             pltpu.roll(tile, 128 - HEAD_SIZE // 2, axis=1),
             pltpu.roll(tile, HEAD_SIZE // 2, axis=1),
         )
-        return (tile * cosine[...] + other * sine[...]).astype(jnp.bfloat16)
+        return tile * cosine[...] + other * sine[...]
 
     def project_keys():
         starts[...] = jnp.broadcast_to(prompt_start[...].astype(jnp.float32), starts.shape)
         loads[0].wait()
         keys = jnp.dot(own_in[...], key_w[...], preferred_element_type=jnp.float32)
         loads[1].wait()
-        values = jnp.dot(
-            own_in[...], value_w[...], preferred_element_type=jnp.float32
-        ).astype(jnp.bfloat16)
-        value_cache[...] = values
+        values = jnp.dot(own_in[...], value_w[...], preferred_element_type=jnp.float32)
+        value_cache[...] = values.astype(jnp.bfloat16)
+        low = lane < HEAD_SIZE
         for p in range(KEY_VALUE_HEADS // 2):
             at = slice(p * 128, (p + 1) * 128)
-            tile = rotated(keys[:, at])
-            key_cache[:, at] = tile
-            pairs[:, p * 256 : p * 256 + 128] = tile
-            pairs[:, p * 256 + 128 : (p + 1) * 256] = values[:, at]
+            key, value = rotated(keys[:, at]), values[:, at]
+            key_cache[:, at] = key.astype(jnp.bfloat16)
+            sides = (
+                jnp.where(low, key, pltpu.roll(value, HEAD_SIZE, axis=1)),
+                jnp.where(low, pltpu.roll(key, HEAD_SIZE, axis=1), value),
+            )
+            for c in (0, 1):
+                to = (c * SIDE + p) * 128
+                pairs[:, to : to + 128] = sides[c].astype(jnp.bfloat16)
 
     def project_queries():
         loads[2].wait()
@@ -727,7 +739,9 @@
             )
             for p in range(4):
                 at = c * 512 + p * 128
-                queries[:, at : at + 128] = rotated(part[:, p * 128 : (p + 1) * 128])
+                queries[:, at : at + 128] = rotated(part[:, p * 128 : (p + 1) * 128]).astype(
+                    jnp.bfloat16
+                )
 
     def make_tables():
         expert = lax.broadcasted_iota(jnp.int32, (EXPERTS, rows), 0)
@@ -754,7 +768,7 @@
     attention_section(
         plane, weight_copy, project_keys, project_queries, make_tables,
         queries, pairs, starts, given, attention, tables,
-        near, store, asked, begin, packed, peak, total, bias, done,
+        near, store, asked, begin, packed, peak, total, bias, done, replies,
         *attention_sems,
     )
 
@@ -788,10 +802,11 @@
         return pltpu.VMEM(shape, jnp.float32)
 
     others = len(OTHERS)
-    counts = (others, 6, 32, 6, 3)
+    friends = len(FRIENDS)
+    counts = (others, 6, 32, 2 * friends, friends)
     attention_sems = [dma((n,)) for n in counts for _ in (0, 1)] + [dma((8,))]
     expert_sems = [dma((n,)) for n in (20, 8, 16, 2, 4) for _ in (0, 1)]
-    both = 2 * PAIR * rows
+    both = 2 * HEADS * rows
     return pl.pallas_call(
         layer_kernel,
         out_shape=(
@@ -815,14 +830,15 @@
             brief(rows, width),
             full(CHIPS, 8, rows),
             brief(rows, 512),
-            brief(CHIPS, 2 * rows, 256),
-            brief(4, rows, PAIR_WIDTH),
-            full(4, 8, rows),
-            brief(2, both, 128),
-            full(2, both, 128),
-            full(2, both, 128),
+            brief(CHIPS, 2 * rows, 128),
+            brief(KEY_VALUE_HEADS, rows, ASK),
+            full(KEY_VALUE_HEADS, 8, rows),
+            brief(SIDE, both, 128),
+            full(SIDE, both, 128),
+            full(SIDE, both, 128),
             full(2 * rows, KEYS),
-            brief(4, rows, PAIR_WIDTH),
+            brief(KEY_VALUE_HEADS, rows, ASK),
+            brief(KEY_VALUE_HEADS, rows, ASK),
             brief(CHIPS, rows, width),
             brief(CHIPS, rows, width),
             brief(2, 3, width, FF),
@@ -848,6 +864,21 @@
     )
 
 
+def publish(*results):
+    def kernel(*refs):
+        for src, dst in zip(refs[: len(results)], refs[len(results) :]):
+            dst[...] = src[...]
+
+    vmem = pl.BlockSpec(memory_space=pltpu.VMEM)
+    return pl.pallas_call(
+        kernel,
+        out_shape=tuple(jax.ShapeDtypeStruct(r.shape, r.dtype) for r in results),
+        in_specs=[vmem] * len(results),
+        out_specs=(vmem,) * len(results),
+        name="publish",
+    )(*results)
+
+
 def rotation_tables(offsets):
     half = HEAD_SIZE // 2
     freqs = 10000.0 ** (-jnp.arange(half, dtype=jnp.float32) / half)
@@ -872,20 +903,21 @@
 ):
     rows = hidden.shape[0]
     positions = lax.axis_index("exp") * rows + jnp.arange(rows, dtype=jnp.int32)
-    return run_layer(
+    results = run_layer(
         hidden,
-        attn_gain[None],
+        attn_gain,
         query_weight,
         key_matrix,
         value_matrix,
         output_weight,
         prompt_start[None],
         rotation_tables(positions - prompt_start),
-        ffn_gain[None],
+        ffn_gain,
         routes.T,
         route_weights.T,
         expert_weights[0],
     )
+    return publish(*results)
 
 
 def solution(mesh):

time: 143 us -> 134 us (0.937)
  local copies, waits for them, and re-layouts: 7.56 us -> 0.09 us
  Pallas kernels: 133 us -> 131 us
    unnamed x3 -> x0, local copies, waits for them, and re-layouts: 4.9 us -> none
    pallas_call x1, Pallas kernels: 133 us -> 129 us  [run_layer(): pl.pallas_call(layer_kernel, out_shape=(jax.ShapeDtypeStruct((rows, width...]
    broadcast_in_dim x2 -> x0, local copies, waits for them, and re-layouts: 2.58 us -> none  [the longest x1 1.3 us: shards(): attn_gain[None]]
    pallas_call x0 -> x1, Pallas kernels: none -> 1.93 us  [publish(): pl.pallas_call(kernel, out_shape=tuple((jax.ShapeDtypeStruct(r.shape, r.d...]
where the time goes in v7:
time: 134 us
  Pallas kernels  131 us (98%)
  other arithmetic  1.65 us (1%)
    pallas_call x1, Pallas kernels, run_layer(): pl.pallas_call(layer_kernel, out_shape=(jax.ShapeDtypeStruct((rows, width...  129 us

profile of v7, /device:TPU:0, one launch (start us, length us, event | category | flops | bytes accessed | tf_op | source)
XLA Modules:
  0.0 133.6 jit_solution(9662996841886999330)
XLA Ops:
  0.6 0.7 subtract_convert_fusion
  1.3 0.1 mul.28
  1.4 1.0 fusion
  2.4 129.3 %layer.1 = (bf16[128,1536]{1,0:T(8,128)(2,1)}, bf16[128,512]{1,0:T(8,128)(2,1)}, bf16[128,512]{1,0:T(8,128)(2,1)}) custom-call(bf16[128,1536]{1,0:T(8,128)(2,1)} %hidden.1, f32[1536]{0:T(1024)} %attn_gain.1, bf16[1536,1536]{1,0:T(8,128)(2,1)} %wq.1, bf16[1536,512]{1,0:T(8,128)(2,1)} %wk.1, bf16[1536,512]{1,0:T(8,128)(2,1)} %wv.1, bf16[1536,1536]{1,0:T(8,128)(2,1)} %wo.1, ...), custom_call_target="tpu_custom_call" | custom-call | tf_op jit(solution)/shard_map/layer/pallas_call | solution.py:810
  131.7 1.9 %publish.1 = (bf16[128,1536]{1,0:T(8,128)(2,1)}, bf16[128,512]{1,0:T(8,128)(2,1)}, bf16[128,512]{1,0:T(8,128)(2,1)}) custom-call(bf16[128,1536]{1,0:T(8,128)(2,1)} %get-tuple-element.6.refs_0_, bf16[128,512]{1,0:T(8,128)(2,1)} %get-tuple-element.7.refs_1_, bf16[128,512]{1,0:T(8,128)(2,1)} %get-tuple-element.8.refs_2_), custom_call_target="tpu_custom_call" | custom-call | tf_op jit(solution)/shard_map/publish/pallas_call | solution.py:873
  (3 shorter events, 0.0 us)

commit v8 on v7

--- a/solution.py
+++ b/solution.py
@@ -1,3 +1,5 @@
+import math
+
 import jax
 import jax.numpy as jnp
 from jax import lax
@@ -88,7 +90,7 @@
 def attention_section(
     plane, weight_copy, project_keys, project_queries, make_tables,
     queries, pairs, starts, given, out, held,
-    near, store, asked, begin, packed, peak, total, bias, done, replies,
+    near, store, asked, begin, begins, packed, peak, total, bias, done, replies,
     give, take, x_send, x_recv, y_send, y_recv, q_send, q_recv, o_send, o_recv, sems,
 ):
     core = plane.core
@@ -221,6 +223,9 @@
     upper = core == 1
     for which in range(SIDE):
         for side in (0, 1):
+            begins[2 * which + side] = jnp.broadcast_to(
+                begin[2 * which + side, 0:1, :], (rows, rows)
+            ).T
             tiles = [
                 asked[2 * which + side, :, i * 128 : (i + 1) * 128].astype(jnp.float32)
                 for i in (0, 1)
@@ -239,6 +244,8 @@
     peak[...] = jnp.full_like(peak, LOW)
     total[...] = jnp.zeros_like(total)
     both = 2 * HEADS * rows
+    lane_number = lax.broadcasted_iota(jnp.int32, (1, 128), 1).astype(jnp.float32)
+    row_number = lax.broadcasted_iota(jnp.int32, (rows, 128), 0).astype(jnp.float32)
 
     def member(which):
         flip = lax.rem(plane.x + which, 2)
@@ -247,16 +254,16 @@
     def visit(which, chip):
         stream_chip = member(which)
         at = chip * (2 * rows)
+        shift = (stream_chip * (2 * rows) - at).astype(jnp.float32)
+        base = at.astype(jnp.float32)
         for side in (0, 1):
-            first = jnp.broadcast_to(begin[2 * which + side, 0:1, :], (rows, rows)).T
-            first = jnp.concatenate([first] * (KEYS // rows), axis=1).astype(jnp.int32)
-            key_pos = at + lax.broadcasted_iota(jnp.int32, (rows, KEYS), 1)
-            own_pos = (2 * stream_chip + side) * rows + lax.broadcasted_iota(
-                jnp.int32, (rows, KEYS), 0
-            )
-            bias[side * rows : (side + 1) * rows, :] = jnp.where(
-                (key_pos >= first) & (key_pos <= own_pos), 0.0, LOW
-            )
+            first = begins[2 * which + side] - base
+            last = row_number + (shift + side * rows)
+            for j in range(KEYS // 128):
+                key_number = lane_number + j * 128
+                bias[side * rows : (side + 1) * rows, j * 128 : (j + 1) * 128] = jnp.where(
+                    (key_number >= first) & (key_number <= last), 0.0, LOW
+                )
         tile = store[pl.ds(chip, 2)].reshape(KEYS, 128)
         scores = lax.dot_general(
             packed[which], tile, (((1,), (1,)), ((), ())), preferred_element_type=jnp.float32
@@ -274,6 +281,32 @@
             probs, beside, preferred_element_type=jnp.float32
         )
 
+    def answer(which):
+        for side in (0, 1):
+            high, turned = [], []
+            for n in range(HEADS):
+                at = (n * 2 + side) * rows
+                sums_here = total[which, at : at + rows, :]
+                high.append(sums_here / pltpu.roll(sums_here, HEAD_SIZE, axis=1))
+                turned.append(pltpu.roll(high[n], HEAD_SIZE, axis=1))
+            tiles = (
+                jnp.where(upper, high[0], jnp.where(low, turned[0], high[1])),
+                jnp.where(upper, jnp.where(low, turned[1], high[2]), turned[2]),
+            )
+            for i in (0, 1):
+                done[2 * which + side, :, i * 128 : (i + 1) * 128] = tiles[i].astype(jnp.bfloat16)
+
+    def reply(n, incoming=False):
+        return remote(
+            done.at[other(n, False)],
+            replies.at[other(n, True) if incoming else mine],
+            o_send.at[n],
+            o_recv.at[n],
+            plane.friend_device(*FRIENDS[n]),
+        )
+
+    own_reply = pltpu.make_async_copy(done.at[mine], replies.at[mine], sems.at[7])
+
     def phase(step, carry):
         @pl.when(step == 1)
         def _():
@@ -295,46 +328,35 @@
         row = lax.rem(plane.y + dy, SIDE) * SIDE
 
         def one(t, carry):
-            which = lax.div(t, 2)
-            chip = row + 2 * lax.rem(t, 2)
+            turn, part = lax.div(t, 2), lax.rem(t, 2)
+            dx = jnp.where(turn == 0, 2, jnp.where(turn == 1, 1, jnp.where(turn == 2, 3, 0)))
+            which = lax.rem(plane.x + dx, SIDE)
+            chip = row + 2 * part
+
             @pl.when(chip <= member(which))
             def _():
                 visit(which, chip)
 
+            @pl.when((step == 3) & (part == 1))
+            def _():
+                answer(which)
+
+            for column in range(SIDE):
+
+                @pl.when((step == 3) & (part == 1) & (dx == column))
+                def _():
+                    for n, friend in enumerate(FRIENDS):
+                        if friend[0] == column:
+                            reply(n).start()
+                    if column == 0:
+                        own_reply.start()
+
             return carry
 
         return lax.fori_loop(0, 2 * SIDE, one, carry)
 
     lax.fori_loop(0, 4, phase, 0)
 
-    for which in range(SIDE):
-        for side in (0, 1):
-            high, turned = [], []
-            for n in range(HEADS):
-                at = (n * 2 + side) * rows
-                sums_here = total[which, at : at + rows, :]
-                high.append(sums_here / pltpu.roll(sums_here, HEAD_SIZE, axis=1))
-                turned.append(pltpu.roll(high[n], HEAD_SIZE, axis=1))
-            answer = (
-                jnp.where(upper, high[0], jnp.where(low, turned[0], high[1])),
-                jnp.where(upper, jnp.where(low, turned[1], high[2]), turned[2]),
-            )
-            for i in (0, 1):
-                done[2 * which + side, :, i * 128 : (i + 1) * 128] = answer[i].astype(jnp.bfloat16)
-
-    def reply(n, incoming=False):
-        return remote(
-            done.at[other(n, False)],
-            replies.at[other(n, True) if incoming else mine],
-            o_send.at[n],
-            o_recv.at[n],
-            plane.friend_device(*FRIENDS[n]),
-        )
-
-    for n in range(len(FRIENDS)):
-        reply(n).start()
-    own_reply = pltpu.make_async_copy(done.at[mine], replies.at[mine], sems.at[7])
-    own_reply.start()
     for n in (0, 1):
         weight_copy(n, True).wait_recv()
         weight_copy(2 + n).start()
@@ -639,13 +661,26 @@
     return (values * lax.rsqrt(mean_square + epsilon) * gain[None]).astype(jnp.bfloat16)
 
 
+def rotation_tables(plane, prompt_start, cosine, sine):
+    rows = prompt_start.shape[1]
+    half = HEAD_SIZE // 2
+    lane = lax.broadcasted_iota(jnp.int32, (rows, 128), 1)
+    begin = jnp.broadcast_to(prompt_start[...].astype(jnp.float32), (rows, rows)).T
+    first = (plane.chip(0, 0) * 2 + plane.core) * rows
+    position = first + lax.broadcasted_iota(jnp.int32, (rows, 128), 0)
+    power = lax.rem(lane, half).astype(jnp.float32) / half
+    angle = (position.astype(jnp.float32) - begin) * jnp.exp(power * -math.log(10000.0))
+    cosine[...] = jnp.cos(angle)
+    sine[...] = jnp.where(lax.rem(lane, HEAD_SIZE) < half, -jnp.sin(angle), jnp.sin(angle))
+
+
 def layer_kernel(
-    hidden, attn_gain, wq, wk, wv, wo, prompt_start, cosine, sine, ffn_gain, routes, route_weights,
+    hidden, attn_gain, wq, wk, wv, wo, prompt_start, ffn_gain, routes, route_weights,
     first,
     out, key_cache, value_cache,
-    query_w, key_w, value_w, output_w, own_in, residual,
+    query_w, key_w, value_w, output_w, own_in, residual, cosine, sine,
     queries, pairs, starts, given, attention, tables,
-    near, store, asked, begin, packed, peak, total, bias, done, replies,
+    near, store, asked, begin, begins, packed, peak, total, bias, done, replies,
     rows_in, sums, weights, picked, made, hold_q, hold_r, hold_p, hold_d,
     *sems,
 ):
@@ -691,9 +726,10 @@
             )
         )
     ]
-    for load in loads:
+    for load in loads[:2]:
         load.start()
     own_in[...] = normed(hidden[...].astype(jnp.float32), attn_gain[...])
+    rotation_tables(plane, prompt_start, cosine, sine)
     arrived()
     for n in (0, 1, 4):
         weight_copy(n).start()
@@ -710,6 +746,8 @@
         return tile * cosine[...] + other * sine[...]
 
     def project_keys():
+        for load in loads[2:]:
+            load.start()
         starts[...] = jnp.broadcast_to(prompt_start[...].astype(jnp.float32), starts.shape)
         loads[0].wait()
         keys = jnp.dot(own_in[...], key_w[...], preferred_element_type=jnp.float32)
@@ -768,7 +806,7 @@
     attention_section(
         plane, weight_copy, project_keys, project_queries, make_tables,
         queries, pairs, starts, given, attention, tables,
-        near, store, asked, begin, packed, peak, total, bias, done, replies,
+        near, store, asked, begin, begins, packed, peak, total, bias, done, replies,
         *attention_sems,
     )
 
@@ -788,7 +826,7 @@
     )
 
 
-def run_layer(hidden, attn_gain, wq, wk, wv, wo, starts, trig, ffn_gain, routes, gains, first):
+def run_layer(hidden, attn_gain, wq, wk, wv, wo, starts, ffn_gain, routes, gains, first):
     rows, width = hidden.shape
     cache = wk.shape[1]
     dma = pltpu.SemaphoreType.DMA
@@ -814,7 +852,7 @@
             jax.ShapeDtypeStruct((rows, cache), jnp.bfloat16),
             jax.ShapeDtypeStruct((rows, cache), jnp.bfloat16),
         ),
-        in_specs=[vmem, vmem, hbm, hbm, hbm, hbm] + [vmem] * 6 + [hbm],
+        in_specs=[vmem, vmem, hbm, hbm, hbm, hbm] + [vmem] * 4 + [hbm],
         out_specs=(vmem,) * 3,
         scratch_shapes=[
             brief(*wq.shape),
@@ -823,6 +861,8 @@
             brief(*wo.shape),
             brief(rows, width),
             full(rows, width),
+            full(rows, 128),
+            full(rows, 128),
             brief(rows, width),
             brief(rows, 2 * cache),
             full(8, rows),
@@ -833,6 +873,7 @@
             brief(CHIPS, 2 * rows, 128),
             brief(KEY_VALUE_HEADS, rows, ASK),
             full(KEY_VALUE_HEADS, 8, rows),
+            full(KEY_VALUE_HEADS, rows, rows),
             brief(SIDE, both, 128),
             full(SIDE, both, 128),
             full(SIDE, both, 128),
@@ -860,7 +901,7 @@
         ),
         name="layer",
     )(
-        hidden, attn_gain, wq, wk, wv, wo, starts, *trig, ffn_gain, routes, gains, first
+        hidden, attn_gain, wq, wk, wv, wo, starts, ffn_gain, routes, gains, first
     )
 
 
@@ -877,15 +918,6 @@
         out_specs=(vmem,) * len(results),
         name="publish",
     )(*results)
-
-
-def rotation_tables(offsets):
-    half = HEAD_SIZE // 2
-    freqs = 10000.0 ** (-jnp.arange(half, dtype=jnp.float32) / half)
-    freqs = jnp.tile(freqs, 128 // half)
-    sign = jnp.where(jnp.arange(128) % HEAD_SIZE < half, -1.0, 1.0)
-    angle = offsets.astype(jnp.float32)[:, None] * freqs[None, :]
-    return jnp.cos(angle), jnp.sin(angle) * sign[None, :]
 
 
 def shards(
@@ -901,8 +933,6 @@
     route_weights,
     expert_weights,
 ):
-    rows = hidden.shape[0]
-    positions = lax.axis_index("exp") * rows + jnp.arange(rows, dtype=jnp.int32)
     results = run_layer(
         hidden,
         attn_gain,
@@ -911,7 +941,6 @@
         value_matrix,
         output_weight,
         prompt_start[None],
-        rotation_tables(positions - prompt_start),
         ffn_gain,
         routes.T,
         route_weights.T,

time: 134 us -> 128 us (0.955)
  Pallas kernels: 131 us -> 127 us
  other arithmetic: 1.65 us -> 0 us
    pallas_call x1, Pallas kernels: 129 us -> 125 us  [run_layer(): pl.pallas_call(layer_kernel, out_shape=(jax.ShapeDtypeStruct((rows, width...]
where the time goes in v8:
time: 128 us
  Pallas kernels  127 us (99%)
    pallas_call x1, Pallas kernels, run_layer(): pl.pallas_call(layer_kernel, out_shape=(jax.ShapeDtypeStruct((rows, width...  125 us

profile of v8, /device:TPU:0, one launch (start us, length us, event | category | flops | bytes accessed | tf_op | source)
XLA Modules:
  0.0 127.9 jit_solution(8889303160668739350)
XLA Ops:
  0.6 125.3 %layer.1 = (bf16[128,1536]{1,0:T(8,128)(2,1)}, bf16[128,512]{1,0:T(8,128)(2,1)}, bf16[128,512]{1,0:T(8,128)(2,1)}) custom-call(bf16[128,1536]{1,0:T(8,128)(2,1)} %hidden.1, f32[1536]{0:T(1024)} %attn_gain.1, bf16[1536,1536]{1,0:T(8,128)(2,1)} %wq.1, bf16[1536,512]{1,0:T(8,128)(2,1)} %wk.1, bf16[1536,512]{1,0:T(8,128)(2,1)} %wv.1, bf16[1536,1536]{1,0:T(8,128)(2,1)} %wo.1, ...), custom_call_target="tpu_custom_call" | custom-call | tf_op jit(solution)/shard_map/layer/pallas_call | solution.py:848
  126.0 1.9 %publish.1 = (bf16[128,1536]{1,0:T(8,128)(2,1)}, bf16[128,512]{1,0:T(8,128)(2,1)}, bf16[128,512]{1,0:T(8,128)(2,1)}) custom-call(bf16[128,1536]{1,0:T(8,128)(2,1)} %get-tuple-element.6.refs_0_, bf16[128,512]{1,0:T(8,128)(2,1)} %get-tuple-element.7.refs_1_, bf16[128,512]{1,0:T(8,128)(2,1)} %get-tuple-element.8.refs_2_), custom_call_target="tpu_custom_call" | custom-call | tf_op jit(solution)/shard_map/publish/pallas_call | solution.py:914

commit v9 on v8

--- a/solution.py
+++ b/solution.py
@@ -527,7 +527,7 @@
             device(0, ENDS[side]),
         )
 
-    PAIRS = [(group, j) for j in (0, 1) for group in (0, 1)]
+    PAIRS = [(0, 1), (1, 0), (1, 1), (0, 0)]
     slot = lax.broadcasted_iota(jnp.int32, (SLOTS, rows), 0).astype(jnp.float32)
 
     def group_step(g, carry):
@@ -599,7 +599,7 @@
     def add(at, held):
         sums[at] = (sums[at].astype(jnp.float32) + held.astype(jnp.float32)).astype(jnp.bfloat16)
 
-    for group, j in PAIRS:
+    def relay_sums(group, j):
         for side in (0, 1):
             k = group * 4 + j * 2 + side
             give_far(group, j, side).wait_recv()
@@ -618,20 +618,23 @@
             + hold_r[k + 1].astype(jnp.float32)
         )
 
+    for group, j in PAIRS[:3]:
+        relay_sums(group, j)
     at, value = total(0, 1)
     sums[at] = value.astype(jnp.bfloat16)
     for n in (0, 1):
         give_across(n).start()
+    relay_sums(0, 0)
     for side in (0, 1):
         at, value = total(1, side)
         sums[at] = value.astype(jnp.bfloat16)
         give_back(side, 0).start()
-    _, value = total(0, 0)
-    out_sum = value + residual[...]
     for side in (0, 1):
         give_across(side).wait_recv()
         add((place((0, ENDS[side])), part(side)), hold_p[side])
         give_back(side, 1).start()
+    _, value = total(0, 0)
+    out_sum = value + residual[...]
     for side in (0, 1):
         for late in (0, 1):
             give_back(side, late).wait_recv()

time: 128 us -> 127 us (level)
    pallas_call x1, Pallas kernels: 125 us -> 124 us  [run_layer(): pl.pallas_call(layer_kernel, out_shape=(jax.ShapeDtypeStruct((rows, width...]
where the time goes in v9:
time: 127 us
  Pallas kernels  126 us (99%)
    pallas_call x1, Pallas kernels, run_layer(): pl.pallas_call(layer_kernel, out_shape=(jax.ShapeDtypeStruct((rows, width...  124 us

profile of v9, /device:TPU:0, one launch (start us, length us, event | category | flops | bytes accessed | tf_op | source)
XLA Modules:
  0.0 126.6 jit_solution(1236155554666869785)
XLA Ops:
  0.6 124.0 %layer.1 = (bf16[128,1536]{1,0:T(8,128)(2,1)}, bf16[128,512]{1,0:T(8,128)(2,1)}, bf16[128,512]{1,0:T(8,128)(2,1)}) custom-call(bf16[128,1536]{1,0:T(8,128)(2,1)} %hidden.1, f32[1536]{0:T(1024)} %attn_gain.1, bf16[1536,1536]{1,0:T(8,128)(2,1)} %wq.1, bf16[1536,512]{1,0:T(8,128)(2,1)} %wk.1, bf16[1536,512]{1,0:T(8,128)(2,1)} %wv.1, bf16[1536,1536]{1,0:T(8,128)(2,1)} %wo.1, ...), custom_call_target="tpu_custom_call" | custom-call | tf_op jit(solution)/shard_map/layer/pallas_call | solution.py:851
  124.7 1.9 %publish.1 = (bf16[128,1536]{1,0:T(8,128)(2,1)}, bf16[128,512]{1,0:T(8,128)(2,1)}, bf16[128,512]{1,0:T(8,128)(2,1)}) custom-call(bf16[128,1536]{1,0:T(8,128)(2,1)} %get-tuple-element.6.refs_0_, bf16[128,512]{1,0:T(8,128)(2,1)} %get-tuple-element.7.refs_1_, bf16[128,512]{1,0:T(8,128)(2,1)} %get-tuple-element.8.refs_2_), custom_call_target="tpu_custom_call" | custom-call | tf_op jit(solution)/shard_map/publish/pallas_call | solution.py:917

commit v10 on v9

--- a/solution.py
+++ b/solution.py
@@ -196,17 +196,19 @@
             across(h, n).start()
         along(h, 0, 0).start()
         along(h, 0, 1).start()
-    project_queries()
-    own_asked.start()
-    for n in range(len(FRIENDS)):
-        ask(n).start()
-        tell(n).start()
+    project_queries(0)
     for n in range(3):
         i = (1, 2, 3)[n]
         for h in (0, 1):
             across(h, n, True).wait_recv()
             along(h, i, 0).start()
             along(h, i, 1).start()
+    project_queries(1)
+    project_queries(2)
+    own_asked.start()
+    for n in range(len(FRIENDS)):
+        ask(n).start()
+        tell(n).start()
     for n in range(len(OTHERS)):
         table(n).start()
 
@@ -770,19 +772,19 @@
                 to = (c * SIDE + p) * 128
                 pairs[:, to : to + 128] = sides[c].astype(jnp.bfloat16)
 
-    def project_queries():
-        loads[2].wait()
-        for c in range(3):
-            part = jnp.dot(
-                own_in[...],
-                query_w[:, c * 512 : (c + 1) * 512],
-                preferred_element_type=jnp.float32,
+    def project_queries(c):
+        if c == 0:
+            loads[2].wait()
+        part = jnp.dot(
+            own_in[...],
+            query_w[:, c * 512 : (c + 1) * 512],
+            preferred_element_type=jnp.float32,
+        )
+        for p in range(4):
+            at = c * 512 + p * 128
+            queries[:, at : at + 128] = rotated(part[:, p * 128 : (p + 1) * 128]).astype(
+                jnp.bfloat16
             )
-            for p in range(4):
-                at = c * 512 + p * 128
-                queries[:, at : at + 128] = rotated(part[:, p * 128 : (p + 1) * 128]).astype(
-                    jnp.bfloat16
-                )
 
     def make_tables():
         expert = lax.broadcasted_iota(jnp.int32, (EXPERTS, rows), 0)

time: 127 us -> 130 us (1.024)
  Pallas kernels: 126 us -> 129 us
    pallas_call x1, Pallas kernels: 124 us -> 127 us  [run_layer(): pl.pallas_call(layer_kernel, out_shape=(jax.ShapeDtypeStruct((rows, width...]
where the time goes in v10:
time: 130 us; the launch traced here: 129 us
  Pallas kernels  129 us (99%)
    pallas_call x1, Pallas kernels, run_layer(): pl.pallas_call(layer_kernel, out_shape=(jax.ShapeDtypeStruct((rows, width...  127 us

profile of v10, /device:TPU:0, one launch (start us, length us, event | category | flops | bytes accessed | tf_op | source)
XLA Modules:
  0.0 129.4 jit_solution(8520333230084065552)
XLA Ops:
  0.6 126.9 %layer.1 = (bf16[128,1536]{1,0:T(8,128)(2,1)}, bf16[128,512]{1,0:T(8,128)(2,1)}, bf16[128,512]{1,0:T(8,128)(2,1)}) custom-call(bf16[128,1536]{1,0:T(8,128)(2,1)} %hidden.1, f32[1536]{0:T(1024)} %attn_gain.1, bf16[1536,1536]{1,0:T(8,128)(2,1)} %wq.1, bf16[1536,512]{1,0:T(8,128)(2,1)} %wk.1, bf16[1536,512]{1,0:T(8,128)(2,1)} %wv.1, bf16[1536,1536]{1,0:T(8,128)(2,1)} %wo.1, ...), custom_call_target="tpu_custom_call" | custom-call | tf_op jit(solution)/shard_map/layer/pallas_call | solution.py:853
  127.5 1.9 %publish.1 = (bf16[128,1536]{1,0:T(8,128)(2,1)}, bf16[128,512]{1,0:T(8,128)(2,1)}, bf16[128,512]{1,0:T(8,128)(2,1)}) custom-call(bf16[128,1536]{1,0:T(8,128)(2,1)} %get-tuple-element.6.refs_0_, bf16[128,512]{1,0:T(8,128)(2,1)} %get-tuple-element.7.refs_1_, bf16[128,512]{1,0:T(8,128)(2,1)} %get-tuple-element.8.refs_2_), custom_call_target="tpu_custom_call" | custom-call | tf_op jit(solution)/shard_map/publish/pallas_call | solution.py:919

commit v11 on v9

--- a/solution.py
+++ b/solution.py
@@ -183,12 +183,17 @@
     own_begin = pltpu.make_async_copy(starts, begin.at[mine], sems.at[5])
     own_table = pltpu.make_async_copy(given.at[here], held.at[here], sems.at[6])
 
+    project_queries()
+    own_asked.start()
+    own_begin.start()
+    for n in range(len(FRIENDS)):
+        ask(n).start()
+        tell(n).start()
     project_keys()
     swap.start()
     for h in (0, 1):
         if h == 1:
             make_tables()
-            own_begin.start()
             own_table.start()
             swap.wait_recv()
         keep(h).start()
@@ -196,11 +201,6 @@
             across(h, n).start()
         along(h, 0, 0).start()
         along(h, 0, 1).start()
-    project_queries()
-    own_asked.start()
-    for n in range(len(FRIENDS)):
-        ask(n).start()
-        tell(n).start()
     for n in range(3):
         i = (1, 2, 3)[n]
         for h in (0, 1):
@@ -729,8 +729,8 @@
             )
         )
     ]
-    for load in loads[:2]:
-        load.start()
+    for n in (2, 0, 1):
+        loads[n].start()
     own_in[...] = normed(hidden[...].astype(jnp.float32), attn_gain[...])
     rotation_tables(plane, prompt_start, cosine, sine)
     arrived()
@@ -749,9 +749,8 @@
         return tile * cosine[...] + other * sine[...]
 
     def project_keys():
-        for load in loads[2:]:
+        for load in loads[3:]:
             load.start()
-        starts[...] = jnp.broadcast_to(prompt_start[...].astype(jnp.float32), starts.shape)
         loads[0].wait()
         keys = jnp.dot(own_in[...], key_w[...], preferred_element_type=jnp.float32)
         loads[1].wait()
@@ -771,6 +770,7 @@
                 pairs[:, to : to + 128] = sides[c].astype(jnp.bfloat16)
 
     def project_queries():
+        starts[...] = jnp.broadcast_to(prompt_start[...].astype(jnp.float32), starts.shape)
         loads[2].wait()
         for c in range(3):
             part = jnp.dot(

time: 127 us -> 125 us (0.984)
  Pallas kernels: 126 us -> 124 us
    pallas_call x1, Pallas kernels: 124 us -> 122 us  [run_layer(): pl.pallas_call(layer_kernel, out_shape=(jax.ShapeDtypeStruct((rows, width...]
where the time goes in v11:
time: 125 us
  Pallas kernels  124 us (99%)
    pallas_call x1, Pallas kernels, run_layer(): pl.pallas_call(layer_kernel, out_shape=(jax.ShapeDtypeStruct((rows, width...  122 us

profile of v11, /device:TPU:0, one launch (start us, length us, event | category | flops | bytes accessed | tf_op | source)
XLA Modules:
  0.0 124.8 jit_solution(5365094108356089361)
XLA Ops:
  0.6 122.2 %layer.1 = (bf16[128,1536]{1,0:T(8,128)(2,1)}, bf16[128,512]{1,0:T(8,128)(2,1)}, bf16[128,512]{1,0:T(8,128)(2,1)}) custom-call(bf16[128,1536]{1,0:T(8,128)(2,1)} %hidden.1, f32[1536]{0:T(1024)} %attn_gain.1, bf16[1536,1536]{1,0:T(8,128)(2,1)} %wq.1, bf16[1536,512]{1,0:T(8,128)(2,1)} %wk.1, bf16[1536,512]{1,0:T(8,128)(2,1)} %wv.1, bf16[1536,1536]{1,0:T(8,128)(2,1)} %wo.1, ...), custom_call_target="tpu_custom_call" | custom-call | tf_op jit(solution)/shard_map/layer/pallas_call | solution.py:851
  122.9 1.9 %publish.1 = (bf16[128,1536]{1,0:T(8,128)(2,1)}, bf16[128,512]{1,0:T(8,128)(2,1)}, bf16[128,512]{1,0:T(8,128)(2,1)}) custom-call(bf16[128,1536]{1,0:T(8,128)(2,1)} %get-tuple-element.6.refs_0_, bf16[128,512]{1,0:T(8,128)(2,1)} %get-tuple-element.7.refs_1_, bf16[128,512]{1,0:T(8,128)(2,1)} %get-tuple-element.8.refs_2_), custom_call_target="tpu_custom_call" | custom-call | tf_op jit(solution)/shard_map/publish/pallas_call | solution.py:917

commit v12 on v11

--- a/solution.py
+++ b/solution.py
@@ -201,22 +201,11 @@
             across(h, n).start()
         along(h, 0, 0).start()
         along(h, 0, 1).start()
-    for n in range(3):
-        i = (1, 2, 3)[n]
-        for h in (0, 1):
-            across(h, n, True).wait_recv()
-            along(h, i, 0).start()
-            along(h, i, 1).start()
-    for n in range(len(OTHERS)):
-        table(n).start()
-
     own_asked.wait()
     own_begin.wait()
     for n in range(len(FRIENDS)):
         ask(n, True).wait_recv()
         tell(n, True).wait_recv()
-    for h in (0, 1):
-        keep(h).wait()
 
     lane = lax.broadcasted_iota(jnp.int32, (rows, 128), 1)
     low = lane < HEAD_SIZE
@@ -243,6 +232,18 @@
                 )
     peak[...] = jnp.full_like(peak, LOW)
     total[...] = jnp.zeros_like(total)
+    for n in range(3):
+        i = (1, 2, 3)[n]
+        for h in (0, 1):
+            across(h, n, True).wait_recv()
+            along(h, i, 0).start()
+            along(h, i, 1).start()
+    for n in range(len(OTHERS)):
+        table(n).start()
+
+    for h in (0, 1):
+        keep(h).wait()
+
     both = 2 * HEADS * rows
     lane_number = lax.broadcasted_iota(jnp.int32, (1, 128), 1).astype(jnp.float32)
     row_number = lax.broadcasted_iota(jnp.int32, (rows, 128), 0).astype(jnp.float32)

time: 125 us -> 127 us (1.016)
  no operation moved by 1% of the time
where the time goes in v12:
time: 127 us; the launch traced here: 126 us
  Pallas kernels  125 us (98%)
    pallas_call x1, Pallas kernels, run_layer(): pl.pallas_call(layer_kernel, out_shape=(jax.ShapeDtypeStruct((rows, width...  123 us

profile of v12, /device:TPU:0, one launch (start us, length us, event | category | flops | bytes accessed | tf_op | source)
XLA Modules:
  0.0 126.0 jit_solution(12889574743246527420)
XLA Ops:
  0.6 123.5 %layer.1 = (bf16[128,1536]{1,0:T(8,128)(2,1)}, bf16[128,512]{1,0:T(8,128)(2,1)}, bf16[128,512]{1,0:T(8,128)(2,1)}) custom-call(bf16[128,1536]{1,0:T(8,128)(2,1)} %hidden.1, f32[1536]{0:T(1024)} %attn_gain.1, bf16[1536,1536]{1,0:T(8,128)(2,1)} %wq.1, bf16[1536,512]{1,0:T(8,128)(2,1)} %wk.1, bf16[1536,512]{1,0:T(8,128)(2,1)} %wv.1, bf16[1536,1536]{1,0:T(8,128)(2,1)} %wo.1, ...), custom_call_target="tpu_custom_call" | custom-call | tf_op jit(solution)/shard_map/layer/pallas_call | solution.py:852
  124.1 1.9 %publish.1 = (bf16[128,1536]{1,0:T(8,128)(2,1)}, bf16[128,512]{1,0:T(8,128)(2,1)}, bf16[128,512]{1,0:T(8,128)(2,1)}) custom-call(bf16[128,1536]{1,0:T(8,128)(2,1)} %get-tuple-element.6.refs_0_, bf16[128,512]{1,0:T(8,128)(2,1)} %get-tuple-element.7.refs_1_, bf16[128,512]{1,0:T(8,128)(2,1)} %get-tuple-element.8.refs_2_), custom_call_target="tpu_custom_call" | custom-call | tf_op jit(solution)/shard_map/publish/pallas_call | solution.py:918
